TPU v7x, 256 devices: a whole 4x4x8 slice. The times are simulated.
256 devices in a mesh: tm: 16 (over y, x_lo, core), space: 16 (over x_hi, z).
Axes of the slice: x: 4 (x_hi: 2, x_lo: 2; x = x_hi * 2 + x_lo), y: 4, z: 8, core: 2. Of those that a mesh axis runs over, the one named last changes fastest.
Arguments:
- eigvec: bfloat16 [16, 2, 3, 16384, 384], P('tm', None, None, 'space'), may hold values from -1 to 1
- momenta: int32 [2, 3], replicated, may hold values from -2 to 2
- peram: bfloat16 [16, 2, 384, 4, 384], P('tm', None, 'space'), may hold values from -0.0078125 to 0.0078125
Outputs:
- dressed: bfloat16 [16, 384, 4, 2, 384], P('tm', 'space')
All inputs are finite; a program needn't handle non-finite values.
Results may differ from a plain program's by a relative error of at most 0.0073.
Values may be sent and summed in bfloat16 or wider, within the bound.
No kernel may reach another device: no remote copies, remote signals or barrier semaphores. Data moves between devices by JAX's collectives and lax.ppermute only.
A program may use at most 128 MiB of HBM per device.

v0:
```python
import math

import jax
import jax.numpy as jnp
from jax import lax
from jax.sharding import PartitionSpec as P

SPIN = 4
COLORS = 3
LAT = 32


def in_blocks(x, dim, peers):
    before, after = (x.shape[:dim], x.shape[dim + 1 :])
    return jnp.moveaxis(x.reshape(*before, peers, -1, *after), dim, 0)


def sum_at_owner(x, axis, dim):
    parts = in_blocks(x, dim, lax.axis_size(axis))
    arrived = lax.all_to_all(parts, axis, split_axis=0, concat_axis=0, tiled=True)
    return arrived.sum(axis=0)


def partner(value, axis, stride):
    mask = 2**stride
    pairs = [(source, source ^ mask) for source in range(lax.axis_size(axis))]
    return lax.ppermute(value, axis, pairs)


def in_order(parts, dim):
    parts = jnp.moveaxis(parts, 0, dim)
    lengths = parts.shape
    return parts.reshape(*lengths[:dim], lengths[dim] * lengths[dim + 1], *lengths[dim + 2 :])


def from_everyone(x, axis):
    copies = jnp.broadcast_to(x, (lax.axis_size(axis), *x.shape))
    return lax.all_to_all(copies, axis, split_axis=0, concat_axis=0, tiled=True)


def collect(x, axis, dim):
    return in_order(from_everyone(x, axis), dim)


def phase_gram(vectors, momentum, coord_x, coord_y, coord_z):
    sites_dev = vectors.shape[2]
    nvec = vectors.shape[3]
    winding = jnp.mod(momentum[0] * coord_x + momentum[1] * coord_y + momentum[2] * coord_z, LAT)
    theta = winding.astype(jnp.float32) * (2.0 * math.pi / LAT)
    cosine = jnp.cos(theta)[None, :, None]
    sine = jnp.sin(theta)[None, :, None]
    real_part = vectors[0].astype(jnp.float32)
    imag_part = vectors[1].astype(jnp.float32)
    phased_re = (cosine * real_part + sine * imag_part).astype(jnp.bfloat16)
    phased_im = (cosine * imag_part - sine * real_part).astype(jnp.bfloat16)
    upper = jnp.concatenate([phased_re, phased_im], axis=-1)
    lower = jnp.concatenate([phased_im, -phased_re], axis=-1)
    right = jnp.stack([upper, lower]).reshape(2 * COLORS * sites_dev, 2 * nvec)
    left = vectors.reshape(2 * COLORS * sites_dev, nvec)
    return lax.dot_general(
        left, right, (((0,), (0,)), ((), ())), preferred_element_type=jnp.float32
    )


def complex_left(block_re, block_im):
    rows = block_re.shape[0]
    cols = block_re.shape[1]
    stacked = jnp.stack(
        [
            jnp.concatenate([block_re, -block_im], axis=1),
            jnp.concatenate([block_im, block_re], axis=1),
        ],
        axis=1,
    )
    return stacked.reshape(2 * rows, 2 * cols)


def local(eigvec, momenta, peram):
    vectors = eigvec[0]
    sites_dev = vectors.shape[2]
    nvec = vectors.shape[3]
    nrows = peram.shape[2]
    sites = lax.axis_index("space") * sites_dev + jnp.arange(sites_dev, dtype=jnp.int32)
    coord_x = sites % LAT
    coord_y = sites // LAT % LAT
    coord_z = sites // (LAT * LAT)
    sink_part = phase_gram(vectors, momenta[0], coord_x, coord_y, coord_z)
    source_part = phase_gram(vectors, momenta[1], coord_x, coord_y, coord_z)
    bit_count = lax.axis_size("tm").bit_length() - 1
    share = sum_at_owner(source_part, "space", 0).astype(jnp.bfloat16)
    for bit in range(bit_count):
        share = partner(share, "tm", bit)
    source = collect(share, "space", 0)
    tau = peram[0].reshape(2, nrows, SPIN * nvec)
    own_rows = sum_at_owner(sink_part, "space", 0).astype(jnp.bfloat16)
    block_re = own_rows[:, :nvec]
    block_im = own_rows[:, nvec:]
    piece = lax.all_gather(tau, "space", axis=1, tiled=True)
    count = piece.shape[1]
    flat = piece.reshape(2 * count, SPIN * nvec)
    mixed = jnp.dot(
        complex_left(block_re, block_im), flat, preferred_element_type=jnp.float32
    ).reshape(nrows, 2, SPIN * nvec)
    mixed = mixed.astype(jnp.bfloat16)
    mixed_re = mixed[:, 0].reshape(nrows * SPIN, nvec)
    mixed_im = mixed[:, 1].reshape(nrows * SPIN, nvec)
    source_re = source[:, :nvec]
    source_im = source[:, nvec:]
    right = jnp.concatenate([source, jnp.concatenate([-source_im, source_re], axis=1)], axis=0)
    dressed = jnp.dot(
        jnp.concatenate([mixed_re, mixed_im], axis=1), right, preferred_element_type=jnp.float32
    )
    return dressed.reshape(1, nrows, SPIN, 2, nvec).astype(jnp.bfloat16)


def solution(mesh):
    return jax.shard_map(
        local,
        mesh=mesh,
        in_specs=(P("tm", None, None, "space", None), P(), P("tm", None, "space", None, None)),
        out_specs=P("tm", "space", None, None, None),
        check_vma=False,
    )
```

profile of v0, /device:TPU:8, one launch (start us, length us, event | category | flops | bytes accessed | tf_op | source)
XLA Modules:
  0.0 170.0 jit_solution(3619409923708085660)
XLA Ops:
  6.5 1.6 fusion.47
  8.1 2.0 %fusion.36 = (f32[1024]{0:T(1024)S(1)}, f32[1024]{0:T(1024)S(1)}) fusion(s32[]{:T(128)} %bitcast.19, s32[]{:T(128)} %bitcast.18, s32[]{:T(128)S(6)} %mul.158, s32[]{:T(128)} %bitcast.17), kind=kLoop, calls=%fused_computation.71 | loop fusion | flops 60416 | bytes 8208 | tf_op jit(solution)/shard_map/sin | solution.py:51
  10.1 1.9 %fusion.38 = (f32[1024]{0:T(1024)S(1)}, f32[1024]{0:T(1024)S(1)}) fusion(s32[]{:T(128)} %bitcast.2, s32[]{:T(128)} %bitcast.1, s32[]{:T(128)S(6)} %mul.158, s32[]{:T(128)} %bitcast), kind=kLoop, calls=%fused_computation.73 | loop fusion | flops 60416 | bytes 8208 | tf_op jit(solution)/shard_map/sin | solution.py:51
  12.0 0.0 copy-start
  12.0 5.1 %fusion.42 = (bf16[3,1024,384]{2,1,0:T(8,128)(2,1)S(1)}, bf16[3,1024,384]{2,1,0:T(8,128)(2,1)}, bf16[3,1024,384]{2,1,0:T(8,128)(2,1)S(1)}, bf16[3,1024,384]{2,1,0:T(8,128)(2,1)S(1)}) fusion(bf16[1,2,3,1024,384]{4,3,2,1,0:T(8,128)(2,1)} %param.3, f32[1024]{0:T(1024)S(1)} %get-tuple-element.32, f32[1024]{0:T(1024)S(1)} %get-tuple-element.33, ...), kind=kLoop, calls=%fused_computation.78 | loop fusion | flops 14155776 | bytes 14172160 | tf_op jit(solution)/shard_map/neg | solution.py:57
  17.1 0.0 copy-done
  17.1 2.7 %fusion.3 = (bf16[3,1024,384]{2,1,0:T(8,128)(2,1)}, bf16[3,1024,384]{2,1,0:T(8,128)(2,1)S(1)}) fusion(f32[1024]{0:T(1024)S(1)} %get-tuple-element.32, f32[1024]{0:T(1024)S(1)} %get-tuple-element.33, bf16[1,2,3,1024,384]{4,3,2,1,0:T(8,128)(2,1)S(1)} %copy-done, f32[1024]{0:T(1024)S(1)} %get-tuple-element.34, f32[1024]{0:T(1024)S(1)} %get-tuple-element.35), kind=kLoop, calls=%fused_computation.13 | loop fusion | flops 11796480 | bytes 9453568 | tf_op jit(solution)/shard_map/convert_element_type | solution.py:55
  19.8 3.9 %maximum_bitcast_fusion.2 = (bf16[1,3,1024,768]{3,2,1,0:T(8,128)(2,1)}, bf16[1,3,1024,768]{3,2,1,0:T(8,128)(2,1)}) fusion(bf16[3,1024,384]{2,1,0:T(8,128)(2,1)S(1)} %get-tuple-element.10, bf16[3,1024,384]{2,1,0:T(8,128)(2,1)S(1)} %get-tuple-element.12, bf16[3,1024,384]{2,1,0:T(8,128)(2,1)S(1)} %get-tuple-element.11), kind=kLoop, calls=%fused_computation.20 | loop fusion | flops 18874368 | bytes 16515072 | tf_op jit(solution)/shard_map/stack | solution.py:58
  23.7 8.3 %pad_maximum_fusion.1 = bf16[2,3,1024,768]{3,2,1,0:T(8,128)(2,1)} fusion(bf16[1,3,1024,768]{3,2,1,0:T(8,128)(2,1)} %get-tuple-element.16, bf16[1,3,1024,768]{3,2,1,0:T(8,128)(2,1)} %get-tuple-element.15), kind=kLoop, calls=%fused_computation.1 | loop fusion | flops 4718592 | bytes 18874368 | tf_op jit(solution)/shard_map/stack | solution.py:58
  32.0 9.9 %fusion.49 = f32[768,384]{0,1:T(8,128)} fusion(bf16[6144,768]{1,0:T(8,128)(2,1)} %bitcast.58, bf16[6144,384]{1,0:T(8,128)(2,1)} %bitcast.56), kind=kOutput, calls=%fused_computation.83 | convolution fusion | flops 3623878656 | bytes 15335424 | tf_op jit(solution)/shard_map/dot_general | solution.py:60
  41.9 11.0 %all-to-all-start.1 = ((f32[16,24,768]{2,1,0:T(8,128)}), f32[16,24,768]{2,1,0:T(8,128)S(1)}, u32[]{:S(2)}, u32[]{:S(2)}) async-start(f32[16,24,768]{2,1,0:T(8,128)} %bitcast.63), calls=%async_computation.1 | async-start | bytes 2359296 | tf_op jit(solution)/shard_map/all_to_all | solution.py:20
  52.9 0.2 all-gather.2.cloned.1.call-start
  53.1 1.6 reshape_squeeze.14
  54.8 0.0 all-gather.2.cloned.1.call-update
  54.8 7.7 %maximum_bitcast_fusion = (bf16[1,3,1024,768]{3,2,1,0:T(8,128)(2,1)}, bf16[1,3,1024,768]{3,2,1,0:T(8,128)(2,1)}) fusion(bf16[3,1024,384]{2,1,0:T(8,128)(2,1)} %get-tuple-element.9, bf16[3,1024,384]{2,1,0:T(8,128)(2,1)} %get-tuple-element.6, bf16[3,1024,384]{2,1,0:T(8,128)(2,1)S(1)} %get-tuple-element.5), kind=kLoop, calls=%fused_computation.18 | loop fusion | flops 18874368 | bytes 16515072 | tf_op jit(solution)/shard_map/stack | solution.py:58
  62.5 8.3 %pad_maximum_fusion = bf16[2,3,1024,768]{3,2,1,0:T(8,128)(2,1)} fusion(bf16[1,3,1024,768]{3,2,1,0:T(8,128)(2,1)} %get-tuple-element.14, bf16[1,3,1024,768]{3,2,1,0:T(8,128)(2,1)} %get-tuple-element.13), kind=kLoop, calls=%fused_computation | loop fusion | flops 4718592 | bytes 18874368 | tf_op jit(solution)/shard_map/stack | solution.py:58
  70.8 9.9 %fusion.48 = f32[768,384]{0,1:T(8,128)} fusion(bf16[6144,768]{1,0:T(8,128)(2,1)} %bitcast.59, bf16[6144,384]{1,0:T(8,128)(2,1)} %bitcast.57), kind=kOutput, calls=%fused_computation.82 | convolution fusion | flops 3623878656 | bytes 15335424 | tf_op jit(solution)/shard_map/dot_general | solution.py:60
  80.7 6.2 %all-to-all-done.1 = f32[16,24,768]{2,1,0:T(8,128)S(1)} async-done(((f32[16,24,768]{2,1,0:T(8,128)}), f32[16,24,768]{2,1,0:T(8,128)S(1)}, u32[]{:S(2)}, u32[]{:S(2)}) %all-to-all-start.1) | async-done | bytes 1179680 | tf_op jit(solution)/shard_map/all_to_all | solution.py:20
  86.9 3.8 %all-to-all-start = ((f32[16,24,768]{2,1,0:T(8,128)}), f32[16,24,768]{2,1,0:T(8,128)S(1)}, u32[]{:S(2)}, u32[]{:S(2)}) async-start(f32[16,24,768]{2,1,0:T(8,128)} %bitcast.12), calls=%async_computation | async-start | bytes 2359296 | tf_op jit(solution)/shard_map/all_to_all | solution.py:20
  90.8 0.1 reduce_sum.19
  90.8 0.1 collective-permute-start
  90.9 1.2 collective-permute-done
  92.1 0.5 collective-permute-start.1
  92.7 3.5 %collective-permute-done.1 = bf16[24,768]{1,0:T(8,128)(2,1)S(1)} collective-permute-done((bf16[24,768]{1,0:T(8,128)(2,1)S(1)}, bf16[24,768]{1,0:T(8,128)(2,1)S(1)}, u32[]{:S(2)}, u32[]{:S(2)}) %collective-permute-start.1) | collective-permute-done | bytes 36896 | tf_op jit(solution)/shard_map/ppermute | solution.py:27
  96.2 0.4 collective-permute-start.2
  96.6 3.5 %collective-permute-done.2 = bf16[24,768]{1,0:T(8,128)(2,1)S(1)} collective-permute-done((bf16[24,768]{1,0:T(8,128)(2,1)S(1)}, bf16[24,768]{1,0:T(8,128)(2,1)S(1)}, u32[]{:S(2)}, u32[]{:S(2)}) %collective-permute-start.2) | collective-permute-done | bytes 36896 | tf_op jit(solution)/shard_map/ppermute | solution.py:27
  100.1 2.4 %collective-permute-start.3 = (bf16[24,768]{1,0:T(8,128)(2,1)S(1)}, bf16[24,768]{1,0:T(8,128)(2,1)S(1)}, u32[]{:S(2)}, u32[]{:S(2)}) collective-permute-start(bf16[24,768]{1,0:T(8,128)(2,1)S(1)} %collective-permute-done.2), channel_id=1, source_target_pairs={{0,128},{16,144},{32,160},{48,176},{64,192},{80,208},{96,224},{112... | collective-permute-start | bytes 110600 | tf_op jit(solution)/shard_map/ppermute | solution.py:27
  102.5 20.5 %all-to-all-done = f32[16,24,768]{2,1,0:T(8,128)S(1)} async-done(((f32[16,24,768]{2,1,0:T(8,128)}), f32[16,24,768]{2,1,0:T(8,128)S(1)}, u32[]{:S(2)}, u32[]{:S(2)}) %all-to-all-start) | async-done | bytes 1179680 | tf_op jit(solution)/shard_map/all_to_all | solution.py:20
  123.0 0.0 collective-permute-done.3
  123.0 0.9 broadcast_in_dim.2
  123.8 4.7 %all-to-all-start.2 = ((bf16[16,24,768]{2,1,0:T(8,128)(2,1)}), bf16[16,24,768]{2,1,0:T(8,128)(2,1)S(1)}, u32[]{:S(2)}, u32[]{:S(2)}) async-start(bf16[16,24,768]{2,1,0:T(8,128)(2,1)} %broadcast_in_dim.2), calls=%async_computation.2 | async-start | bytes 1179648 | tf_op jit(solution)/shard_map/all_to_all | solution.py:38
  128.6 0.1 reduce_sum.18
  128.7 22.8 %all-to-all-done.2 = bf16[16,24,768]{2,1,0:T(8,128)(2,1)S(1)} async-done(((bf16[16,24,768]{2,1,0:T(8,128)(2,1)}), bf16[16,24,768]{2,1,0:T(8,128)(2,1)S(1)}, u32[]{:S(2)}, u32[]{:S(2)}) %all-to-all-start.2) | async-done | bytes 589856 | tf_op jit(solution)/shard_map/all_to_all | solution.py:38
  151.5 0.1 slice_negate_fusion
  151.6 8.1 %all-gather.2.cloned.1.call-done = bf16[2,384,1536]{2,1,0:T(8,128)(2,1)} async-done(((bf16[2,24,1536]{2,1,0:T(8,128)(2,1)}), bf16[2,384,1536]{2,1,0:T(8,128)(2,1)}) %all-gather.2.cloned.1.call-update) | async-done | bytes 2359312 | tf_op jit(solution)/shard_map/all_gather | solution.py:98
  159.7 2.2 %convolution_convert_fusion = bf16[24,2,1536]{2,0,1:T(8,128)(2,1)S(1)} fusion(bf16[768,1536,1]{1,0,2:T(8,128)(2,1)} %bitcast.60, bf16[24,1,768]{2,0,1:T(8,128)(2,1)S(1)} %get-tuple-element.25, bf16[24,1,768]{2,0,1:T(8,128)(2,1)S(1)} %get-tuple-element.24), kind=kOutput, calls=%fused_computation.22 | convolution fusion | flops 113356800 | bytes 2580480 | tf_op jit(solution)/shard_map/dot_general | solution.py:101
  161.9 0.1 reshape_squeeze.15
  162.0 0.1 reshape_squeeze.16
  162.1 0.3 fusion.14
  162.4 0.7 convert_element_type.83
  (3 shorter events, 0.0 us)
Async XLA Ops:
  12.0 5.1 %copy-start = (bf16[1,2,3,1024,384]{4,3,2,1,0:T(8,128)(2,1)S(1)}, bf16[1,2,3,1024,384]{4,3,2,1,0:T(8,128)(2,1)}, u32[]{:S(2)}) copy-start(bf16[1,2,3,1024,384]{4,3,2,1,0:T(8,128)(2,1)} %param.3) | copy-start | bytes 14155780
  41.9 45.1 %all-to-all-start.1 = ((f32[16,24,768]{2,1,0:T(8,128)}), f32[16,24,768]{2,1,0:T(8,128)S(1)}, u32[]{:S(2)}, u32[]{:S(2)}) async-start(f32[16,24,768]{2,1,0:T(8,128)} %bitcast.63), calls=%async_computation.1 | async-start | bytes 2359296 | tf_op jit(solution)/shard_map/all_to_all | solution.py:20
  52.9 106.8 %all-gather.2.cloned.1.call-start = ((), (), s32[]{:S(2)}) async-start(), calls=%async_computation.3 | async-start | bytes 2506752 | tf_op jit(solution)/shard_map/all_gather | solution.py:98
  86.9 36.0 %all-to-all-start = ((f32[16,24,768]{2,1,0:T(8,128)}), f32[16,24,768]{2,1,0:T(8,128)S(1)}, u32[]{:S(2)}, u32[]{:S(2)}) async-start(f32[16,24,768]{2,1,0:T(8,128)} %bitcast.12), calls=%async_computation | async-start | bytes 2359296 | tf_op jit(solution)/shard_map/all_to_all | solution.py:20
  90.8 1.3 collective-permute-start
  92.1 4.0 %collective-permute-start.1 = (bf16[24,768]{1,0:T(8,128)(2,1)S(1)}, bf16[24,768]{1,0:T(8,128)(2,1)S(1)}, u32[]{:S(2)}, u32[]{:S(2)}) collective-permute-start(bf16[24,768]{1,0:T(8,128)(2,1)S(1)} %collective-permute-done), channel_id=1, source_target_pairs={{0,32},{16,48},{32,0},{48,16},{64,96},{80,112},{96,64},{112,80},{1... | collective-permute-start | bytes 110600 | tf_op jit(solution)/shard_map/ppermute | solution.py:27
  96.2 4.0 %collective-permute-start.2 = (bf16[24,768]{1,0:T(8,128)(2,1)S(1)}, bf16[24,768]{1,0:T(8,128)(2,1)S(1)}, u32[]{:S(2)}, u32[]{:S(2)}) collective-permute-start(bf16[24,768]{1,0:T(8,128)(2,1)S(1)} %collective-permute-done.1), channel_id=1, source_target_pairs={{0,64},{16,80},{32,96},{48,112},{64,0},{80,16},{96,32},{112,48},{1... | collective-permute-start | bytes 110600 | tf_op jit(solution)/shard_map/ppermute | solution.py:27
  100.1 22.9 %collective-permute-start.3 = (bf16[24,768]{1,0:T(8,128)(2,1)S(1)}, bf16[24,768]{1,0:T(8,128)(2,1)S(1)}, u32[]{:S(2)}, u32[]{:S(2)}) collective-permute-start(bf16[24,768]{1,0:T(8,128)(2,1)S(1)} %collective-permute-done.2), channel_id=1, source_target_pairs={{0,128},{16,144},{32,160},{48,176},{64,192},{80,208},{96,224},{112... | collective-permute-start | bytes 110600 | tf_op jit(solution)/shard_map/ppermute | solution.py:27
  123.8 27.7 %all-to-all-start.2 = ((bf16[16,24,768]{2,1,0:T(8,128)(2,1)}), bf16[16,24,768]{2,1,0:T(8,128)(2,1)S(1)}, u32[]{:S(2)}, u32[]{:S(2)}) async-start(bf16[16,24,768]{2,1,0:T(8,128)(2,1)} %broadcast_in_dim.2), calls=%async_computation.2 | async-start | bytes 1179648 | tf_op jit(solution)/shard_map/all_to_all | solution.py:38
Sparse Core Ops, SparseCore 0:
  56.3 103.3 all-gather.1
where the time goes:
time: 170 us
  waiting for transfers between devices  65.9 us (39%)
  other arithmetic  40 us (24%)
  starting transfers between devices  23.3 us (14%)
  matrix products  22.3 us (13%)
  between operations  13.5 us (8%)
  local copies, waits for them, and re-layouts  4.88 us (3%)
    another operation x4, other arithmetic, phase_gram(): right = jnp.stack([upper, lower]).reshape(2 * COLORS * sites_dev, 2 * nvec)  28.2 us
    all_to_all x2, waiting for transfers between devices, sum_at_owner(): lax.all_to_all(parts, axis, split_axis=0, concat_axis=0, tiled=True)  26.7 us
    all_to_all x1, waiting for transfers between devices, from_everyone(): return lax.all_to_all(copies, axis, split_axis=0, concat_axis=0, tiled=True)  22.8 us
    dot_general x2, matrix products, phase_gram(): lax.dot_general(left, right, (((0,), (0,)), ((), ())), preferred_element_...  19.8 us
    all_to_all x2, starting transfers between devices, sum_at_owner(): lax.all_to_all(parts, axis, split_axis=0, concat_axis=0, tiled=True)  14.8 us
    ppermute x4, waiting for transfers between devices, partner(): return lax.ppermute(value, axis, pairs)  8.2 us
    all_gather x1, waiting for transfers between devices, local(): piece = lax.all_gather(tau, 'space', axis=1, tiled=True)  8.14 us
    neg x1, other arithmetic, phase_gram(): lower = jnp.concatenate([phased_im, -phased_re], axis=-1)  5.05 us
  transfers between devices with their start and end apart: 8, of which 7 were waited for; matrix products, arithmetic and copies ran while one was open for 17% of the time, Pallas kernels for 0%

commit v1 on v0

v1 whole, which is shorter than its diff:
```python
import functools, math
import jax, jax.numpy as jnp
from jax import lax
from jax.experimental import pallas as pl
from jax.experimental.pallas import tpu as pltpu
from jax.sharding import PartitionSpec as P

LAT=32
LANES=128


def phase_of(winding):
    octant = winding + 4
    quadrant = (octant >> 3) & 3
    angle = ((octant & 7) - 4).astype(jnp.float32) * (2.0 * math.pi / LAT)
    square = angle * angle
    sine = angle * (1 + square * (-1 / 6 + square * (1 / 120 + square * (-1 / 5040 + square * (1 / 362880)))))
    cosine = 1 + square * (-1 / 2 + square * (1 / 24 + square * (-1 / 720 + square * (1 / 40320 - square * (1 / 3628800)))))
    swap = (quadrant & 1) == 1
    cos_out = jnp.where(swap, sine, cosine)
    sin_out = jnp.where(swap, cosine, sine)
    cos_out = jnp.where((quadrant == 1) | (quadrant == 2), -cos_out, cos_out)
    sin_out = jnp.where(quadrant >= 2, -sin_out, sin_out)
    return cos_out, sin_out


def gram_kernel(which, split, momenta, vec_ref, *refs):
    left_ref, right_ref, acc_ref = refs[-3:]
    step = pl.program_id(0)
    _, _, colors, sites, nvec = vec_ref.shape
    space = lax.axis_index("space")
    half = space // 8
    row = lax.broadcasted_iota(jnp.int32, (sites, LANES), 0) + step * sites
    winding = momenta[which, 0] * (row & 31) + momenta[which, 1] * (row >> 5) + momenta[which, 2] * space
    cosine, sine = phase_of(winding & 31)
    cosine = jnp.concatenate([cosine] * (nvec // LANES), axis=1)
    sine = jnp.concatenate([sine] * (nvec // LANES), axis=1)
    for color in range(colors):
        re = vec_ref[0, 0, color]
        im = vec_ref[0, 1, color]
        re32 = re.astype(jnp.float32)
        im32 = im.astype(jnp.float32)
        at = pl.ds(color * sites, sites)
        right_ref[at, :nvec] = (cosine * re32 + sine * im32).astype(jnp.bfloat16)
        right_ref[at, nvec:] = (cosine * im32 - sine * re32).astype(jnp.bfloat16)
        left_ref[at, :nvec] = re
        left_ref[at, nvec:] = im
    part = lax.dot_general(left_ref[...], right_ref[...], (((0,), (0,)), ((), ())), preferred_element_type=jnp.float32)
    @pl.when(step == 0)
    def _():
        acc_ref[...] = part
    @pl.when(step > 0)
    def _():
        acc_ref[...] += part
    @pl.when(step == pl.num_programs(0) - 1)
    def _():
        def put(out_ref, start):
            rows = out_ref.shape[0]
            real = pl.ds(start, rows)
            imag = pl.ds(start + nvec, rows)
            out_ref[:, :nvec] = (acc_ref[real, :nvec] + acc_ref[imag, nvec:]).astype(out_ref.dtype)
            out_ref[:, nvec:] = (acc_ref[real, nvec:] - acc_ref[imag, :nvec]).astype(out_ref.dtype)

        if split:
            rows = nvec // 2
            put(refs[0], pl.multiple_of((1 - half) * rows, rows))
            put(refs[1], pl.multiple_of(half * rows, rows))
        else:
            put(refs[0], 0)


def gram(eigvec, momenta, which, split, chunk=256):
    _, _, colors, sites, nvec = eigvec.shape
    depth = colors * chunk
    if split:
        outs = [((nvec // 2, 2 * nvec), jnp.bfloat16), ((nvec // 2, 2 * nvec), jnp.float32)]
    else:
        outs = [((nvec, 2 * nvec), jnp.bfloat16)]
    return pl.pallas_call(
        functools.partial(gram_kernel, which, split),
        grid_spec=pltpu.PrefetchScalarGridSpec(
            num_scalar_prefetch=1,
            grid=(sites // chunk,),
            in_specs=[pl.BlockSpec((1, 2, colors, chunk, nvec), lambda i, m: (0, 0, 0, i, 0))],
            out_specs=[pl.BlockSpec(shape, lambda i, m: (0, 0)) for shape, _ in outs],
            scratch_shapes=[
                pltpu.VMEM((depth, 2 * nvec), jnp.bfloat16),
                pltpu.VMEM((depth, 2 * nvec), jnp.bfloat16),
                pltpu.VMEM((2 * nvec, 2 * nvec), jnp.float32),
            ],
        ),
        out_shape=[jax.ShapeDtypeStruct(shape, kind) for shape, kind in outs],
        compiler_params=pltpu.CompilerParams(
            dimension_semantics=("arbitrary",), vmem_limit_bytes=62 << 20
        ),
        cost_estimate=pl.CostEstimate(
            flops=8 * nvec * nvec * colors * sites, bytes_accessed=eigvec.size * 2, transcendentals=0
        ),
    )(momenta, eigvec)


Z_GROUPS = [list(range(8)), list(range(8, 16))]
SPIN = 4


def exchange(parts, groups=None):
    return lax.all_to_all(parts, "space", split_axis=0, concat_axis=0, tiled=True, axis_index_groups=groups)


def swap(value, bit):
    return lax.ppermute(value, "space", [(i, i ^ bit) for i in range(16)])


def total(parts):
    return parts.astype(jnp.float32).sum(axis=0).astype(jnp.bfloat16)


def steps(eigvec, momenta, peram):
    tau = peram[0]
    nrows, nvec = tau.shape[1], tau.shape[3]
    place = lax.axis_index("space")
    spins = jnp.broadcast_to(tau.transpose(2, 0, 1, 3).reshape(2, 1, 2, 2, nrows, nvec), (2, 4, 2, 2, nrows, nvec))
    tau = exchange(spins.reshape(16, 2, nrows, nvec))
    tau = tau.transpose(1, 0, 2, 3).reshape(2 * nvec, nvec)
    (source,) = gram(eigvec, momenta, 1, False)
    source = exchange(source.reshape(16, nrows, 2 * nvec))
    share = total(source)
    share = lax.ppermute(share, "tm", [(t, 15 - t) for t in range(16)])
    source = exchange(jnp.broadcast_to(share, (16, *share.shape)))
    send, keep = gram(eigvec, momenta, 0, True)
    arrived = swap(send, 8)
    pair = (keep + arrived.astype(jnp.float32)).astype(jnp.bfloat16)
    parts = exchange(pair.reshape(8, nrows, 2 * nvec), Z_GROUPS)
    rows = total(parts)[None]
    rows = jnp.concatenate([rows, swap(rows, 1)])
    rows = jnp.concatenate([rows, swap(rows, 8)])
    rows_re, rows_im = rows[..., :nvec], rows[..., nvec:]
    left = jnp.concatenate(
        [jnp.concatenate([rows_re, -rows_im], axis=-1), jnp.concatenate([rows_im, rows_re], axis=-1)], axis=1
    ).reshape(8 * nrows, 2 * nvec)
    mixed = jnp.dot(left, tau, preferred_element_type=jnp.float32).astype(jnp.bfloat16)
    mixed = mixed.reshape(2, 2, 2, nrows, nvec)
    mixed = jnp.stack([mixed[0], swap(mixed[1], 8)])
    mixed = jnp.stack([mixed[:, 0], swap(mixed[:, 1], 1)], axis=1)
    mixed = jnp.where(place % 2 == 1, mixed[:, ::-1], mixed)
    mixed = jnp.where(place // 8 == 1, mixed[::-1], mixed)
    mixed = mixed.transpose(3, 0, 1, 2, 4).reshape(nrows * SPIN, 2 * nvec)
    source = source.reshape(nvec, 2 * nvec)
    source_re, source_im = source[:, :nvec], source[:, nvec:]
    right = jnp.concatenate([source, jnp.concatenate([-source_im, source_re], axis=1)], axis=0)
    dressed = jnp.dot(mixed, right, preferred_element_type=jnp.float32)
    return dressed.reshape(1, nrows, SPIN, 2, nvec).astype(jnp.bfloat16)


def solution(mesh):
    return jax.shard_map(
        steps,
        mesh=mesh,
        in_specs=(P("tm", None, None, "space", None), P(), P("tm", None, "space", None, None)),
        out_specs=P("tm", "space", None, None, None),
        check_vma=False,
    )
```

time: 170 us -> 130 us (0.76)
  other arithmetic: 40 us -> 2.29 us
  matrix products: 22.3 us -> 0.82 us
  starting transfers between devices: 23.3 us -> 43.7 us
  Pallas kernels: 0 us -> 19.8 us
  between operations: 13.5 us -> 0.18 us
  waiting for transfers between devices: 65.9 us -> 59 us
    ppermute x4 -> x6, waiting for transfers between devices: 8.2 us -> 37.6 us  [the longest x5 33.5 us: swap(): return lax.ppermute(value, 'space', [(i, i ^ bit) for i in range(16)])]
    another operation x5 -> x1, other arithmetic: 28.2 us -> 0.02 us  [steps(): mixed = jnp.stack([mixed[:, 0], swap(mixed[:, 1], 1)], axis=1)]
    all_to_all x3 -> x4, waiting for transfers between devices: 49.6 us -> 21.4 us  [exchange(): lax.all_to_all(parts, 'space', split_axis=0, concat_axis=0, tiled=True, a...]
    dot_general x4 -> x2, matrix products: 22.3 us -> 0.82 us  [the longest x1 0.51 us: steps(): dressed = jnp.dot(mixed, right, preferred_element_type=jnp.float32)]
    pallas_call x0 -> x2, Pallas kernels: none -> 19.8 us  [gram(): pl.pallas_call(functools.partial(gram_kernel, which, split), grid_spec=pl...]
    all_to_all x3 -> x4, starting transfers between devices: 19.6 us -> 30.6 us  [exchange(): lax.all_to_all(parts, 'space', split_axis=0, concat_axis=0, tiled=True, a...]
    ppermute x4 -> x6, starting transfers between devices: 3.46 us -> 13.1 us  [the longest x5 13 us: swap(): return lax.ppermute(value, 'space', [(i, i ^ bit) for i in range(16)])]
    all_gather x1 -> x0, waiting for transfers between devices: 8.14 us -> none  [local(): piece = lax.all_gather(tau, 'space', axis=1, tiled=True)]
  transfers between devices with their start and end apart: 8 -> 10, of which waited for: 7 -> 9; matrix products, arithmetic and copies ran while one was open for 17% -> 1% of each run, Pallas kernels for 0% -> 8%
where the time goes in v1:
time: 130 us; the launch traced here: 129 us
  waiting for transfers between devices  59 us (45%)
  starting transfers between devices  43.7 us (34%)
  Pallas kernels  19.8 us (15%)
  local copies, waits for them, and re-layouts  3.47 us (3%)
  other arithmetic  2.29 us (2%)
    ppermute x5, waiting for transfers between devices, swap(): return lax.ppermute(value, 'space', [(i, i ^ bit) for i in range(16)])  33.5 us
    all_to_all x4, starting transfers between devices, exchange(): lax.all_to_all(parts, 'space', split_axis=0, concat_axis=0, tiled=True, a...  30.6 us
    all_to_all x4, waiting for transfers between devices, exchange(): lax.all_to_all(parts, 'space', split_axis=0, concat_axis=0, tiled=True, a...  21.4 us
    pallas_call x2, Pallas kernels, gram(): pl.pallas_call(functools.partial(gram_kernel, which, split), grid_spec=pl...  19.8 us
    ppermute x5, starting transfers between devices, swap(): return lax.ppermute(value, 'space', [(i, i ^ bit) for i in range(16)])  13 us
    ppermute x1, waiting for transfers between devices, steps(): share = lax.ppermute(share, 'tm', [(t, 15 - t) for t in range(16)])  4.16 us
  transfers between devices with their start and end apart: 10, of which 9 were waited for; matrix products, arithmetic and copies ran while one was open for 1% of the time, Pallas kernels for 8%

profile of v1, /device:TPU:8, one launch (start us, length us, event | category | flops | bytes accessed | tf_op | source)
XLA Modules:
  0.0 129.2 jit_solution(2696280483324487106)
XLA Ops:
  0.0 9.9 %shard_map.37 = (bf16[192,768]{1,0:T(8,128)(2,1)}, f32[192,768]{1,0:T(8,128)}) custom-call(s32[2,3]{1,0:T(2,128)} %momenta.3, bf16[1,2,3,1024,384]{4,3,2,1,0:T(8,128)(2,1)} %vec_ref.3), custom_call_target="tpu_custom_call" | custom-call | flops 3623878656 | bytes 4718592 | tf_op jit(solution)/shard_map/pallas_call | solution.py:79
  9.9 3.0 %collective-permute-start = (bf16[192,768]{1,0:T(8,128)(2,1)}, bf16[192,768]{1,0:T(8,128)(2,1)S(1)}, u32[]{:S(2)}, u32[]{:S(2)}) collective-permute-start(bf16[192,768]{1,0:T(8,128)(2,1)} %get-tuple-element.8), channel_id=1, source_target_pairs={{0,8},{1,9},{2,10},{3,11},{4,12},{5,13},{6,14},{7,15},{8,0},{9,1},... | collective-permute-start | bytes 884744 | tf_op jit(solution)/shard_map/ppermute | solution.py:111
  13.0 7.4 %collective-permute-done = bf16[192,768]{1,0:T(8,128)(2,1)S(1)} collective-permute-done((bf16[192,768]{1,0:T(8,128)(2,1)}, bf16[192,768]{1,0:T(8,128)(2,1)S(1)}, u32[]{:S(2)}, u32[]{:S(2)}) %collective-permute-start) | collective-permute-done | bytes 294944 | tf_op jit(solution)/shard_map/ppermute | solution.py:111
  20.4 1.8 %add_convert_fusion = bf16[192,768]{1,0:T(8,128)(2,1)} fusion(f32[192,768]{1,0:T(8,128)} %get-tuple-element.7, bf16[192,768]{1,0:T(8,128)(2,1)S(1)} %collective-permute-done), kind=kLoop, calls=%fused_computation.4 | loop fusion | flops 442368 | bytes 1179648 | tf_op jit(solution)/shard_map/convert_element_type | solution.py:132
  22.2 8.5 %all-to-all-start = ((bf16[8,24,768]{2,1,0:T(8,128)(2,1)}), bf16[8,24,768]{2,1,0:T(8,128)(2,1)S(1)}, u32[]{:S(2)}, u32[]{:S(2)}) async-start(bf16[8,24,768]{2,1,0:T(8,128)(2,1)} %bitcast), calls=%async_computation | async-start | bytes 589824 | tf_op jit(solution)/shard_map/all_to_all | solution.py:107
  30.7 9.8 %shard_map.38 = bf16[384,768]{1,0:T(8,128)(2,1)} custom-call(s32[2,3]{1,0:T(2,128)} %momenta.3, bf16[1,2,3,1024,384]{4,3,2,1,0:T(8,128)(2,1)} %vec_ref.3), custom_call_target="tpu_custom_call" | custom-call | flops 3623878656 | bytes 4718592 | tf_op jit(solution)/shard_map/pallas_call | solution.py:79
  40.5 0.0 copy-start
  40.5 1.9 %all-to-all-done = bf16[8,24,768]{2,1,0:T(8,128)(2,1)S(1)} async-done(((bf16[8,24,768]{2,1,0:T(8,128)(2,1)}), bf16[8,24,768]{2,1,0:T(8,128)(2,1)S(1)}, u32[]{:S(2)}, u32[]{:S(2)}) %all-to-all-start) | async-done | bytes 294944 | tf_op jit(solution)/shard_map/all_to_all | solution.py:107
  42.4 8.0 %all-to-all-start.2 = ((bf16[16,24,768]{2,1,0:T(8,128)(2,1)}), bf16[16,24,768]{2,1,0:T(8,128)(2,1)S(1)}, u32[]{:S(2)}, u32[]{:S(2)}) async-start(bf16[16,24,768]{2,1,0:T(8,128)(2,1)} %bitcast.43), calls=%async_computation.2 | async-start | bytes 1179648 | tf_op jit(solution)/shard_map/all_to_all | solution.py:107
  50.5 0.0 copy-done
  50.5 16.4 %all-to-all-done.2 = bf16[16,24,768]{2,1,0:T(8,128)(2,1)S(1)} async-done(((bf16[16,24,768]{2,1,0:T(8,128)(2,1)}), bf16[16,24,768]{2,1,0:T(8,128)(2,1)S(1)}, u32[]{:S(2)}, u32[]{:S(2)}) %all-to-all-start.2) | async-done | bytes 589856 | tf_op jit(solution)/shard_map/all_to_all | solution.py:107
  66.9 0.9 broadcast_in_dim.15
  67.8 5.3 %all-to-all-start.1 = ((bf16[16,2,24,384]{3,2,1,0:T(8,128)(2,1)}), bf16[16,2,24,384]{3,2,1,0:T(8,128)(2,1)S(1)}, u32[]{:S(2)}, u32[]{:S(2)}) async-start(bf16[16,2,24,384]{3,2,1,0:T(8,128)(2,1)} %bitcast.6), calls=%async_computation.1 | async-start | bytes 1179648 | tf_op jit(solution)/shard_map/all_to_all | solution.py:107
  73.2 2.0 %collective-permute-start.1 = (bf16[1,24,768]{2,1,0:T(8,128)(2,1)S(1)}, bf16[1,24,768]{2,1,0:T(8,128)(2,1)S(1)}, u32[]{:S(2)}, u32[]{:S(2)}) collective-permute-start(bf16[1,24,768]{2,1,0:T(8,128)(2,1)S(1)} %bitcast.45), channel_id=1, source_target_pairs={{0,1},{1,0},{2,3},{3,2},{4,5},{5,4},{6,7},{7,6},{8,9},{9,8},{10,11... | collective-permute-start | bytes 110600 | tf_op jit(solution)/shard_map/ppermute | solution.py:111
  75.2 12.0 %collective-permute-done.1 = bf16[1,24,768]{2,1,0:T(8,128)(2,1)S(1)} collective-permute-done((bf16[1,24,768]{2,1,0:T(8,128)(2,1)S(1)}, bf16[1,24,768]{2,1,0:T(8,128)(2,1)S(1)}, u32[]{:S(2)}, u32[]{:S(2)}) %collective-permute-start.1) | collective-permute-done | bytes 36896 | tf_op jit(solution)/shard_map/ppermute | solution.py:111
  87.2 3.2 %collective-permute-start.2 = (bf16[2,24,768]{2,1,0:T(8,128)(2,1)S(1)}, bf16[2,24,768]{2,1,0:T(8,128)(2,1)S(1)}, u32[]{:S(2)}, u32[]{:S(2)}) collective-permute-start(bf16[2,24,768]{2,1,0:T(8,128)(2,1)S(1)} %pad_maximum_fusion.3), channel_id=1, source_target_pairs={{0,8},{1,9},{2,10},{3,11},{4,12},{5,13},{6,14},{7,15},{8,0},{9,1},... | collective-permute-start | bytes 221192 | tf_op jit(solution)/shard_map/ppermute | solution.py:111
  90.4 2.7 %collective-permute-done.2 = bf16[2,24,768]{2,1,0:T(8,128)(2,1)S(1)} collective-permute-done((bf16[2,24,768]{2,1,0:T(8,128)(2,1)S(1)}, bf16[2,24,768]{2,1,0:T(8,128)(2,1)S(1)}, u32[]{:S(2)}, u32[]{:S(2)}) %collective-permute-start.2) | collective-permute-done | bytes 73760 | tf_op jit(solution)/shard_map/ppermute | solution.py:111
  93.2 0.1 reduce_sum.25
  93.3 0.1 collective-permute-start.5
  93.4 0.0 all-to-all-done.1
  93.4 0.1 copy.14
  93.5 4.2 %collective-permute-done.5 = bf16[24,768]{1,0:T(8,128)(2,1)S(1)} collective-permute-done((bf16[24,768]{1,0:T(8,128)(2,1)S(1)}, bf16[24,768]{1,0:T(8,128)(2,1)S(1)}, u32[]{:S(2)}, u32[]{:S(2)}) %collective-permute-start.5) | collective-permute-done | bytes 36896 | tf_op jit(solution)/shard_map/ppermute | solution.py:128
  97.6 0.9 broadcast_in_dim.16
  98.5 8.7 %all-to-all-start.3 = ((bf16[16,24,768]{2,1,0:T(8,128)(2,1)}), bf16[16,24,768]{2,1,0:T(8,128)(2,1)S(1)}, u32[]{:S(2)}, u32[]{:S(2)}) async-start(bf16[16,24,768]{2,1,0:T(8,128)(2,1)} %broadcast_in_dim.16), calls=%async_computation.3 | async-start | bytes 1179648 | tf_op jit(solution)/shard_map/all_to_all | solution.py:107
  107.2 0.3 convolution_convert_fusion
  107.6 3.5 %collective-permute-start.3 = (bf16[2,2,24,384]{3,2,1,0:T(8,128)(2,1)S(1)}, bf16[2,2,24,384]{3,2,1,0:T(8,128)(2,1)S(1)}, u32[]{:S(2)}, u32[]{:S(2)}) collective-permute-start(bf16[2,2,24,384]{3,2,1,0:T(8,128)(2,1)S(1)} %bitcast.52), channel_id=1, source_target_pairs={{0,8},{1,9},{2,10},{3,11},{4,12},{5,13},{6,14},{7,15},{8,0},{9,1},... | collective-permute-start | bytes 221192 | tf_op jit(solution)/shard_map/ppermute | solution.py:111
  111.1 3.7 %collective-permute-done.3 = bf16[2,2,24,384]{3,2,1,0:T(8,128)(2,1)S(1)} collective-permute-done((bf16[2,2,24,384]{3,2,1,0:T(8,128)(2,1)S(1)}, bf16[2,2,24,384]{3,2,1,0:T(8,128)(2,1)S(1)}, u32[]{:S(2)}, u32[]{:S(2)}) %collective-permute-start.3) | collective-permute-done | bytes 73760 | tf_op jit(solution)/shard_map/ppermute | solution.py:111
  114.8 1.2 collective-permute-start.4
  116.0 7.7 %collective-permute-done.4 = bf16[2,2,24,384]{3,2,1,0:T(8,128)(2,1)S(1)} collective-permute-done((bf16[2,2,24,384]{3,2,1,0:T(8,128)(2,1)S(1)}, bf16[2,2,24,384]{3,2,1,0:T(8,128)(2,1)S(1)}, u32[]{:S(2)}, u32[]{:S(2)}) %collective-permute-start.4) | collective-permute-done | bytes 73760 | tf_op jit(solution)/shard_map/ppermute | solution.py:111
  123.8 0.1 copy.16
  123.9 0.1 reshape.37
  124.0 3.1 %all-to-all-done.3 = bf16[16,24,768]{2,1,0:T(8,128)(2,1)S(1)} async-done(((bf16[16,24,768]{2,1,0:T(8,128)(2,1)}), bf16[16,24,768]{2,1,0:T(8,128)(2,1)S(1)}, u32[]{:S(2)}, u32[]{:S(2)}) %all-to-all-start.3) | async-done | bytes 589856 | tf_op jit(solution)/shard_map/all_to_all | solution.py:107
  127.1 0.1 slice_negate_fusion
  127.2 0.1 maximum_bitcast_fusion
  127.3 0.6 copy.17
  127.9 0.5 fusion
  128.5 0.8 copy.18
  (11 shorter events, 0.3 us)
Async XLA Ops:
  9.9 10.5 %collective-permute-start = (bf16[192,768]{1,0:T(8,128)(2,1)}, bf16[192,768]{1,0:T(8,128)(2,1)S(1)}, u32[]{:S(2)}, u32[]{:S(2)}) collective-permute-start(bf16[192,768]{1,0:T(8,128)(2,1)} %get-tuple-element.8), channel_id=1, source_target_pairs={{0,8},{1,9},{2,10},{3,11},{4,12},{5,13},{6,14},{7,15},{8,0},{9,1},... | collective-permute-start | bytes 884744 | tf_op jit(solution)/shard_map/ppermute | solution.py:111
  22.2 20.2 %all-to-all-start = ((bf16[8,24,768]{2,1,0:T(8,128)(2,1)}), bf16[8,24,768]{2,1,0:T(8,128)(2,1)S(1)}, u32[]{:S(2)}, u32[]{:S(2)}) async-start(bf16[8,24,768]{2,1,0:T(8,128)(2,1)} %bitcast), calls=%async_computation | async-start | bytes 589824 | tf_op jit(solution)/shard_map/all_to_all | solution.py:107
  40.5 9.9 %copy-start = (bf16[1,2,24,4,384]{4,3,2,1,0:T(4,128)(2,1)S(1)}, bf16[1,2,24,4,384]{4,3,2,1,0:T(4,128)(2,1)}, u32[]{:S(2)}) copy-start(bf16[1,2,24,4,384]{4,3,2,1,0:T(4,128)(2,1)} %param.5) | copy-start | bytes 442372
  42.4 24.5 %all-to-all-start.2 = ((bf16[16,24,768]{2,1,0:T(8,128)(2,1)}), bf16[16,24,768]{2,1,0:T(8,128)(2,1)S(1)}, u32[]{:S(2)}, u32[]{:S(2)}) async-start(bf16[16,24,768]{2,1,0:T(8,128)(2,1)} %bitcast.43), calls=%async_computation.2 | async-start | bytes 1179648 | tf_op jit(solution)/shard_map/all_to_all | solution.py:107
  67.8 25.6 %all-to-all-start.1 = ((bf16[16,2,24,384]{3,2,1,0:T(8,128)(2,1)}), bf16[16,2,24,384]{3,2,1,0:T(8,128)(2,1)S(1)}, u32[]{:S(2)}, u32[]{:S(2)}) async-start(bf16[16,2,24,384]{3,2,1,0:T(8,128)(2,1)} %bitcast.6), calls=%async_computation.1 | async-start | bytes 1179648 | tf_op jit(solution)/shard_map/all_to_all | solution.py:107
  73.2 14.0 %collective-permute-start.1 = (bf16[1,24,768]{2,1,0:T(8,128)(2,1)S(1)}, bf16[1,24,768]{2,1,0:T(8,128)(2,1)S(1)}, u32[]{:S(2)}, u32[]{:S(2)}) collective-permute-start(bf16[1,24,768]{2,1,0:T(8,128)(2,1)S(1)} %bitcast.45), channel_id=1, source_target_pairs={{0,1},{1,0},{2,3},{3,2},{4,5},{5,4},{6,7},{7,6},{8,9},{9,8},{10,11... | collective-permute-start | bytes 110600 | tf_op jit(solution)/shard_map/ppermute | solution.py:111
  87.2 5.9 %collective-permute-start.2 = (bf16[2,24,768]{2,1,0:T(8,128)(2,1)S(1)}, bf16[2,24,768]{2,1,0:T(8,128)(2,1)S(1)}, u32[]{:S(2)}, u32[]{:S(2)}) collective-permute-start(bf16[2,24,768]{2,1,0:T(8,128)(2,1)S(1)} %pad_maximum_fusion.3), channel_id=1, source_target_pairs={{0,8},{1,9},{2,10},{3,11},{4,12},{5,13},{6,14},{7,15},{8,0},{9,1},... | collective-permute-start | bytes 221192 | tf_op jit(solution)/shard_map/ppermute | solution.py:111
  93.3 4.4 %collective-permute-start.5 = (bf16[24,768]{1,0:T(8,128)(2,1)S(1)}, bf16[24,768]{1,0:T(8,128)(2,1)S(1)}, u32[]{:S(2)}, u32[]{:S(2)}) collective-permute-start(bf16[24,768]{1,0:T(8,128)(2,1)S(1)} %reduce_sum.25), channel_id=1, source_target_pairs={{0,240},{16,224},{32,208},{48,192},{64,176},{80,160},{96,144},{112... | collective-permute-start | bytes 110600 | tf_op jit(solution)/shard_map/ppermute | solution.py:128
  98.5 28.6 %all-to-all-start.3 = ((bf16[16,24,768]{2,1,0:T(8,128)(2,1)}), bf16[16,24,768]{2,1,0:T(8,128)(2,1)S(1)}, u32[]{:S(2)}, u32[]{:S(2)}) async-start(bf16[16,24,768]{2,1,0:T(8,128)(2,1)} %broadcast_in_dim.16), calls=%async_computation.3 | async-start | bytes 1179648 | tf_op jit(solution)/shard_map/all_to_all | solution.py:107
  107.6 7.2 %collective-permute-start.3 = (bf16[2,2,24,384]{3,2,1,0:T(8,128)(2,1)S(1)}, bf16[2,2,24,384]{3,2,1,0:T(8,128)(2,1)S(1)}, u32[]{:S(2)}, u32[]{:S(2)}) collective-permute-start(bf16[2,2,24,384]{3,2,1,0:T(8,128)(2,1)S(1)} %bitcast.52), channel_id=1, source_target_pairs={{0,8},{1,9},{2,10},{3,11},{4,12},{5,13},{6,14},{7,15},{8,0},{9,1},... | collective-permute-start | bytes 221192 | tf_op jit(solution)/shard_map/ppermute | solution.py:111
  114.8 8.9 %collective-permute-start.4 = (bf16[2,2,24,384]{3,2,1,0:T(8,128)(2,1)S(1)}, bf16[2,2,24,384]{3,2,1,0:T(8,128)(2,1)S(1)}, u32[]{:S(2)}, u32[]{:S(2)}) collective-permute-start(bf16[2,2,24,384]{3,2,1,0:T(8,128)(2,1)S(1)} %get-tuple-element.12), channel_id=1, source_target_pairs={{0,1},{1,0},{2,3},{3,2},{4,5},{5,4},{6,7},{7,6},{8,9},{9,8},{10,11... | collective-permute-start | bytes 221192 | tf_op jit(solution)/shard_map/ppermute | solution.py:111

commit v2 on v1

v2 whole, which is shorter than its diff:
```python
import functools, math
import jax, jax.numpy as jnp
from jax import lax
from jax.experimental import pallas as pl
from jax.experimental.pallas import tpu as pltpu
from jax.sharding import PartitionSpec as P

LAT=32
LANES = 128
MEMBER_BITS = (0, 1, 8, 9)
QUAD_BITS = (0, 2, 4, 6)


def phase_of(winding):
    octant = winding + 4
    quadrant = (octant >> 3) & 3
    angle = ((octant & 7) - 4).astype(jnp.float32) * (2.0 * math.pi / LAT)
    square = angle * angle
    sine = angle * (1 + square * (-1 / 6 + square * (1 / 120 + square * (-1 / 5040 + square * (1 / 362880)))))
    cosine = 1 + square * (-1 / 2 + square * (1 / 24 + square * (-1 / 720 + square * (1 / 40320 - square * (1 / 3628800)))))
    swap = (quadrant & 1) == 1
    cos_out = jnp.where(swap, sine, cosine)
    sin_out = jnp.where(swap, cosine, sine)
    cos_out = jnp.where((quadrant == 1) | (quadrant == 2), -cos_out, cos_out)
    sin_out = jnp.where(quadrant >= 2, -sin_out, sin_out)
    return cos_out, sin_out


def gram_kernel(which, momenta, vec_ref, keep_ref, *refs):
    send_refs = refs[:3]
    left_ref, right_ref, acc_ref = refs[3:]
    step = pl.program_id(0)
    _, _, colors, sites, nvec = vec_ref.shape
    space = lax.axis_index("space")
    row = lax.broadcasted_iota(jnp.int32, (sites, LANES), 0) + step * sites
    winding = momenta[which, 0] * (row & 31) + momenta[which, 1] * (row >> 5) + momenta[which, 2] * space
    cosine, sine = phase_of(winding & 31)
    cosine = jnp.concatenate([cosine] * (nvec // LANES), axis=1)
    sine = jnp.concatenate([sine] * (nvec // LANES), axis=1)
    for color in range(colors):
        re = vec_ref[0, 0, color]
        im = vec_ref[0, 1, color]
        re32 = re.astype(jnp.float32)
        im32 = im.astype(jnp.float32)
        at = pl.ds(color * sites, sites)
        right_ref[at, :nvec] = (cosine * re32 + sine * im32).astype(jnp.bfloat16)
        right_ref[at, nvec:] = (cosine * im32 - sine * re32).astype(jnp.bfloat16)
        left_ref[at, :nvec] = re
        left_ref[at, nvec:] = im
    part = lax.dot_general(
        left_ref[...], right_ref[...], (((0,), (0,)), ((), ())), preferred_element_type=jnp.float32
    )

    @pl.when(step == 0)
    def _():
        acc_ref[...] = part

    @pl.when(step > 0)
    def _():
        acc_ref[...] += part

    @pl.when(step == pl.num_programs(0) - 1)
    def _():
        rows = nvec // 16
        for member, out_ref in enumerate((keep_ref, *send_refs)):
            target = space ^ MEMBER_BITS[member]
            for quad in range(4):
                owner = (target & 9) | (2 * quad)
                start = pl.multiple_of(owner * rows, 8)
                real = pl.ds(start, rows)
                imag = pl.ds(pl.multiple_of(start + nvec, 8), rows)
                at = pl.ds(quad * rows, rows)
                out_ref[at, :nvec] = (acc_ref[real, :nvec] + acc_ref[imag, nvec:]).astype(out_ref.dtype)
                out_ref[at, nvec:] = (acc_ref[real, nvec:] - acc_ref[imag, :nvec]).astype(out_ref.dtype)


def gram(eigvec, momenta, which, chunk=256):
    _, _, colors, sites, nvec = eigvec.shape
    depth = colors * chunk
    shape = (nvec // 4, 2 * nvec)
    kinds = [jnp.float32] + [jnp.bfloat16] * 3
    return pl.pallas_call(
        functools.partial(gram_kernel, which),
        grid_spec=pltpu.PrefetchScalarGridSpec(
            num_scalar_prefetch=1,
            grid=(sites // chunk,),
            in_specs=[pl.BlockSpec((1, 2, colors, chunk, nvec), lambda i, m: (0, 0, 0, i, 0))],
            out_specs=[pl.BlockSpec(shape, lambda i, m: (0, 0)) for _ in kinds],
            scratch_shapes=[
                pltpu.VMEM((depth, 2 * nvec), jnp.bfloat16),
                pltpu.VMEM((depth, 2 * nvec), jnp.bfloat16),
                pltpu.VMEM((2 * nvec, 2 * nvec), jnp.float32),
            ],
        ),
        out_shape=[jax.ShapeDtypeStruct(shape, kind) for kind in kinds],
        compiler_params=pltpu.CompilerParams(
            dimension_semantics=("arbitrary",), vmem_limit_bytes=62 << 20
        ),
        cost_estimate=pl.CostEstimate(
            flops=8 * nvec * nvec * colors * sites, bytes_accessed=eigvec.size * 2, transcendentals=0
        ),
    )(momenta, eigvec)


SPIN = 4


def exchange(parts):
    return lax.all_to_all(parts, "space", split_axis=0, concat_axis=0, tiled=True)


def swap(value, bits):
    return lax.ppermute(value, "space", [(i, i ^ bits) for i in range(16)])


def reduce_rows(parts):
    keep = parts[0]
    rows = keep.shape[0] // 4
    arrived = [swap(parts[m], MEMBER_BITS[m]) for m in (1, 2, 3)]
    for value in arrived:
        keep = keep + value.astype(jnp.float32)
    keep = keep.reshape(4, rows, keep.shape[1])
    quad = lax.axis_index("space") // 2 % 4
    parts = [lax.dynamic_index_in_dim(keep, quad ^ m, keepdims=False) for m in range(4)]
    sends = [part.astype(jnp.bfloat16) for part in parts[1:]]
    arrived = [swap(sends[m - 1], QUAD_BITS[m]) for m in (1, 2, 3)]
    out = parts[0]
    for value in arrived:
        out = out + value.astype(jnp.float32)
    return out.astype(jnp.bfloat16)


def steps(eigvec, momenta, peram):
    tau = peram[0]
    nrows, nvec = tau.shape[1], tau.shape[3]
    place = lax.axis_index("space")
    spins = jnp.broadcast_to(tau.transpose(2, 0, 1, 3).reshape(2, 1, 2, 2, nrows, nvec), (2, 4, 2, 2, nrows, nvec))
    tau = exchange(spins.reshape(16, 2, nrows, nvec))
    tau = tau.transpose(1, 0, 2, 3).reshape(2 * nvec, nvec)
    source = gram(eigvec, momenta, 1)
    sink = gram(eigvec, momenta, 0)
    share = reduce_rows(source)
    share = lax.ppermute(share, "tm", [(t, 15 - t) for t in range(16)])
    source = exchange(jnp.broadcast_to(share, (16, *share.shape)))
    rows = reduce_rows(sink)
    rows = jnp.stack([rows] + [swap(rows, MEMBER_BITS[m]) for m in (1, 2, 3)])
    rows_re, rows_im = rows[..., :nvec], rows[..., nvec:]
    left = jnp.concatenate(
        [jnp.concatenate([rows_re, -rows_im], axis=-1), jnp.concatenate([rows_im, rows_re], axis=-1)], axis=1
    ).reshape(8 * nrows, 2 * nvec)
    mixed = jnp.dot(left, tau, preferred_element_type=jnp.float32).astype(jnp.bfloat16)
    mixed = mixed.reshape(4, 2, nrows, nvec)
    mixed = jnp.stack([mixed[0]] + [swap(mixed[m], MEMBER_BITS[m]) for m in (1, 2, 3)])
    mixed = mixed.reshape(2, 2, 2, nrows, nvec)
    mixed = jnp.where(place % 2 == 1, mixed[:, ::-1], mixed)
    mixed = jnp.where(place // 8 == 1, mixed[::-1], mixed)
    mixed = mixed.transpose(3, 0, 1, 2, 4).reshape(nrows * SPIN, 2 * nvec)
    source = source.reshape(nvec, 2 * nvec)
    source_re, source_im = source[:, :nvec], source[:, nvec:]
    right = jnp.concatenate([source, jnp.concatenate([-source_im, source_re], axis=1)], axis=0)
    dressed = jnp.dot(mixed, right, preferred_element_type=jnp.float32)
    return dressed.reshape(1, nrows, SPIN, 2, nvec).astype(jnp.bfloat16)


def solution(mesh):
    return jax.shard_map(
        steps,
        mesh=mesh,
        in_specs=(P("tm", None, None, "space", None), P(), P("tm", None, "space", None, None)),
        out_specs=P("tm", "space", None, None, None),
        check_vma=False,
    )
```

time: 130 us -> 99.1 us (0.76)
  waiting for transfers between devices: 59 us -> 20.8 us
  starting transfers between devices: 43.7 us -> 52.2 us
  other arithmetic: 2.29 us -> 0.64 us
    all_to_all x4 -> x2, waiting for transfers between devices: 21.4 us -> 0.58 us  [exchange(): lax.all_to_all(parts, 'space', split_axis=0, concat_axis=0, tiled=True)]
    ppermute x5 -> x18, starting transfers between devices: 13 us -> 33.3 us  [swap(): return lax.ppermute(value, 'space', [(i, i ^ bits) for i in range(16)])]
    ppermute x5 -> x18, waiting for transfers between devices: 33.5 us -> 19.8 us  [swap(): return lax.ppermute(value, 'space', [(i, i ^ bits) for i in range(16)])]
    all_to_all x4 -> x2, starting transfers between devices: 30.6 us -> 18.8 us  [exchange(): lax.all_to_all(parts, 'space', split_axis=0, concat_axis=0, tiled=True)]
    ppermute x1, waiting for transfers between devices: 4.16 us -> 0.45 us  [steps(): share = lax.ppermute(share, 'tm', [(t, 15 - t) for t in range(16)])]
    convert_element_type x1 -> x2, other arithmetic: 1.84 us -> 0.04 us  [reduce_rows(): return out.astype(jnp.bfloat16)]
  transfers between devices with their start and end apart: 10 -> 21, of which waited for: 9 -> 7; matrix products, arithmetic and copies ran while one was open for 1% -> 2% of each run, Pallas kernels for 8% -> 10%
where the time goes in v2:
time: 99.1 us; the launch traced here: 98.3 us
  starting transfers between devices  52.2 us (53%)
  waiting for transfers between devices  20.8 us (21%)
  Pallas kernels  20.1 us (20%)
  local copies, waits for them, and re-layouts  3.54 us (4%)
    ppermute x18, starting transfers between devices, swap(): return lax.ppermute(value, 'space', [(i, i ^ bits) for i in range(16)])  33.3 us
    pallas_call x2, Pallas kernels, gram(): pl.pallas_call(functools.partial(gram_kernel, which), grid_spec=pltpu.Pre...  20.1 us
    ppermute x18, waiting for transfers between devices, swap(): return lax.ppermute(value, 'space', [(i, i ^ bits) for i in range(16)])  19.8 us
    all_to_all x2, starting transfers between devices, exchange(): lax.all_to_all(parts, 'space', split_axis=0, concat_axis=0, tiled=True)  18.8 us
  transfers between devices with their start and end apart: 21, of which 7 were waited for; matrix products, arithmetic and copies ran while one was open for 2% of the time, Pallas kernels for 10%

profile of v2, /device:TPU:8, one launch (start us, length us, event | category | flops | bytes accessed | tf_op | source)
XLA Modules:
  0.0 98.3 jit_solution(15531480190731208110)
XLA Ops:
  0.0 0.0 copy-start.2
  0.0 10.1 %shard_map.37 = (f32[96,768]{1,0:T(8,128)}, bf16[96,768]{1,0:T(8,128)(2,1)}, bf16[96,768]{1,0:T(8,128)(2,1)}, bf16[96,768]{1,0:T(8,128)(2,1)}) custom-call(s32[2,3]{1,0:T(2,128)} %momenta.3, bf16[1,2,3,1024,384]{4,3,2,1,0:T(8,128)(2,1)} %vec_ref.3), custom_call_target="tpu_custom_call" | custom-call | flops 3623878656 | bytes 4718592 | tf_op jit(solution)/shard_map/pallas_call | solution.py:82
  10.1 1.9 %collective-permute-start = (bf16[96,768]{1,0:T(8,128)(2,1)}, bf16[96,768]{1,0:T(8,128)(2,1)S(1)}, u32[]{:S(2)}, u32[]{:S(2)}) collective-permute-start(bf16[96,768]{1,0:T(8,128)(2,1)} %get-tuple-element.14), channel_id=1, source_target_pairs={{0,1},{1,0},{2,3},{3,2},{4,5},{5,4},{6,7},{7,6},{8,9},{9,8},{10,11... | collective-permute-start | bytes 442376 | tf_op jit(solution)/shard_map/ppermute | solution.py:113
  12.0 3.0 %collective-permute-start.1 = (bf16[96,768]{1,0:T(8,128)(2,1)}, bf16[96,768]{1,0:T(8,128)(2,1)S(1)}, u32[]{:S(2)}, u32[]{:S(2)}) collective-permute-start(bf16[96,768]{1,0:T(8,128)(2,1)} %get-tuple-element.15), channel_id=1, source_target_pairs={{0,8},{1,9},{2,10},{3,11},{4,12},{5,13},{6,14},{7,15},{8,0},{9,1},... | collective-permute-start | bytes 442376 | tf_op jit(solution)/shard_map/ppermute | solution.py:113
  15.0 0.0 collective-permute-start.2
  15.1 0.0 copy-done.2
  15.1 0.9 broadcast_in_dim.11
  16.0 11.0 %all-to-all-start = ((bf16[16,2,24,384]{3,2,1,0:T(8,128)(2,1)}), bf16[16,2,24,384]{3,2,1,0:T(8,128)(2,1)S(1)}, u32[]{:S(2)}, u32[]{:S(2)}) async-start(bf16[16,2,24,384]{3,2,1,0:T(8,128)(2,1)} %bitcast.13), calls=%async_computation | async-start | bytes 1179648 | tf_op jit(solution)/shard_map/all_to_all | solution.py:109
  27.0 0.0 copy-start.1
  27.0 10.0 %shard_map.38 = (f32[96,768]{1,0:T(8,128)}, bf16[96,768]{1,0:T(8,128)(2,1)}, bf16[96,768]{1,0:T(8,128)(2,1)}, bf16[96,768]{1,0:T(8,128)(2,1)}) custom-call(s32[2,3]{1,0:T(2,128)} %momenta.3, bf16[1,2,3,1024,384]{4,3,2,1,0:T(8,128)(2,1)} %vec_ref.3), custom_call_target="tpu_custom_call" | custom-call | flops 3623878656 | bytes 4718592 | tf_op jit(solution)/shard_map/pallas_call | solution.py:82
  37.0 1.9 %collective-permute-start.12 = (bf16[96,768]{1,0:T(8,128)(2,1)}, bf16[96,768]{1,0:T(8,128)(2,1)S(1)}, u32[]{:S(2)}, u32[]{:S(2)}) collective-permute-start(bf16[96,768]{1,0:T(8,128)(2,1)} %get-tuple-element.18), channel_id=1, source_target_pairs={{0,1},{1,0},{2,3},{3,2},{4,5},{5,4},{6,7},{7,6},{8,9},{9,8},{10,11... | collective-permute-start | bytes 442376 | tf_op jit(solution)/shard_map/ppermute | solution.py:113
  39.0 3.0 %collective-permute-start.13 = (bf16[96,768]{1,0:T(8,128)(2,1)}, bf16[96,768]{1,0:T(8,128)(2,1)S(1)}, u32[]{:S(2)}, u32[]{:S(2)}) collective-permute-start(bf16[96,768]{1,0:T(8,128)(2,1)} %get-tuple-element.19), channel_id=1, source_target_pairs={{0,8},{1,9},{2,10},{3,11},{4,12},{5,13},{6,14},{7,15},{8,0},{9,1},... | collective-permute-start | bytes 442376 | tf_op jit(solution)/shard_map/ppermute | solution.py:113
  41.9 0.0 collective-permute-done
  41.9 0.1 collective-permute-start.14
  42.0 0.0 collective-permute-done.1
  42.0 0.0 collective-permute-done.2
  42.0 0.0 copy-done.1
  42.0 0.1 convert_add_fusion.1
  42.1 2.9 %collective-permute-start.3 = (bf16[24,768]{1,0:T(8,128)(2,1)S(1)}, bf16[24,768]{1,0:T(8,128)(2,1)S(1)}, u32[]{:S(2)}, u32[]{:S(2)}) collective-permute-start(bf16[24,768]{1,0:T(8,128)(2,1)S(1)} %get-tuple-element.23), channel_id=1, source_target_pairs={{0,2},{1,3},{2,0},{3,1},{4,6},{5,7},{6,4},{7,5},{8,10},{9,11},{10,... | collective-permute-start | bytes 110600 | tf_op jit(solution)/shard_map/ppermute | solution.py:113
  45.1 3.6 %collective-permute-start.4 = (bf16[24,768]{1,0:T(8,128)(2,1)S(1)}, bf16[24,768]{1,0:T(8,128)(2,1)S(1)}, u32[]{:S(2)}, u32[]{:S(2)}) collective-permute-start(bf16[24,768]{1,0:T(8,128)(2,1)S(1)} %get-tuple-element.25), channel_id=1, source_target_pairs={{0,4},{1,5},{2,6},{3,7},{4,0},{5,1},{6,2},{7,3},{8,12},{9,13},{10,... | collective-permute-start | bytes 110600 | tf_op jit(solution)/shard_map/ppermute | solution.py:113
  48.6 0.0 collective-permute-done.12
  48.6 0.1 collective-permute-start.5
  48.7 0.0 collective-permute-done.13
  48.7 2.4 %collective-permute-done.14 = bf16[96,768]{1,0:T(8,128)(2,1)S(1)} collective-permute-done((bf16[96,768]{1,0:T(8,128)(2,1)}, bf16[96,768]{1,0:T(8,128)(2,1)S(1)}, u32[]{:S(2)}, u32[]{:S(2)}) %collective-permute-start.14) | collective-permute-done | bytes 147488 | tf_op jit(solution)/shard_map/ppermute | solution.py:113
  51.1 0.0 copy-done
  51.1 0.1 convert_add_fusion
  51.2 2.0 %collective-permute-start.15 = (bf16[24,768]{1,0:T(8,128)(2,1)S(1)}, bf16[24,768]{1,0:T(8,128)(2,1)S(1)}, u32[]{:S(2)}, u32[]{:S(2)}) collective-permute-start(bf16[24,768]{1,0:T(8,128)(2,1)S(1)} %get-tuple-element.26), channel_id=1, source_target_pairs={{0,2},{1,3},{2,0},{3,1},{4,6},{5,7},{6,4},{7,5},{8,10},{9,11},{10,... | collective-permute-start | bytes 110600 | tf_op jit(solution)/shard_map/ppermute | solution.py:113
  53.2 3.3 %collective-permute-start.16 = (bf16[24,768]{1,0:T(8,128)(2,1)S(1)}, bf16[24,768]{1,0:T(8,128)(2,1)S(1)}, u32[]{:S(2)}, u32[]{:S(2)}) collective-permute-start(bf16[24,768]{1,0:T(8,128)(2,1)S(1)} %get-tuple-element.28), channel_id=1, source_target_pairs={{0,4},{1,5},{2,6},{3,7},{4,0},{5,1},{6,2},{7,3},{8,12},{9,13},{10,... | collective-permute-start | bytes 110600 | tf_op jit(solution)/shard_map/ppermute | solution.py:113
  56.5 0.0 collective-permute-done.3
  56.5 1.3 %collective-permute-start.17 = (bf16[24,768]{1,0:T(8,128)(2,1)S(1)}, bf16[24,768]{1,0:T(8,128)(2,1)S(1)}, u32[]{:S(2)}, u32[]{:S(2)}) collective-permute-start(bf16[24,768]{1,0:T(8,128)(2,1)S(1)} %get-tuple-element.27), channel_id=1, source_target_pairs={{0,6},{1,7},{2,4},{3,5},{4,2},{5,3},{6,0},{7,1},{8,14},{9,15},{10,... | collective-permute-start | bytes 110600 | tf_op jit(solution)/shard_map/ppermute | solution.py:113
  57.8 0.0 collective-permute-done.4
  57.8 0.0 collective-permute-done.5
  57.8 0.6 collective-permute-start.6
  58.5 2.0 %collective-permute-start.7 = (bf16[24,768]{1,0:T(8,128)(2,1)S(1)}, bf16[24,768]{1,0:T(8,128)(2,1)S(1)}, u32[]{:S(2)}, u32[]{:S(2)}) collective-permute-start(bf16[24,768]{1,0:T(8,128)(2,1)S(1)} %fusion.8), channel_id=1, source_target_pairs={{0,8},{1,9},{2,10},{3,11},{4,12},{5,13},{6,14},{7,15},{8,0},{9,1},... | collective-permute-start | bytes 110600 | tf_op jit(solution)/shard_map/ppermute | solution.py:113
  60.4 0.0 collective-permute-done.15
  60.4 2.5 %collective-permute-start.8 = (bf16[24,768]{1,0:T(8,128)(2,1)S(1)}, bf16[24,768]{1,0:T(8,128)(2,1)S(1)}, u32[]{:S(2)}, u32[]{:S(2)}) collective-permute-start(bf16[24,768]{1,0:T(8,128)(2,1)S(1)} %fusion.8), channel_id=1, source_target_pairs={{0,9},{1,8},{2,11},{3,10},{4,13},{5,12},{6,15},{7,14},{8,1},{9,0},... | collective-permute-start | bytes 110600 | tf_op jit(solution)/shard_map/ppermute | solution.py:113
  62.9 0.0 collective-permute-done.16
  62.9 0.0 collective-permute-done.17
  63.0 0.1 collective-permute-start.18
  63.1 0.0 collective-permute-done.6
  63.1 0.9 collective-permute-done.7
  63.9 2.9 %collective-permute-done.8 = bf16[24,768]{1,0:T(8,128)(2,1)S(1)} collective-permute-done((bf16[24,768]{1,0:T(8,128)(2,1)S(1)}, bf16[24,768]{1,0:T(8,128)(2,1)S(1)}, u32[]{:S(2)}, u32[]{:S(2)}) %collective-permute-start.8) | collective-permute-done | bytes 36896 | tf_op jit(solution)/shard_map/ppermute | solution.py:113
  66.9 0.4 collective-permute-done.18
  67.3 0.0 all-to-all-done
  67.3 0.9 broadcast_in_dim.12
  68.2 7.8 %all-to-all-start.1 = ((bf16[16,24,768]{2,1,0:T(8,128)(2,1)}), bf16[16,24,768]{2,1,0:T(8,128)(2,1)S(1)}, u32[]{:S(2)}, u32[]{:S(2)}) async-start(bf16[16,24,768]{2,1,0:T(8,128)(2,1)} %broadcast_in_dim.12), calls=%async_computation.1 | async-start | bytes 1179648 | tf_op jit(solution)/shard_map/all_to_all | solution.py:109
  76.0 0.1 copy.15
  76.1 0.3 convolution_convert_fusion
  76.4 2.0 %collective-permute-start.9 = (bf16[2,24,384]{2,1,0:T(8,128)(2,1)S(1)}, bf16[2,24,384]{2,1,0:T(8,128)(2,1)S(1)}, u32[]{:S(2)}, u32[]{:S(2)}) collective-permute-start(bf16[2,24,384]{2,1,0:T(8,128)(2,1)S(1)} %bitcast.87), channel_id=1, source_target_pairs={{0,1},{1,0},{2,3},{3,2},{4,5},{5,4},{6,7},{7,6},{8,9},{9,8},{10,11... | collective-permute-start | bytes 110600 | tf_op jit(solution)/shard_map/ppermute | solution.py:113
  78.4 3.0 %collective-permute-start.10 = (bf16[2,24,384]{2,1,0:T(8,128)(2,1)S(1)}, bf16[2,24,384]{2,1,0:T(8,128)(2,1)S(1)}, u32[]{:S(2)}, u32[]{:S(2)}) collective-permute-start(bf16[2,24,384]{2,1,0:T(8,128)(2,1)S(1)} %bitcast.85), channel_id=1, source_target_pairs={{0,8},{1,9},{2,10},{3,11},{4,12},{5,13},{6,14},{7,15},{8,0},{9,1},... | collective-permute-start | bytes 110600 | tf_op jit(solution)/shard_map/ppermute | solution.py:113
  81.4 0.1 collective-permute-start.11
  81.5 10.8 %collective-permute-done.9 = bf16[2,24,384]{2,1,0:T(8,128)(2,1)S(1)} collective-permute-done((bf16[2,24,384]{2,1,0:T(8,128)(2,1)S(1)}, bf16[2,24,384]{2,1,0:T(8,128)(2,1)S(1)}, u32[]{:S(2)}, u32[]{:S(2)}) %collective-permute-start.9) | collective-permute-done | bytes 36896 | tf_op jit(solution)/shard_map/ppermute | solution.py:113
  92.3 0.0 collective-permute-done.10
  92.3 2.8 %collective-permute-done.11 = bf16[2,24,384]{2,1,0:T(8,128)(2,1)S(1)} collective-permute-done((bf16[2,24,384]{2,1,0:T(8,128)(2,1)S(1)}, bf16[2,24,384]{2,1,0:T(8,128)(2,1)S(1)}, u32[]{:S(2)}, u32[]{:S(2)}) %collective-permute-start.11) | collective-permute-done | bytes 36896 | tf_op jit(solution)/shard_map/ppermute | solution.py:113
  95.2 0.1 copy.16
  95.3 0.1 broadcast_select_fusion
  95.4 0.1 fusion.1
  95.5 0.1 reshape.51
  95.6 0.6 all-to-all-done.1
  96.2 0.1 slice_negate_fusion
  96.3 0.1 maximum_bitcast_fusion
  96.4 0.6 copy.18
  97.0 0.5 fusion
  97.5 0.8 copy.19
  (11 shorter events, 0.2 us)
Async XLA Ops:
  0.0 15.1 %copy-start.2 = (bf16[1,2,24,4,384]{4,3,2,1,0:T(4,128)(2,1)S(1)}, bf16[1,2,24,4,384]{4,3,2,1,0:T(4,128)(2,1)}, u32[]{:S(2)}) copy-start(bf16[1,2,24,4,384]{4,3,2,1,0:T(4,128)(2,1)} %param.5) | copy-start | bytes 442372
  10.1 31.9 %collective-permute-start = (bf16[96,768]{1,0:T(8,128)(2,1)}, bf16[96,768]{1,0:T(8,128)(2,1)S(1)}, u32[]{:S(2)}, u32[]{:S(2)}) collective-permute-start(bf16[96,768]{1,0:T(8,128)(2,1)} %get-tuple-element.14), channel_id=1, source_target_pairs={{0,1},{1,0},{2,3},{3,2},{4,5},{5,4},{6,7},{7,6},{8,9},{9,8},{10,11... | collective-permute-start | bytes 442376 | tf_op jit(solution)/shard_map/ppermute | solution.py:113
  12.0 30.0 %collective-permute-start.1 = (bf16[96,768]{1,0:T(8,128)(2,1)}, bf16[96,768]{1,0:T(8,128)(2,1)S(1)}, u32[]{:S(2)}, u32[]{:S(2)}) collective-permute-start(bf16[96,768]{1,0:T(8,128)(2,1)} %get-tuple-element.15), channel_id=1, source_target_pairs={{0,8},{1,9},{2,10},{3,11},{4,12},{5,13},{6,14},{7,15},{8,0},{9,1},... | collective-permute-start | bytes 442376 | tf_op jit(solution)/shard_map/ppermute | solution.py:113
  15.0 27.0 %collective-permute-start.2 = (bf16[96,768]{1,0:T(8,128)(2,1)}, bf16[96,768]{1,0:T(8,128)(2,1)S(1)}, u32[]{:S(2)}, u32[]{:S(2)}) collective-permute-start(bf16[96,768]{1,0:T(8,128)(2,1)} %get-tuple-element.16), channel_id=1, source_target_pairs={{0,9},{1,8},{2,11},{3,10},{4,13},{5,12},{6,15},{7,14},{8,1},{9,0},... | collective-permute-start | bytes 442376 | tf_op jit(solution)/shard_map/ppermute | solution.py:113
  16.0 51.4 %all-to-all-start = ((bf16[16,2,24,384]{3,2,1,0:T(8,128)(2,1)}), bf16[16,2,24,384]{3,2,1,0:T(8,128)(2,1)S(1)}, u32[]{:S(2)}, u32[]{:S(2)}) async-start(bf16[16,2,24,384]{3,2,1,0:T(8,128)(2,1)} %bitcast.13), calls=%async_computation | async-start | bytes 1179648 | tf_op jit(solution)/shard_map/all_to_all | solution.py:109
  27.0 15.0 %copy-start.1 = (f32[96,768]{1,0:T(8,128)S(1)}, f32[96,768]{1,0:T(8,128)}, u32[]{:S(2)}) copy-start(f32[96,768]{1,0:T(8,128)} %get-tuple-element.13) | copy-start | bytes 884740
  37.0 14.1 %copy-start = (f32[96,768]{1,0:T(8,128)S(1)}, f32[96,768]{1,0:T(8,128)}, u32[]{:S(2)}) copy-start(f32[96,768]{1,0:T(8,128)} %get-tuple-element.17) | copy-start | bytes 884740
  37.0 11.6 %collective-permute-start.12 = (bf16[96,768]{1,0:T(8,128)(2,1)}, bf16[96,768]{1,0:T(8,128)(2,1)S(1)}, u32[]{:S(2)}, u32[]{:S(2)}) collective-permute-start(bf16[96,768]{1,0:T(8,128)(2,1)} %get-tuple-element.18), channel_id=1, source_target_pairs={{0,1},{1,0},{2,3},{3,2},{4,5},{5,4},{6,7},{7,6},{8,9},{9,8},{10,11... | collective-permute-start | bytes 442376 | tf_op jit(solution)/shard_map/ppermute | solution.py:113
  39.0 9.8 %collective-permute-start.13 = (bf16[96,768]{1,0:T(8,128)(2,1)}, bf16[96,768]{1,0:T(8,128)(2,1)S(1)}, u32[]{:S(2)}, u32[]{:S(2)}) collective-permute-start(bf16[96,768]{1,0:T(8,128)(2,1)} %get-tuple-element.19), channel_id=1, source_target_pairs={{0,8},{1,9},{2,10},{3,11},{4,12},{5,13},{6,14},{7,15},{8,0},{9,1},... | collective-permute-start | bytes 442376 | tf_op jit(solution)/shard_map/ppermute | solution.py:113
  41.9 9.2 %collective-permute-start.14 = (bf16[96,768]{1,0:T(8,128)(2,1)}, bf16[96,768]{1,0:T(8,128)(2,1)S(1)}, u32[]{:S(2)}, u32[]{:S(2)}) collective-permute-start(bf16[96,768]{1,0:T(8,128)(2,1)} %get-tuple-element.20), channel_id=1, source_target_pairs={{0,9},{1,8},{2,11},{3,10},{4,13},{5,12},{6,15},{7,14},{8,1},{9,0},... | collective-permute-start | bytes 442376 | tf_op jit(solution)/shard_map/ppermute | solution.py:113
  42.1 14.4 %collective-permute-start.3 = (bf16[24,768]{1,0:T(8,128)(2,1)S(1)}, bf16[24,768]{1,0:T(8,128)(2,1)S(1)}, u32[]{:S(2)}, u32[]{:S(2)}) collective-permute-start(bf16[24,768]{1,0:T(8,128)(2,1)S(1)} %get-tuple-element.23), channel_id=1, source_target_pairs={{0,2},{1,3},{2,0},{3,1},{4,6},{5,7},{6,4},{7,5},{8,10},{9,11},{10,... | collective-permute-start | bytes 110600 | tf_op jit(solution)/shard_map/ppermute | solution.py:113
  45.1 12.7 %collective-permute-start.4 = (bf16[24,768]{1,0:T(8,128)(2,1)S(1)}, bf16[24,768]{1,0:T(8,128)(2,1)S(1)}, u32[]{:S(2)}, u32[]{:S(2)}) collective-permute-start(bf16[24,768]{1,0:T(8,128)(2,1)S(1)} %get-tuple-element.25), channel_id=1, source_target_pairs={{0,4},{1,5},{2,6},{3,7},{4,0},{5,1},{6,2},{7,3},{8,12},{9,13},{10,... | collective-permute-start | bytes 110600 | tf_op jit(solution)/shard_map/ppermute | solution.py:113
  48.6 9.2 %collective-permute-start.5 = (bf16[24,768]{1,0:T(8,128)(2,1)S(1)}, bf16[24,768]{1,0:T(8,128)(2,1)S(1)}, u32[]{:S(2)}, u32[]{:S(2)}) collective-permute-start(bf16[24,768]{1,0:T(8,128)(2,1)S(1)} %get-tuple-element.24), channel_id=1, source_target_pairs={{0,6},{1,7},{2,4},{3,5},{4,2},{5,3},{6,0},{7,1},{8,14},{9,15},{10,... | collective-permute-start | bytes 110600 | tf_op jit(solution)/shard_map/ppermute | solution.py:113
  51.2 9.2 %collective-permute-start.15 = (bf16[24,768]{1,0:T(8,128)(2,1)S(1)}, bf16[24,768]{1,0:T(8,128)(2,1)S(1)}, u32[]{:S(2)}, u32[]{:S(2)}) collective-permute-start(bf16[24,768]{1,0:T(8,128)(2,1)S(1)} %get-tuple-element.26), channel_id=1, source_target_pairs={{0,2},{1,3},{2,0},{3,1},{4,6},{5,7},{6,4},{7,5},{8,10},{9,11},{10,... | collective-permute-start | bytes 110600 | tf_op jit(solution)/shard_map/ppermute | solution.py:113
  53.2 9.7 %collective-permute-start.16 = (bf16[24,768]{1,0:T(8,128)(2,1)S(1)}, bf16[24,768]{1,0:T(8,128)(2,1)S(1)}, u32[]{:S(2)}, u32[]{:S(2)}) collective-permute-start(bf16[24,768]{1,0:T(8,128)(2,1)S(1)} %get-tuple-element.28), channel_id=1, source_target_pairs={{0,4},{1,5},{2,6},{3,7},{4,0},{5,1},{6,2},{7,3},{8,12},{9,13},{10,... | collective-permute-start | bytes 110600 | tf_op jit(solution)/shard_map/ppermute | solution.py:113
  56.5 6.4 %collective-permute-start.17 = (bf16[24,768]{1,0:T(8,128)(2,1)S(1)}, bf16[24,768]{1,0:T(8,128)(2,1)S(1)}, u32[]{:S(2)}, u32[]{:S(2)}) collective-permute-start(bf16[24,768]{1,0:T(8,128)(2,1)S(1)} %get-tuple-element.27), channel_id=1, source_target_pairs={{0,6},{1,7},{2,4},{3,5},{4,2},{5,3},{6,0},{7,1},{8,14},{9,15},{10,... | collective-permute-start | bytes 110600 | tf_op jit(solution)/shard_map/ppermute | solution.py:113
  57.8 5.2 %collective-permute-start.6 = (bf16[24,768]{1,0:T(8,128)(2,1)S(1)}, bf16[24,768]{1,0:T(8,128)(2,1)S(1)}, u32[]{:S(2)}, u32[]{:S(2)}) collective-permute-start(bf16[24,768]{1,0:T(8,128)(2,1)S(1)} %fusion.8), channel_id=1, source_target_pairs={{0,1},{1,0},{2,3},{3,2},{4,5},{5,4},{6,7},{7,6},{8,9},{9,8},{10,11... | collective-permute-start | bytes 110600 | tf_op jit(solution)/shard_map/ppermute | solution.py:113
  58.5 5.5 %collective-permute-start.7 = (bf16[24,768]{1,0:T(8,128)(2,1)S(1)}, bf16[24,768]{1,0:T(8,128)(2,1)S(1)}, u32[]{:S(2)}, u32[]{:S(2)}) collective-permute-start(bf16[24,768]{1,0:T(8,128)(2,1)S(1)} %fusion.8), channel_id=1, source_target_pairs={{0,8},{1,9},{2,10},{3,11},{4,12},{5,13},{6,14},{7,15},{8,0},{9,1},... | collective-permute-start | bytes 110600 | tf_op jit(solution)/shard_map/ppermute | solution.py:113
  60.4 6.4 %collective-permute-start.8 = (bf16[24,768]{1,0:T(8,128)(2,1)S(1)}, bf16[24,768]{1,0:T(8,128)(2,1)S(1)}, u32[]{:S(2)}, u32[]{:S(2)}) collective-permute-start(bf16[24,768]{1,0:T(8,128)(2,1)S(1)} %fusion.8), channel_id=1, source_target_pairs={{0,9},{1,8},{2,11},{3,10},{4,13},{5,12},{6,15},{7,14},{8,1},{9,0},... | collective-permute-start | bytes 110600 | tf_op jit(solution)/shard_map/ppermute | solution.py:113
  63.0 4.4 %collective-permute-start.18 = (bf16[24,768]{1,0:T(8,128)(2,1)S(1)}, bf16[24,768]{1,0:T(8,128)(2,1)S(1)}, u32[]{:S(2)}, u32[]{:S(2)}) collective-permute-start(bf16[24,768]{1,0:T(8,128)(2,1)S(1)} %fusion.5), channel_id=1, source_target_pairs={{0,240},{16,224},{32,208},{48,192},{64,176},{80,160},{96,144},{112... | collective-permute-start | bytes 110600 | tf_op jit(solution)/shard_map/ppermute | solution.py:143
  68.2 28.0 %all-to-all-start.1 = ((bf16[16,24,768]{2,1,0:T(8,128)(2,1)}), bf16[16,24,768]{2,1,0:T(8,128)(2,1)S(1)}, u32[]{:S(2)}, u32[]{:S(2)}) async-start(bf16[16,24,768]{2,1,0:T(8,128)(2,1)} %broadcast_in_dim.12), calls=%async_computation.1 | async-start | bytes 1179648 | tf_op jit(solution)/shard_map/all_to_all | solution.py:109
  76.4 15.9 %collective-permute-start.9 = (bf16[2,24,384]{2,1,0:T(8,128)(2,1)S(1)}, bf16[2,24,384]{2,1,0:T(8,128)(2,1)S(1)}, u32[]{:S(2)}, u32[]{:S(2)}) collective-permute-start(bf16[2,24,384]{2,1,0:T(8,128)(2,1)S(1)} %bitcast.87), channel_id=1, source_target_pairs={{0,1},{1,0},{2,3},{3,2},{4,5},{5,4},{6,7},{7,6},{8,9},{9,8},{10,11... | collective-permute-start | bytes 110600 | tf_op jit(solution)/shard_map/ppermute | solution.py:113
  78.4 13.9 %collective-permute-start.10 = (bf16[2,24,384]{2,1,0:T(8,128)(2,1)S(1)}, bf16[2,24,384]{2,1,0:T(8,128)(2,1)S(1)}, u32[]{:S(2)}, u32[]{:S(2)}) collective-permute-start(bf16[2,24,384]{2,1,0:T(8,128)(2,1)S(1)} %bitcast.85), channel_id=1, source_target_pairs={{0,8},{1,9},{2,10},{3,11},{4,12},{5,13},{6,14},{7,15},{8,0},{9,1},... | collective-permute-start | bytes 110600 | tf_op jit(solution)/shard_map/ppermute | solution.py:113
  81.4 13.7 %collective-permute-start.11 = (bf16[2,24,384]{2,1,0:T(8,128)(2,1)S(1)}, bf16[2,24,384]{2,1,0:T(8,128)(2,1)S(1)}, u32[]{:S(2)}, u32[]{:S(2)}) collective-permute-start(bf16[2,24,384]{2,1,0:T(8,128)(2,1)S(1)} %bitcast.83), channel_id=1, source_target_pairs={{0,9},{1,8},{2,11},{3,10},{4,13},{5,12},{6,15},{7,14},{8,1},{9,0},... | collective-permute-start | bytes 110600 | tf_op jit(solution)/shard_map/ppermute | solution.py:113

commit v3 on v2

--- a/solution.py
+++ b/solution.py
@@ -9,6 +9,7 @@
 LANES = 128
 MEMBER_BITS = (0, 1, 8, 9)
 QUAD_BITS = (0, 2, 4, 6)
+QUAD_GROUPS = [[8 * h + 2 * q + lo for q in range(4)] for h in (0, 1) for lo in (0, 1)]
 
 
 def phase_of(winding):
@@ -105,57 +106,75 @@
 SPIN = 4
 
 
-def exchange(parts):
-    return lax.all_to_all(parts, "space", split_axis=0, concat_axis=0, tiled=True)
-
-
 def swap(value, bits):
     return lax.ppermute(value, "space", [(i, i ^ bits) for i in range(16)])
 
 
-def reduce_rows(parts):
-    keep = parts[0]
-    rows = keep.shape[0] // 4
-    arrived = [swap(parts[m], MEMBER_BITS[m]) for m in (1, 2, 3)]
-    for value in arrived:
-        keep = keep + value.astype(jnp.float32)
-    keep = keep.reshape(4, rows, keep.shape[1])
-    quad = lax.axis_index("space") // 2 % 4
-    parts = [lax.dynamic_index_in_dim(keep, quad ^ m, keepdims=False) for m in range(4)]
-    sends = [part.astype(jnp.bfloat16) for part in parts[1:]]
-    arrived = [swap(sends[m - 1], QUAD_BITS[m]) for m in (1, 2, 3)]
+def around(parts, bits):
+    return [parts[0]] + [swap(parts[m], bits[m]) for m in (1, 2, 3)]
+
+
+def wide_sum(parts):
     out = parts[0]
-    for value in arrived:
+    for value in parts[1:]:
         out = out + value.astype(jnp.float32)
-    return out.astype(jnp.bfloat16)
+    return out
+
+
+def in_place(parts, here):
+    parts = jnp.stack(parts)
+    return jnp.stack([lax.dynamic_index_in_dim(parts, m ^ here, keepdims=False) for m in range(4)])
+
+
+def spread(total, here):
+    rows = total.shape[0] // 4
+    total = total.reshape(4, rows, total.shape[1])
+    parts = [lax.dynamic_index_in_dim(total, here ^ m, keepdims=False) for m in range(4)]
+    return parts[:1] + [part.astype(jnp.bfloat16) for part in parts[1:]]
 
 
 def steps(eigvec, momenta, peram):
     tau = peram[0]
     nrows, nvec = tau.shape[1], tau.shape[3]
     place = lax.axis_index("space")
-    spins = jnp.broadcast_to(tau.transpose(2, 0, 1, 3).reshape(2, 1, 2, 2, nrows, nvec), (2, 4, 2, 2, nrows, nvec))
-    tau = exchange(spins.reshape(16, 2, nrows, nvec))
-    tau = tau.transpose(1, 0, 2, 3).reshape(2 * nvec, nvec)
+    quad = place // 2 % 4
+    member = place // 8 * 2 + place % 2
+    tau = tau.transpose(2, 1, 0, 3).reshape(SPIN, nrows, 2 * nvec)
+    spins = [lax.dynamic_index_in_dim(tau, member ^ m, keepdims=False) for m in range(4)]
     source = gram(eigvec, momenta, 1)
     sink = gram(eigvec, momenta, 0)
-    share = reduce_rows(source)
-    share = lax.ppermute(share, "tm", [(t, 15 - t) for t in range(16)])
-    source = exchange(jnp.broadcast_to(share, (16, *share.shape)))
-    rows = reduce_rows(sink)
-    rows = jnp.stack([rows] + [swap(rows, MEMBER_BITS[m]) for m in (1, 2, 3)])
+    first = around([source[0]] + [jnp.concatenate([source[m], spins[m]]) for m in (1, 2, 3)], MEMBER_BITS)
+    source = wide_sum([first[0]] + [part[: 4 * nrows] for part in first[1:]])
+    spins = in_place([spins[0]] + [part[4 * nrows :] for part in first[1:]], member)
+    spins = lax.all_to_all(
+        jnp.broadcast_to(spins, (4, *spins.shape)),
+        "space",
+        split_axis=0,
+        concat_axis=0,
+        tiled=True,
+        axis_index_groups=QUAD_GROUPS,
+    )
+    tau = spins.reshape(4, 2, 2, nrows, 2, nvec).transpose(4, 1, 0, 2, 3, 5).reshape(2 * nvec, nvec)
+    sink = wide_sum(around(sink, MEMBER_BITS))
+    source = wide_sum(around(spread(source, quad), QUAD_BITS)).astype(jnp.bfloat16)
+    share = lax.ppermute(source, "tm", [(t, 15 - t) for t in range(16)])
+    sink = spread(sink, quad)
+    second = around([share] + [jnp.concatenate([share, sink[m]]) for m in (1, 2, 3)], QUAD_BITS)
+    rows = wide_sum([sink[0]] + [part[nrows:] for part in second[1:]]).astype(jnp.bfloat16)
+    share = in_place([second[0]] + [part[:nrows] for part in second[1:]], quad)
+    third = jnp.concatenate([share.reshape(4 * nrows, 2 * nvec), rows])
+    third = around([third] * 4, MEMBER_BITS)
+    rows = jnp.stack([part[4 * nrows :] for part in third])
+    source = in_place([part[: 4 * nrows] for part in third], member)
+    source = source.reshape(2, 2, 4, nrows, 2 * nvec).transpose(0, 2, 1, 3, 4).reshape(nvec, 2 * nvec)
     rows_re, rows_im = rows[..., :nvec], rows[..., nvec:]
     left = jnp.concatenate(
         [jnp.concatenate([rows_re, -rows_im], axis=-1), jnp.concatenate([rows_im, rows_re], axis=-1)], axis=1
     ).reshape(8 * nrows, 2 * nvec)
     mixed = jnp.dot(left, tau, preferred_element_type=jnp.float32).astype(jnp.bfloat16)
     mixed = mixed.reshape(4, 2, nrows, nvec)
-    mixed = jnp.stack([mixed[0]] + [swap(mixed[m], MEMBER_BITS[m]) for m in (1, 2, 3)])
-    mixed = mixed.reshape(2, 2, 2, nrows, nvec)
-    mixed = jnp.where(place % 2 == 1, mixed[:, ::-1], mixed)
-    mixed = jnp.where(place // 8 == 1, mixed[::-1], mixed)
-    mixed = mixed.transpose(3, 0, 1, 2, 4).reshape(nrows * SPIN, 2 * nvec)
-    source = source.reshape(nvec, 2 * nvec)
+    mixed = in_place(around([mixed[m] for m in range(4)], MEMBER_BITS), member)
+    mixed = mixed.transpose(2, 0, 1, 3).reshape(nrows * SPIN, 2 * nvec)
     source_re, source_im = source[:, :nvec], source[:, nvec:]
     right = jnp.concatenate([source, jnp.concatenate([-source_im, source_re], axis=1)], axis=0)
     dressed = jnp.dot(mixed, right, preferred_element_type=jnp.float32)

time: 99.1 us -> 111 us (1.12)
  waiting for transfers between devices: 20.8 us -> 42.2 us
  starting transfers between devices: 52.2 us -> 40.1 us
  other arithmetic: 0.64 us -> 2.64 us
    ppermute x18, waiting for transfers between devices: 19.8 us -> 36.6 us  [swap(): return lax.ppermute(value, 'space', [(i, i ^ bits) for i in range(16)])]
    all_to_all x2 -> x1, starting transfers between devices: 18.8 us -> 3.48 us  [steps(): lax.all_to_all(jnp.broadcast_to(spins, (4, *spins.shape)), 'space', split...]
    ppermute x1, waiting for transfers between devices: 0.45 us -> 4.26 us  [steps(): share = lax.ppermute(source, 'tm', [(t, 15 - t) for t in range(16)])]
    ppermute x18, starting transfers between devices: 33.3 us -> 36.6 us  [swap(): return lax.ppermute(value, 'space', [(i, i ^ bits) for i in range(16)])]
    transpose x0 -> x4, local copies, waits for them, and re-layouts: none -> 1.25 us  [the longest x1 1.02 us: steps(): tau = tau.transpose(2, 1, 0, 3).reshape(SPIN, nrows, 2 * nvec)]
  transfers between devices with their start and end apart: 21 -> 20, of which waited for: 7 -> 15; matrix products, arithmetic and copies ran while one was open for 2% -> 3% of each run, Pallas kernels for 10% -> 9%
where the time goes in v3:
time: 111 us; the launch traced here: 110 us
  waiting for transfers between devices  42.2 us (38%)
  starting transfers between devices  40.1 us (36%)
  Pallas kernels  19.8 us (18%)
  local copies, waits for them, and re-layouts  4.14 us (4%)
  other arithmetic  2.64 us (2%)
    ppermute x18, waiting for transfers between devices, swap(): return lax.ppermute(value, 'space', [(i, i ^ bits) for i in range(16)])  36.6 us
    ppermute x18, starting transfers between devices, swap(): return lax.ppermute(value, 'space', [(i, i ^ bits) for i in range(16)])  36.6 us
    pallas_call x2, Pallas kernels, gram(): pl.pallas_call(functools.partial(gram_kernel, which), grid_spec=pltpu.Pre...  19.8 us
    ppermute x1, waiting for transfers between devices, steps(): share = lax.ppermute(source, 'tm', [(t, 15 - t) for t in range(16)])  4.26 us
    all_to_all x1, starting transfers between devices, steps(): lax.all_to_all(jnp.broadcast_to(spins, (4, *spins.shape)), 'space', split...  3.48 us
  transfers between devices with their start and end apart: 20, of which 15 were waited for; matrix products, arithmetic and copies ran while one was open for 3% of the time, Pallas kernels for 9%

profile of v3, /device:TPU:8, one launch (start us, length us, event | category | flops | bytes accessed | tf_op | source)
XLA Modules:
  0.0 110.1 jit_solution(120267091055106370)
XLA Ops:
  0.0 1.0 copy.12
  1.0 0.1 reshape.49
  1.2 9.9 %shard_map.38 = (f32[96,768]{1,0:T(8,128)}, bf16[96,768]{1,0:T(8,128)(2,1)}, bf16[96,768]{1,0:T(8,128)(2,1)}, bf16[96,768]{1,0:T(8,128)(2,1)}) custom-call(s32[2,3]{1,0:T(2,128)} %momenta.3, bf16[1,2,3,1024,384]{4,3,2,1,0:T(8,128)(2,1)} %vec_ref.3), custom_call_target="tpu_custom_call" | custom-call | flops 3623878656 | bytes 4718592 | tf_op jit(solution)/shard_map/pallas_call | solution.py:83
  11.1 0.9 pad_maximum_fusion.4
  12.0 0.0 copy-start.2
  12.0 0.0 copy-start.1
  12.0 4.5 %collective-permute-start.5 = (bf16[120,768]{1,0:T(8,128)(2,1)S(1)}, bf16[120,768]{1,0:T(8,128)(2,1)S(1)}, u32[]{:S(2)}, u32[]{:S(2)}) collective-permute-start(bf16[120,768]{1,0:T(8,128)(2,1)S(1)} %pad_maximum_fusion.4), channel_id=1, source_target_pairs={{0,9},{1,8},{2,11},{3,10},{4,13},{5,12},{6,15},{7,14},{8,1},{9,0},... | collective-permute-start | bytes 552968 | tf_op jit(solution)/shard_map/ppermute | solution.py:110
  16.5 9.9 %shard_map.37 = (f32[96,768]{1,0:T(8,128)}, bf16[96,768]{1,0:T(8,128)(2,1)}, bf16[96,768]{1,0:T(8,128)(2,1)}, bf16[96,768]{1,0:T(8,128)(2,1)}) custom-call(s32[2,3]{1,0:T(2,128)} %momenta.3, bf16[1,2,3,1024,384]{4,3,2,1,0:T(8,128)(2,1)} %vec_ref.3), custom_call_target="tpu_custom_call" | custom-call | flops 3623878656 | bytes 4718592 | tf_op jit(solution)/shard_map/pallas_call | solution.py:83
  26.4 0.1 collective-permute-start
  26.5 0.5 collective-permute-start.1
  27.0 4.4 %collective-permute-start.2 = (bf16[96,768]{1,0:T(8,128)(2,1)}, bf16[96,768]{1,0:T(8,128)(2,1)S(1)}, u32[]{:S(2)}, u32[]{:S(2)}) collective-permute-start(bf16[96,768]{1,0:T(8,128)(2,1)} %get-tuple-element.16), channel_id=1, source_target_pairs={{0,9},{1,8},{2,11},{3,10},{4,13},{5,12},{6,15},{7,14},{8,1},{9,0},... | collective-permute-start | bytes 442376 | tf_op jit(solution)/shard_map/ppermute | solution.py:110
  31.4 0.6 collective-permute-start.4
  32.0 0.0 copy-done.1
  32.0 0.3 collective-permute-done
  32.3 0.0 collective-permute-start.3
  32.3 5.7 %collective-permute-done.1 = bf16[96,768]{1,0:T(8,128)(2,1)S(1)} collective-permute-done((bf16[96,768]{1,0:T(8,128)(2,1)}, bf16[96,768]{1,0:T(8,128)(2,1)S(1)}, u32[]{:S(2)}, u32[]{:S(2)}) %collective-permute-start.1) | collective-permute-done | bytes 147488 | tf_op jit(solution)/shard_map/ppermute | solution.py:110
  38.0 0.0 collective-permute-done.2
  38.0 1.0 convert_add_fusion.1
  39.1 0.0 collective-permute-done.5
  39.1 1.5 %collective-permute-done.4 = bf16[120,768]{1,0:T(8,128)(2,1)S(1)} collective-permute-done((bf16[120,768]{1,0:T(8,128)(2,1)S(1)}, bf16[120,768]{1,0:T(8,128)(2,1)S(1)}, u32[]{:S(2)}, u32[]{:S(2)}) %collective-permute-start.4) | collective-permute-done | bytes 184352 | tf_op jit(solution)/shard_map/ppermute | solution.py:110
  40.6 0.0 collective-permute-done.3
  40.6 0.1 convert_add_fusion
  40.7 3.4 %collective-permute-start.6 = (bf16[24,768]{1,0:T(8,128)(2,1)S(1)}, bf16[24,768]{1,0:T(8,128)(2,1)S(1)}, u32[]{:S(2)}, u32[]{:S(2)}) collective-permute-start(bf16[24,768]{1,0:T(8,128)(2,1)S(1)} %get-tuple-element.30), channel_id=1, source_target_pairs={{0,2},{1,3},{2,0},{3,1},{4,6},{5,7},{6,4},{7,5},{8,10},{9,11},{10,... | collective-permute-start | bytes 110600 | tf_op jit(solution)/shard_map/ppermute | solution.py:110
  44.1 4.2 %collective-permute-start.8 = (bf16[24,768]{1,0:T(8,128)(2,1)S(1)}, bf16[24,768]{1,0:T(8,128)(2,1)S(1)}, u32[]{:S(2)}, u32[]{:S(2)}) collective-permute-start(bf16[24,768]{1,0:T(8,128)(2,1)S(1)} %get-tuple-element.31), channel_id=1, source_target_pairs={{0,6},{1,7},{2,4},{3,5},{4,2},{5,3},{6,0},{7,1},{8,14},{9,15},{10,... | collective-permute-start | bytes 110600 | tf_op jit(solution)/shard_map/ppermute | solution.py:110
  48.3 0.9 collective-permute-start.7
  49.2 0.0 collective-permute-done.6
  49.2 1.0 collective-permute-done.8
  50.3 5.9 %collective-permute-done.7 = bf16[24,768]{1,0:T(8,128)(2,1)S(1)} collective-permute-done((bf16[24,768]{1,0:T(8,128)(2,1)S(1)}, bf16[24,768]{1,0:T(8,128)(2,1)S(1)}, u32[]{:S(2)}, u32[]{:S(2)}) %collective-permute-start.7) | collective-permute-done | bytes 36896 | tf_op jit(solution)/shard_map/ppermute | solution.py:110
  56.2 0.1 collective-permute-start.9
  56.3 4.3 %collective-permute-done.9 = bf16[24,768]{1,0:T(8,128)(2,1)S(1)} collective-permute-done((bf16[24,768]{1,0:T(8,128)(2,1)S(1)}, bf16[24,768]{1,0:T(8,128)(2,1)S(1)}, u32[]{:S(2)}, u32[]{:S(2)}) %collective-permute-start.9) | collective-permute-done | bytes 36896 | tf_op jit(solution)/shard_map/ppermute | solution.py:160
  60.6 1.5 %collective-permute-start.10 = (bf16[48,768]{1,0:T(8,128)(2,1)S(1)}, bf16[48,768]{1,0:T(8,128)(2,1)S(1)}, u32[]{:S(2)}, u32[]{:S(2)}) collective-permute-start(bf16[48,768]{1,0:T(8,128)(2,1)S(1)} %get-tuple-element.56), channel_id=1, source_target_pairs={{0,2},{1,3},{2,0},{3,1},{4,6},{5,7},{6,4},{7,5},{8,10},{9,11},{10,... | collective-permute-start | bytes 221192 | tf_op jit(solution)/shard_map/ppermute | solution.py:110
  62.2 1.0 collective-permute-start.11
  63.2 4.1 %collective-permute-start.12 = (bf16[48,768]{1,0:T(8,128)(2,1)S(1)}, bf16[48,768]{1,0:T(8,128)(2,1)S(1)}, u32[]{:S(2)}, u32[]{:S(2)}) collective-permute-start(bf16[48,768]{1,0:T(8,128)(2,1)S(1)} %get-tuple-element.58), channel_id=1, source_target_pairs={{0,6},{1,7},{2,4},{3,5},{4,2},{5,3},{6,0},{7,1},{8,14},{9,15},{10,... | collective-permute-start | bytes 221192 | tf_op jit(solution)/shard_map/ppermute | solution.py:110
  67.3 0.9 collective-permute-done.10
  68.2 2.7 %collective-permute-done.11 = bf16[48,768]{1,0:T(8,128)(2,1)S(1)} collective-permute-done((bf16[48,768]{1,0:T(8,128)(2,1)S(1)}, bf16[48,768]{1,0:T(8,128)(2,1)S(1)}, u32[]{:S(2)}, u32[]{:S(2)}) %collective-permute-start.11) | collective-permute-done | bytes 73760 | tf_op jit(solution)/shard_map/ppermute | solution.py:110
  70.9 0.7 collective-permute-done.12
  71.8 4.5 %collective-permute-start.15 = (bf16[120,768]{1,0:T(8,128)(2,1)S(1)}, bf16[120,768]{1,0:T(8,128)(2,1)S(1)}, u32[]{:S(2)}, u32[]{:S(2)}) collective-permute-start(bf16[120,768]{1,0:T(8,128)(2,1)S(1)} %pad_maximum_fusion.5), channel_id=1, source_target_pairs={{0,9},{1,8},{2,11},{3,10},{4,13},{5,12},{6,15},{7,14},{8,1},{9,0},... | collective-permute-start | bytes 552968 | tf_op jit(solution)/shard_map/ppermute | solution.py:110
  76.3 0.9 broadcast_in_dim.3
  77.1 3.5 %all-to-all-start = ((bf16[4,4,24,768]{3,2,1,0:T(8,128)(2,1)}), bf16[4,4,24,768]{3,2,1,0:T(8,128)(2,1)S(1)}, u32[]{:S(2)}, u32[]{:S(2)}) async-start(bf16[4,4,24,768]{3,2,1,0:T(8,128)(2,1)} %broadcast_in_dim.3), calls=%async_computation | async-start | bytes 1179648 | tf_op jit(solution)/shard_map/all_to_all | solution.py:149
  80.6 1.6 %collective-permute-start.14 = (bf16[120,768]{1,0:T(8,128)(2,1)S(1)}, bf16[120,768]{1,0:T(8,128)(2,1)S(1)}, u32[]{:S(2)}, u32[]{:S(2)}) collective-permute-start(bf16[120,768]{1,0:T(8,128)(2,1)S(1)} %pad_maximum_fusion.5), channel_id=1, source_target_pairs={{0,8},{1,9},{2,10},{3,11},{4,12},{5,13},{6,14},{7,15},{8,0},{9,1},... | collective-permute-start | bytes 552968 | tf_op jit(solution)/shard_map/ppermute | solution.py:110
  82.2 0.2 collective-permute-start.13
  82.4 0.0 collective-permute-done.15
  82.4 5.9 %collective-permute-done.14 = bf16[120,768]{1,0:T(8,128)(2,1)S(1)} collective-permute-done((bf16[120,768]{1,0:T(8,128)(2,1)S(1)}, bf16[120,768]{1,0:T(8,128)(2,1)S(1)}, u32[]{:S(2)}, u32[]{:S(2)}) %collective-permute-start.14) | collective-permute-done | bytes 184352 | tf_op jit(solution)/shard_map/ppermute | solution.py:110
  88.3 9.1 %collective-permute-done.13 = bf16[120,768]{1,0:T(8,128)(2,1)S(1)} collective-permute-done((bf16[120,768]{1,0:T(8,128)(2,1)S(1)}, bf16[120,768]{1,0:T(8,128)(2,1)S(1)}, u32[]{:S(2)}, u32[]{:S(2)}) %collective-permute-start.13) | collective-permute-done | bytes 184352 | tf_op jit(solution)/shard_map/ppermute | solution.py:110
  97.4 0.1 pad_maximum_fusion
  97.5 0.1 constant_dynamic-slice_fusion.3
  97.6 0.1 pad_maximum_fusion.1
  97.8 0.1 slice_negate_fusion
  97.9 1.3 %all-to-all-done = bf16[4,4,24,768]{3,2,1,0:T(8,128)(2,1)S(1)} async-done(((bf16[4,4,24,768]{3,2,1,0:T(8,128)(2,1)}), bf16[4,4,24,768]{3,2,1,0:T(8,128)(2,1)S(1)}, u32[]{:S(2)}, u32[]{:S(2)}) %all-to-all-start) | async-done | bytes 589856 | tf_op jit(solution)/shard_map/all_to_all | solution.py:149
  99.2 0.1 reshape.53
  99.3 0.1 copy.13
  99.4 0.3 convolution_convert_fusion
  99.8 2.8 %collective-permute-start.18 = (bf16[2,24,384]{2,1,0:T(8,128)(2,1)S(1)}, bf16[2,24,384]{2,1,0:T(8,128)(2,1)S(1)}, u32[]{:S(2)}, u32[]{:S(2)}) collective-permute-start(bf16[2,24,384]{2,1,0:T(8,128)(2,1)S(1)} %bitcast.121), channel_id=1, source_target_pairs={{0,9},{1,8},{2,11},{3,10},{4,13},{5,12},{6,15},{7,14},{8,1},{9,0},... | collective-permute-start | bytes 110600 | tf_op jit(solution)/shard_map/ppermute | solution.py:110
  102.6 1.9 %collective-permute-start.17 = (bf16[2,24,384]{2,1,0:T(8,128)(2,1)S(1)}, bf16[2,24,384]{2,1,0:T(8,128)(2,1)S(1)}, u32[]{:S(2)}, u32[]{:S(2)}) collective-permute-start(bf16[2,24,384]{2,1,0:T(8,128)(2,1)S(1)} %bitcast.119), channel_id=1, source_target_pairs={{0,8},{1,9},{2,10},{3,11},{4,12},{5,13},{6,14},{7,15},{8,0},{9,1},... | collective-permute-start | bytes 110600 | tf_op jit(solution)/shard_map/ppermute | solution.py:110
  104.5 0.4 collective-permute-start.16
  104.8 0.1 maximum_bitcast_fusion
  104.9 0.6 copy.16
  105.6 0.9 collective-permute-done.18
  106.4 1.6 %collective-permute-done.17 = bf16[2,24,384]{2,1,0:T(8,128)(2,1)S(1)} collective-permute-done((bf16[2,24,384]{2,1,0:T(8,128)(2,1)S(1)}, bf16[2,24,384]{2,1,0:T(8,128)(2,1)S(1)}, u32[]{:S(2)}, u32[]{:S(2)}) %collective-permute-start.17) | collective-permute-done | bytes 36896 | tf_op jit(solution)/shard_map/ppermute | solution.py:110
  108.0 0.4 collective-permute-done.16
  108.5 0.1 copy.14
  108.7 0.1 reshape.57
  108.8 0.5 fusion
  109.3 0.8 copy.17
  (38 shorter events, 0.6 us)
Async XLA Ops:
  12.0 19.4 %copy-start.2 = (bf16[96,768]{1,0:T(8,128)(2,1)S(1)}, bf16[96,768]{1,0:T(8,128)(2,1)}, u32[]{:S(2)}) copy-start(bf16[96,768]{1,0:T(8,128)(2,1)} %get-tuple-element.19) | copy-start | bytes 442372
  12.0 20.0 %copy-start.1 = (bf16[96,768]{1,0:T(8,128)(2,1)S(1)}, bf16[96,768]{1,0:T(8,128)(2,1)}, u32[]{:S(2)}) copy-start(bf16[96,768]{1,0:T(8,128)(2,1)} %get-tuple-element.18) | copy-start | bytes 442372
  12.0 27.0 %collective-permute-start.5 = (bf16[120,768]{1,0:T(8,128)(2,1)S(1)}, bf16[120,768]{1,0:T(8,128)(2,1)S(1)}, u32[]{:S(2)}, u32[]{:S(2)}) collective-permute-start(bf16[120,768]{1,0:T(8,128)(2,1)S(1)} %pad_maximum_fusion.4), channel_id=1, source_target_pairs={{0,9},{1,8},{2,11},{3,10},{4,13},{5,12},{6,15},{7,14},{8,1},{9,0},... | collective-permute-start | bytes 552968 | tf_op jit(solution)/shard_map/ppermute | solution.py:110
  26.4 14.2 %copy-start = (f32[96,768]{1,0:T(8,128)S(1)}, f32[96,768]{1,0:T(8,128)}, u32[]{:S(2)}) copy-start(f32[96,768]{1,0:T(8,128)} %get-tuple-element.17) | copy-start | bytes 884740
  26.4 5.9 %collective-permute-start = (bf16[96,768]{1,0:T(8,128)(2,1)}, bf16[96,768]{1,0:T(8,128)(2,1)S(1)}, u32[]{:S(2)}, u32[]{:S(2)}) collective-permute-start(bf16[96,768]{1,0:T(8,128)(2,1)} %get-tuple-element.14), channel_id=1, source_target_pairs={{0,1},{1,0},{2,3},{3,2},{4,5},{5,4},{6,7},{7,6},{8,9},{9,8},{10,11... | collective-permute-start | bytes 442376 | tf_op jit(solution)/shard_map/ppermute | solution.py:110
  26.5 11.5 %collective-permute-start.1 = (bf16[96,768]{1,0:T(8,128)(2,1)}, bf16[96,768]{1,0:T(8,128)(2,1)S(1)}, u32[]{:S(2)}, u32[]{:S(2)}) collective-permute-start(bf16[96,768]{1,0:T(8,128)(2,1)} %get-tuple-element.15), channel_id=1, source_target_pairs={{0,8},{1,9},{2,10},{3,11},{4,12},{5,13},{6,14},{7,15},{8,0},{9,1},... | collective-permute-start | bytes 442376 | tf_op jit(solution)/shard_map/ppermute | solution.py:110
  27.0 11.0 %collective-permute-start.2 = (bf16[96,768]{1,0:T(8,128)(2,1)}, bf16[96,768]{1,0:T(8,128)(2,1)S(1)}, u32[]{:S(2)}, u32[]{:S(2)}) collective-permute-start(bf16[96,768]{1,0:T(8,128)(2,1)} %get-tuple-element.16), channel_id=1, source_target_pairs={{0,9},{1,8},{2,11},{3,10},{4,13},{5,12},{6,15},{7,14},{8,1},{9,0},... | collective-permute-start | bytes 442376 | tf_op jit(solution)/shard_map/ppermute | solution.py:110
  31.4 9.2 %collective-permute-start.4 = (bf16[120,768]{1,0:T(8,128)(2,1)S(1)}, bf16[120,768]{1,0:T(8,128)(2,1)S(1)}, u32[]{:S(2)}, u32[]{:S(2)}) collective-permute-start(bf16[120,768]{1,0:T(8,128)(2,1)S(1)} %pad_maximum_fusion.3), channel_id=1, source_target_pairs={{0,8},{1,9},{2,10},{3,11},{4,12},{5,13},{6,14},{7,15},{8,0},{9,1},... | collective-permute-start | bytes 552968 | tf_op jit(solution)/shard_map/ppermute | solution.py:110
  32.3 8.3 %collective-permute-start.3 = (bf16[120,768]{1,0:T(8,128)(2,1)S(1)}, bf16[120,768]{1,0:T(8,128)(2,1)S(1)}, u32[]{:S(2)}, u32[]{:S(2)}) collective-permute-start(bf16[120,768]{1,0:T(8,128)(2,1)S(1)} %pad_maximum_fusion.2), channel_id=1, source_target_pairs={{0,1},{1,0},{2,3},{3,2},{4,5},{5,4},{6,7},{7,6},{8,9},{9,8},{10,11... | collective-permute-start | bytes 552968 | tf_op jit(solution)/shard_map/ppermute | solution.py:110
  40.7 8.5 %collective-permute-start.6 = (bf16[24,768]{1,0:T(8,128)(2,1)S(1)}, bf16[24,768]{1,0:T(8,128)(2,1)S(1)}, u32[]{:S(2)}, u32[]{:S(2)}) collective-permute-start(bf16[24,768]{1,0:T(8,128)(2,1)S(1)} %get-tuple-element.30), channel_id=1, source_target_pairs={{0,2},{1,3},{2,0},{3,1},{4,6},{5,7},{6,4},{7,5},{8,10},{9,11},{10,... | collective-permute-start | bytes 110600 | tf_op jit(solution)/shard_map/ppermute | solution.py:110
  44.1 6.2 %collective-permute-start.8 = (bf16[24,768]{1,0:T(8,128)(2,1)S(1)}, bf16[24,768]{1,0:T(8,128)(2,1)S(1)}, u32[]{:S(2)}, u32[]{:S(2)}) collective-permute-start(bf16[24,768]{1,0:T(8,128)(2,1)S(1)} %get-tuple-element.31), channel_id=1, source_target_pairs={{0,6},{1,7},{2,4},{3,5},{4,2},{5,3},{6,0},{7,1},{8,14},{9,15},{10,... | collective-permute-start | bytes 110600 | tf_op jit(solution)/shard_map/ppermute | solution.py:110
  48.3 7.9 %collective-permute-start.7 = (bf16[24,768]{1,0:T(8,128)(2,1)S(1)}, bf16[24,768]{1,0:T(8,128)(2,1)S(1)}, u32[]{:S(2)}, u32[]{:S(2)}) collective-permute-start(bf16[24,768]{1,0:T(8,128)(2,1)S(1)} %get-tuple-element.32), channel_id=1, source_target_pairs={{0,4},{1,5},{2,6},{3,7},{4,0},{5,1},{6,2},{7,3},{8,12},{9,13},{10,... | collective-permute-start | bytes 110600 | tf_op jit(solution)/shard_map/ppermute | solution.py:110
  56.2 4.4 %collective-permute-start.9 = (bf16[24,768]{1,0:T(8,128)(2,1)S(1)}, bf16[24,768]{1,0:T(8,128)(2,1)S(1)}, u32[]{:S(2)}, u32[]{:S(2)}) collective-permute-start(bf16[24,768]{1,0:T(8,128)(2,1)S(1)} %fusion.4), channel_id=1, source_target_pairs={{0,240},{16,224},{32,208},{48,192},{64,176},{80,160},{96,144},{112... | collective-permute-start | bytes 110600 | tf_op jit(solution)/shard_map/ppermute | solution.py:160
  60.6 7.6 %collective-permute-start.10 = (bf16[48,768]{1,0:T(8,128)(2,1)S(1)}, bf16[48,768]{1,0:T(8,128)(2,1)S(1)}, u32[]{:S(2)}, u32[]{:S(2)}) collective-permute-start(bf16[48,768]{1,0:T(8,128)(2,1)S(1)} %get-tuple-element.56), channel_id=1, source_target_pairs={{0,2},{1,3},{2,0},{3,1},{4,6},{5,7},{6,4},{7,5},{8,10},{9,11},{10,... | collective-permute-start | bytes 221192 | tf_op jit(solution)/shard_map/ppermute | solution.py:110
  62.2 8.7 %collective-permute-start.11 = (bf16[48,768]{1,0:T(8,128)(2,1)S(1)}, bf16[48,768]{1,0:T(8,128)(2,1)S(1)}, u32[]{:S(2)}, u32[]{:S(2)}) collective-permute-start(bf16[48,768]{1,0:T(8,128)(2,1)S(1)} %get-tuple-element.57), channel_id=1, source_target_pairs={{0,4},{1,5},{2,6},{3,7},{4,0},{5,1},{6,2},{7,3},{8,12},{9,13},{10,... | collective-permute-start | bytes 221192 | tf_op jit(solution)/shard_map/ppermute | solution.py:110
  63.2 8.4 %collective-permute-start.12 = (bf16[48,768]{1,0:T(8,128)(2,1)S(1)}, bf16[48,768]{1,0:T(8,128)(2,1)S(1)}, u32[]{:S(2)}, u32[]{:S(2)}) collective-permute-start(bf16[48,768]{1,0:T(8,128)(2,1)S(1)} %get-tuple-element.58), channel_id=1, source_target_pairs={{0,6},{1,7},{2,4},{3,5},{4,2},{5,3},{6,0},{7,1},{8,14},{9,15},{10,... | collective-permute-start | bytes 221192 | tf_op jit(solution)/shard_map/ppermute | solution.py:110
  71.8 10.6 %collective-permute-start.15 = (bf16[120,768]{1,0:T(8,128)(2,1)S(1)}, bf16[120,768]{1,0:T(8,128)(2,1)S(1)}, u32[]{:S(2)}, u32[]{:S(2)}) collective-permute-start(bf16[120,768]{1,0:T(8,128)(2,1)S(1)} %pad_maximum_fusion.5), channel_id=1, source_target_pairs={{0,9},{1,8},{2,11},{3,10},{4,13},{5,12},{6,15},{7,14},{8,1},{9,0},... | collective-permute-start | bytes 552968 | tf_op jit(solution)/shard_map/ppermute | solution.py:110
  77.1 22.1 %all-to-all-start = ((bf16[4,4,24,768]{3,2,1,0:T(8,128)(2,1)}), bf16[4,4,24,768]{3,2,1,0:T(8,128)(2,1)S(1)}, u32[]{:S(2)}, u32[]{:S(2)}) async-start(bf16[4,4,24,768]{3,2,1,0:T(8,128)(2,1)} %broadcast_in_dim.3), calls=%async_computation | async-start | bytes 1179648 | tf_op jit(solution)/shard_map/all_to_all | solution.py:149
  80.6 7.7 %collective-permute-start.14 = (bf16[120,768]{1,0:T(8,128)(2,1)S(1)}, bf16[120,768]{1,0:T(8,128)(2,1)S(1)}, u32[]{:S(2)}, u32[]{:S(2)}) collective-permute-start(bf16[120,768]{1,0:T(8,128)(2,1)S(1)} %pad_maximum_fusion.5), channel_id=1, source_target_pairs={{0,8},{1,9},{2,10},{3,11},{4,12},{5,13},{6,14},{7,15},{8,0},{9,1},... | collective-permute-start | bytes 552968 | tf_op jit(solution)/shard_map/ppermute | solution.py:110
  82.2 15.2 %collective-permute-start.13 = (bf16[120,768]{1,0:T(8,128)(2,1)S(1)}, bf16[120,768]{1,0:T(8,128)(2,1)S(1)}, u32[]{:S(2)}, u32[]{:S(2)}) collective-permute-start(bf16[120,768]{1,0:T(8,128)(2,1)S(1)} %pad_maximum_fusion.5), channel_id=1, source_target_pairs={{0,1},{1,0},{2,3},{3,2},{4,5},{5,4},{6,7},{7,6},{8,9},{9,8},{10,11... | collective-permute-start | bytes 552968 | tf_op jit(solution)/shard_map/ppermute | solution.py:110
  99.8 6.7 %collective-permute-start.18 = (bf16[2,24,384]{2,1,0:T(8,128)(2,1)S(1)}, bf16[2,24,384]{2,1,0:T(8,128)(2,1)S(1)}, u32[]{:S(2)}, u32[]{:S(2)}) collective-permute-start(bf16[2,24,384]{2,1,0:T(8,128)(2,1)S(1)} %bitcast.121), channel_id=1, source_target_pairs={{0,9},{1,8},{2,11},{3,10},{4,13},{5,12},{6,15},{7,14},{8,1},{9,0},... | collective-permute-start | bytes 110600 | tf_op jit(solution)/shard_map/ppermute | solution.py:110
  102.6 5.5 %collective-permute-start.17 = (bf16[2,24,384]{2,1,0:T(8,128)(2,1)S(1)}, bf16[2,24,384]{2,1,0:T(8,128)(2,1)S(1)}, u32[]{:S(2)}, u32[]{:S(2)}) collective-permute-start(bf16[2,24,384]{2,1,0:T(8,128)(2,1)S(1)} %bitcast.119), channel_id=1, source_target_pairs={{0,8},{1,9},{2,10},{3,11},{4,12},{5,13},{6,14},{7,15},{8,0},{9,1},... | collective-permute-start | bytes 110600 | tf_op jit(solution)/shard_map/ppermute | solution.py:110
  104.5 4.0 %collective-permute-start.16 = (bf16[2,24,384]{2,1,0:T(8,128)(2,1)S(1)}, bf16[2,24,384]{2,1,0:T(8,128)(2,1)S(1)}, u32[]{:S(2)}, u32[]{:S(2)}) collective-permute-start(bf16[2,24,384]{2,1,0:T(8,128)(2,1)S(1)} %bitcast.117), channel_id=1, source_target_pairs={{0,1},{1,0},{2,3},{3,2},{4,5},{5,4},{6,7},{7,6},{8,9},{9,8},{10,11... | collective-permute-start | bytes 110600 | tf_op jit(solution)/shard_map/ppermute | solution.py:110

commit v4 on v3

v4 whole, which is shorter than its diff:
```python
import functools
import math

import jax
import jax.numpy as jnp
from jax import lax
from jax.experimental import pallas as pl
from jax.experimental.pallas import tpu as pltpu
from jax.sharding import PartitionSpec as P


LAT = 32
LANES = 128
SPIN = 4
MEMBER_BITS = (0, 1, 8, 9)
QUAD_BITS = (0, 2, 4, 6)


def phase_of(winding):
    octant = (winding & 31) + 4
    quadrant = (octant >> 3) & 3
    angle = ((octant & 7) - 4).astype(jnp.float32) * (2.0 * math.pi / LAT)
    square = angle * angle
    sine = angle * (1 + square * (-1 / 6 + square * (1 / 120 + square * (-1 / 5040 + square * (1 / 362880)))))
    cosine = 1 + square * (-1 / 2 + square * (1 / 24 + square * (-1 / 720 + square * (1 / 40320 - square * (1 / 3628800)))))
    swap = (quadrant & 1) == 1
    cos_out = jnp.where(swap, sine, cosine)
    sin_out = jnp.where(swap, cosine, sine)
    cos_out = jnp.where((quadrant == 1) | (quadrant == 2), -cos_out, cos_out)
    sin_out = jnp.where(quadrant >= 2, -sin_out, sin_out)
    return cos_out, sin_out


def gram_kernel(which, chunks, momenta, vec_ref, spin_ref, keep_ref, *refs):
    send_refs = refs[:3]
    vec_buf, y_ref, left0, left1, right0, right1, acc_ref, sems = refs[3:]
    left = (left0, left1)
    right = (right0, right1)
    _, _, colors, sites, nvec = vec_ref.shape
    depth = sites // chunks
    rows_y = depth // LAT

    def fetch(step):
        return pltpu.make_async_copy(
            vec_ref.at[0, :, :, pl.ds(step * depth, depth), :], vec_buf.at[step], sems.at[step])

    for step in range(chunks):
        fetch(step).start()
    space = lax.axis_index("space")
    index = lax.broadcasted_iota(jnp.int32, (LAT, LANES), 0)
    cos_x, sin_x = phase_of(momenta[which, 0] * index)
    cos_y, sin_y = phase_of(momenta[which, 1] * index + momenta[which, 2] * space)
    y_ref[0] = cos_y
    y_ref[1] = sin_y

    def prepare(step):
        fetch(step).wait()
        for y in range(rows_y):
            at_y = step * rows_y + y
            cos_row = jnp.broadcast_to(y_ref[0, at_y : at_y + 1], (LAT, LANES))
            sin_row = jnp.broadcast_to(y_ref[1, at_y : at_y + 1], (LAT, LANES))
            cosine = cos_x * cos_row - sin_x * sin_row
            sine = sin_x * cos_row + cos_x * sin_row
            cosine = jnp.concatenate([cosine] * (nvec // LANES), axis=1)
            sine = jnp.concatenate([sine] * (nvec // LANES), axis=1)
            for color in range(colors):
                re = vec_buf[step, 0, color, y * LAT : (y + 1) * LAT]
                im = vec_buf[step, 1, color, y * LAT : (y + 1) * LAT]
                re32 = re.astype(jnp.float32)
                im32 = im.astype(jnp.float32)
                at = pl.ds(color * depth + y * LAT, LAT)
                right[step % 2][at, :nvec] = (cosine * re32 + sine * im32).astype(jnp.bfloat16)
                right[step % 2][at, nvec:] = (cosine * im32 - sine * re32).astype(jnp.bfloat16)
                left[step % 2][at, :nvec] = re
                left[step % 2][at, nvec:] = im

    prepare(0)
    for step in range(chunks):
        if step + 1 < chunks:
            prepare(step + 1)
        part = lax.dot_general(left[step % 2][...], right[step % 2][...], (((0,), (0,)), ((), ())),
                               preferred_element_type=jnp.float32)
        if step == 0:
            acc_ref[...] = part
        else:
            acc_ref[...] += part
    rows = nvec // 16
    here = space // 8 * 2 + space % 2
    for member, out_ref in enumerate((keep_ref, *send_refs)):
        target = space ^ MEMBER_BITS[member]
        for quad in range(4):
            owner = (target & 9) | (2 * quad)
            start = pl.multiple_of(owner * rows, 8)
            real = pl.ds(start, rows)
            imag = pl.ds(pl.multiple_of(start + nvec, 8), rows)
            at = pl.ds(quad * rows, rows)
            out_ref[at, :nvec] = (acc_ref[real, :nvec] + acc_ref[imag, nvec:]).astype(out_ref.dtype)
            out_ref[at, nvec:] = (acc_ref[real, nvec:] - acc_ref[imag, :nvec]).astype(out_ref.dtype)
        if spin_ref is not None and member:
            out_ref[pl.ds(4 * rows, rows), :] = spin_ref[here ^ member]


def gram(eigvec, momenta, which, spins=None, chunks=4):
    _, _, colors, sites, nvec = eigvec.shape
    depth = sites // chunks
    rows = nvec // 4
    extra = 0 if spins is None else spins.shape[1]
    outs = [((rows, 2 * nvec), jnp.float32)] + [((rows + extra, 2 * nvec), jnp.bfloat16)] * 3
    vmem = pl.BlockSpec(memory_space=pltpu.VMEM)
    kern = functools.partial(gram_kernel, which, chunks)
    if spins is None:
        body = lambda m, v, *r: kern(m, v, None, *r)
        ins = ()
    else:
        body = kern
        ins = (spins,)
    operand = pltpu.VMEM((colors * depth, 2 * nvec), jnp.bfloat16)
    return pl.pallas_call(
        body,
        in_specs=[pl.BlockSpec(memory_space=pltpu.SMEM), pl.BlockSpec(memory_space=pl.ANY)] + [vmem] * len(ins),
        out_specs=[vmem] * 4,
        scratch_shapes=[
            pltpu.VMEM((chunks, 2, colors, depth, nvec), jnp.bfloat16),
            pltpu.VMEM((2, LAT, LANES), jnp.float32),
            operand, operand, operand, operand,
            pltpu.VMEM((2 * nvec, 2 * nvec), jnp.float32),
            pltpu.SemaphoreType.DMA((chunks,)),
        ],
        out_shape=[jax.ShapeDtypeStruct(shape, kind) for shape, kind in outs],
        compiler_params=pltpu.CompilerParams(vmem_limit_bytes=62 << 20),
        cost_estimate=pl.CostEstimate(flops=8 * nvec * nvec * colors * sites, bytes_accessed=eigvec.size * 2, transcendentals=0),
    )(momenta, eigvec, *ins)


def swap(value, bits):
    return lax.ppermute(value, "space", [(i, i ^ bits) for i in range(16)])


def around(parts, bits):
    return [parts[0]] + [swap(parts[m], bits[m]) for m in (1, 2, 3)]


def wide_sum(parts):
    out = parts[0]
    for value in parts[1:]:
        out = out + value.astype(jnp.float32)
    return out


def in_place(parts, here):
    parts = jnp.stack(parts)
    return jnp.stack([lax.dynamic_index_in_dim(parts, m ^ here, keepdims=False) for m in range(4)])


def spread(total, here):
    rows = total.shape[0] // 4
    total = total.reshape(4, rows, total.shape[1])
    parts = [lax.dynamic_index_in_dim(total, here ^ m, keepdims=False) for m in range(4)]
    return parts[:1] + [part.astype(jnp.bfloat16) for part in parts[1:]]


def complex_right(value):
    half = value.shape[1] // 2
    return jnp.concatenate([value, jnp.concatenate([-value[:, half:], value[:, :half]], axis=1)], axis=0)


def by_owner(value, nrows):
    return value.reshape(2, 2, 4, nrows, -1).transpose(0, 2, 1, 3, 4).reshape(16 * nrows, -1)


def steps(eigvec, momenta, peram):
    tau = peram[0]
    nrows, nvec = tau.shape[1], tau.shape[3]
    place = lax.axis_index("space")
    quad = place // 2 % 4
    member = place // 8 * 2 + place % 2
    tau = tau.transpose(2, 1, 0, 3).reshape(SPIN, nrows, 2 * nvec)
    sink = gram(eigvec, momenta, 0, tau)
    source = gram(eigvec, momenta, 1)
    sink = around(sink, MEMBER_BITS)
    spins = [lax.dynamic_index_in_dim(tau, member, keepdims=False)] + [part[4 * nrows :] for part in sink[1:]]
    spins = in_place(spins, member)
    source = around(source, MEMBER_BITS)
    spins = around([spins.reshape(4 * nrows, 2 * nvec)] * 4, QUAD_BITS)
    sink = spread(wide_sum([sink[0]] + [part[: 4 * nrows] for part in sink[1:]]), quad)
    source = wide_sum(source)
    source = spread(source, quad)
    second = around([None] + [jnp.concatenate([source[m], sink[m]]) for m in (1, 2, 3)], QUAD_BITS)
    source = wide_sum([source[0]] + [part[:nrows] for part in second[1:]]).astype(jnp.bfloat16)
    sink = wide_sum([sink[0]] + [part[nrows:] for part in second[1:]]).astype(jnp.bfloat16)
    source = lax.ppermute(source, "tm", [(t, 15 - t) for t in range(16)])
    rows = jnp.concatenate(around([sink] * 4, MEMBER_BITS))
    source = in_place(around([source] * 4, QUAD_BITS), quad).reshape(4 * nrows, 2 * nvec)
    spins = in_place(spins, quad).reshape(4, 4, nrows, 2 * nvec).transpose(1, 0, 2, 3)
    mixed = jnp.dot(rows, complex_right(by_owner(spins, nrows)), preferred_element_type=jnp.float32)
    mixed = mixed.astype(jnp.bfloat16).reshape(4, nrows, 2 * nvec)
    third = around([None] + [jnp.concatenate([source, mixed[m]]) for m in (1, 2, 3)], MEMBER_BITS)
    mixed = in_place([mixed[0]] + [part[4 * nrows :] for part in third[1:]], member)
    mixed = mixed.transpose(1, 0, 2).reshape(nrows * SPIN, 2 * nvec)
    source = in_place([source] + [part[: 4 * nrows] for part in third[1:]], member)
    dressed = jnp.dot(mixed, complex_right(by_owner(source, nrows)), preferred_element_type=jnp.float32)
    return dressed.reshape(1, nrows, SPIN, 2, nvec).astype(jnp.bfloat16)


def solution(mesh):
    return jax.shard_map(
        steps,
        mesh=mesh,
        in_specs=(P("tm", None, None, "space", None), P(), P("tm", None, "space", None, None)),
        out_specs=P("tm", "space", None, None, None),
        check_vma=False,
    )
```

time: 111 us -> 93.1 us (0.84)
  waiting for transfers between devices: 42.2 us -> 20.6 us
  starting transfers between devices: 40.1 us -> 45.6 us
  other arithmetic: 2.64 us -> 0.85 us
    ppermute x18 -> x21, waiting for transfers between devices: 36.6 us -> 19.2 us  [swap(): return lax.ppermute(value, 'space', [(i, i ^ bits) for i in range(16)])]
    ppermute x18 -> x21, starting transfers between devices: 36.6 us -> 45.5 us  [swap(): return lax.ppermute(value, 'space', [(i, i ^ bits) for i in range(16)])]
    all_to_all x1 -> x0, starting transfers between devices: 3.48 us -> none  [steps(): lax.all_to_all(jnp.broadcast_to(spins, (4, *spins.shape)), 'space', split...]
    ppermute x1, waiting for transfers between devices: 4.26 us -> 1.41 us  [steps(): source = lax.ppermute(source, 'tm', [(t, 15 - t) for t in range(16)])]
    all_to_all x1 -> x0, waiting for transfers between devices: 1.31 us -> none  [steps(): lax.all_to_all(jnp.broadcast_to(spins, (4, *spins.shape)), 'space', split...]
  transfers between devices with their start and end apart: 20 -> 22, of which waited for: 15 -> 10; matrix products, arithmetic and copies ran while one was open for 3% -> 2% of each run, Pallas kernels for 9% -> 11%
where the time goes in v4:
time: 93.1 us; the launch traced here: 91.6 us
  starting transfers between devices  45.6 us (49%)
  waiting for transfers between devices  20.6 us (22%)
  Pallas kernels  19.9 us (21%)
  local copies, waits for them, and re-layouts  3.45 us (4%)
    ppermute x21, starting transfers between devices, swap(): return lax.ppermute(value, 'space', [(i, i ^ bits) for i in range(16)])  45.5 us
    pallas_call x2, Pallas kernels, gram(): pl.pallas_call(body, in_specs=[pl.BlockSpec(memory_space=pltpu.SMEM), pl....  19.9 us
    ppermute x21, waiting for transfers between devices, swap(): return lax.ppermute(value, 'space', [(i, i ^ bits) for i in range(16)])  19.2 us
  transfers between devices with their start and end apart: 22, of which 10 were waited for; matrix products, arithmetic and copies ran while one was open for 2% of the time, Pallas kernels for 11%

profile of v4, /device:TPU:8, one launch (start us, length us, event | category | flops | bytes accessed | tf_op | source)
XLA Modules:
  0.0 91.6 jit_solution(8872321157887361358)
XLA Ops:
  0.0 9.8 %shard_map.38 = (f32[96,768]{1,0:T(8,128)}, bf16[96,768]{1,0:T(8,128)(2,1)}, bf16[96,768]{1,0:T(8,128)(2,1)}, bf16[96,768]{1,0:T(8,128)(2,1)}) custom-call(s32[2,3]{1,0:T(2,128)} %m.1, bf16[1,2,3,1024,384]{4,3,2,1,0:T(8,128)(2,1)} %v.1), custom_call_target="tpu_custom_call" | custom-call | flops 3623878656 | bytes 4718592 | tf_op jit(solution)/shard_map/pallas_call | solution.py:118
  9.8 2.0 %collective-permute-start.3 = (bf16[96,768]{1,0:T(8,128)(2,1)}, bf16[96,768]{1,0:T(8,128)(2,1)S(1)}, u32[]{:S(2)}, u32[]{:S(2)}) collective-permute-start(bf16[96,768]{1,0:T(8,128)(2,1)} %get-tuple-element.18), channel_id=1, source_target_pairs={{0,1},{1,0},{2,3},{3,2},{4,5},{5,4},{6,7},{7,6},{8,9},{9,8},{10,11... | collective-permute-start | bytes 442376 | tf_op jit(solution)/shard_map/ppermute | solution.py:136
  11.8 3.0 %collective-permute-start.4 = (bf16[96,768]{1,0:T(8,128)(2,1)}, bf16[96,768]{1,0:T(8,128)(2,1)S(1)}, u32[]{:S(2)}, u32[]{:S(2)}) collective-permute-start(bf16[96,768]{1,0:T(8,128)(2,1)} %get-tuple-element.19), channel_id=1, source_target_pairs={{0,8},{1,9},{2,10},{3,11},{4,12},{5,13},{6,14},{7,15},{8,0},{9,1},... | collective-permute-start | bytes 442376 | tf_op jit(solution)/shard_map/ppermute | solution.py:136
  14.9 0.1 collective-permute-start.5
  14.9 0.1 copy.15
  15.0 0.8 reshape.51.spin_ref
  15.8 10.0 %shard_map.37 = (f32[96,768]{1,0:T(8,128)}, bf16[120,768]{1,0:T(8,128)(2,1)}, bf16[120,768]{1,0:T(8,128)(2,1)}, bf16[120,768]{1,0:T(8,128)(2,1)}) custom-call(s32[2,3]{1,0:T(2,128)} %m.1, bf16[1,2,3,1024,384]{4,3,2,1,0:T(8,128)(2,1)} %v.1, bf16[4,24,768]{2,1,0:T(8,128)(2,1)} %reshape.51.spin_ref), custom_call_target="tpu_custom_call" | custom-call | flops 3623878656 | bytes 4718592 | tf_op jit(solution)/shard_map/pallas_call | solution.py:118
  25.9 2.0 %collective-permute-start = (bf16[120,768]{1,0:T(8,128)(2,1)}, bf16[120,768]{1,0:T(8,128)(2,1)S(1)}, u32[]{:S(2)}, u32[]{:S(2)}) collective-permute-start(bf16[120,768]{1,0:T(8,128)(2,1)} %get-tuple-element.14), channel_id=1, source_target_pairs={{0,1},{1,0},{2,3},{3,2},{4,5},{5,4},{6,7},{7,6},{8,9},{9,8},{10,11... | collective-permute-start | bytes 552968 | tf_op jit(solution)/shard_map/ppermute | solution.py:136
  27.9 3.0 %collective-permute-start.1 = (bf16[120,768]{1,0:T(8,128)(2,1)}, bf16[120,768]{1,0:T(8,128)(2,1)S(1)}, u32[]{:S(2)}, u32[]{:S(2)}) collective-permute-start(bf16[120,768]{1,0:T(8,128)(2,1)} %get-tuple-element.15), channel_id=1, source_target_pairs={{0,8},{1,9},{2,10},{3,11},{4,12},{5,13},{6,14},{7,15},{8,0},{9,1},... | collective-permute-start | bytes 552968 | tf_op jit(solution)/shard_map/ppermute | solution.py:136
  30.9 0.8 constant_dynamic-slice_fusion.20
  31.7 0.0 collective-permute-done.3
  31.7 0.1 collective-permute-start.2
  31.7 0.0 collective-permute-done.4
  31.7 0.0 collective-permute-done.5
  31.7 0.1 convert_add_fusion
  31.8 0.2 collective-permute-done
  32.0 5.9 %collective-permute-done.1 = bf16[120,768]{1,0:T(8,128)(2,1)S(1)} collective-permute-done((bf16[120,768]{1,0:T(8,128)(2,1)}, bf16[120,768]{1,0:T(8,128)(2,1)S(1)}, u32[]{:S(2)}, u32[]{:S(2)}) %collective-permute-start.1) | collective-permute-done | bytes 184352 | tf_op jit(solution)/shard_map/ppermute | solution.py:136
  37.9 1.9 %collective-permute-done.2 = bf16[120,768]{1,0:T(8,128)(2,1)S(1)} collective-permute-done((bf16[120,768]{1,0:T(8,128)(2,1)}, bf16[120,768]{1,0:T(8,128)(2,1)S(1)}, u32[]{:S(2)}, u32[]{:S(2)}) %collective-permute-start.2) | collective-permute-done | bytes 184352 | tf_op jit(solution)/shard_map/ppermute | solution.py:136
  39.8 0.1 convert_add_fusion.1
  40.0 3.8 %collective-permute-start.6 = (bf16[48,768]{1,0:T(8,128)(2,1)S(1)}, bf16[48,768]{1,0:T(8,128)(2,1)S(1)}, u32[]{:S(2)}, u32[]{:S(2)}) collective-permute-start(bf16[48,768]{1,0:T(8,128)(2,1)S(1)} %pad_maximum_fusion.12), channel_id=1, source_target_pairs={{0,2},{1,3},{2,0},{3,1},{4,6},{5,7},{6,4},{7,5},{8,10},{9,11},{10,... | collective-permute-start | bytes 221192 | tf_op jit(solution)/shard_map/ppermute | solution.py:136
  43.8 4.1 %collective-permute-start.7 = (bf16[48,768]{1,0:T(8,128)(2,1)S(1)}, bf16[48,768]{1,0:T(8,128)(2,1)S(1)}, u32[]{:S(2)}, u32[]{:S(2)}) collective-permute-start(bf16[48,768]{1,0:T(8,128)(2,1)S(1)} %pad_maximum_fusion.13), channel_id=1, source_target_pairs={{0,4},{1,5},{2,6},{3,7},{4,0},{5,1},{6,2},{7,3},{8,12},{9,13},{10,... | collective-permute-start | bytes 221192 | tf_op jit(solution)/shard_map/ppermute | solution.py:136
  47.8 0.0 collective-permute-start.8
  48.0 2.5 %collective-permute-start.12 = (bf16[96,768]{1,0:T(8,128)(2,1)S(1)}, bf16[96,768]{1,0:T(8,128)(2,1)S(1)}, u32[]{:S(2)}, u32[]{:S(2)}) collective-permute-start(bf16[96,768]{1,0:T(8,128)(2,1)S(1)} %bitcast.104), channel_id=1, source_target_pairs={{0,2},{1,3},{2,0},{3,1},{4,6},{5,7},{6,4},{7,5},{8,10},{9,11},{10,... | collective-permute-start | bytes 442376 | tf_op jit(solution)/shard_map/ppermute | solution.py:136
  50.5 4.1 %collective-permute-start.13 = (bf16[96,768]{1,0:T(8,128)(2,1)S(1)}, bf16[96,768]{1,0:T(8,128)(2,1)S(1)}, u32[]{:S(2)}, u32[]{:S(2)}) collective-permute-start(bf16[96,768]{1,0:T(8,128)(2,1)S(1)} %bitcast.105), channel_id=1, source_target_pairs={{0,4},{1,5},{2,6},{3,7},{4,0},{5,1},{6,2},{7,3},{8,12},{9,13},{10,... | collective-permute-start | bytes 442376 | tf_op jit(solution)/shard_map/ppermute | solution.py:136
  54.5 0.0 collective-permute-done.6
  54.5 0.0 collective-permute-start.14
  54.6 0.0 collective-permute-done.7
  54.6 1.3 %collective-permute-done.8 = bf16[48,768]{1,0:T(8,128)(2,1)S(1)} collective-permute-done((bf16[48,768]{1,0:T(8,128)(2,1)S(1)}, bf16[48,768]{1,0:T(8,128)(2,1)S(1)}, u32[]{:S(2)}, u32[]{:S(2)}) %collective-permute-start.8) | collective-permute-done | bytes 73760 | tf_op jit(solution)/shard_map/ppermute | solution.py:136
  55.9 0.1 collective-permute-start.15
  56.0 3.0 %collective-permute-start.10 = (bf16[24,768]{1,0:T(8,128)(2,1)S(1)}, bf16[24,768]{1,0:T(8,128)(2,1)S(1)}, u32[]{:S(2)}, u32[]{:S(2)}) collective-permute-start(bf16[24,768]{1,0:T(8,128)(2,1)S(1)} %get-tuple-element.40), channel_id=1, source_target_pairs={{0,8},{1,9},{2,10},{3,11},{4,12},{5,13},{6,14},{7,15},{8,0},{9,1},... | collective-permute-start | bytes 110600 | tf_op jit(solution)/shard_map/ppermute | solution.py:136
  59.0 1.4 %collective-permute-done.15 = bf16[24,768]{1,0:T(8,128)(2,1)S(1)} collective-permute-done((bf16[24,768]{1,0:T(8,128)(2,1)S(1)}, bf16[24,768]{1,0:T(8,128)(2,1)S(1)}, u32[]{:S(2)}, u32[]{:S(2)}) %collective-permute-start.15) | collective-permute-done | bytes 36896 | tf_op jit(solution)/shard_map/ppermute | solution.py:191
  60.4 6.2 %collective-permute-start.11 = (bf16[24,768]{1,0:T(8,128)(2,1)S(1)}, bf16[24,768]{1,0:T(8,128)(2,1)S(1)}, u32[]{:S(2)}, u32[]{:S(2)}) collective-permute-start(bf16[24,768]{1,0:T(8,128)(2,1)S(1)} %get-tuple-element.40), channel_id=1, source_target_pairs={{0,9},{1,8},{2,11},{3,10},{4,13},{5,12},{6,15},{7,14},{8,1},{9,0},... | collective-permute-start | bytes 110600 | tf_op jit(solution)/shard_map/ppermute | solution.py:136
  66.5 0.0 collective-permute-done.12
  66.5 0.0 collective-permute-start.16
  66.5 0.0 collective-permute-done.13
  66.5 3.3 %collective-permute-start.17 = (bf16[24,768]{1,0:T(8,128)(2,1)S(1)}, bf16[24,768]{1,0:T(8,128)(2,1)S(1)}, u32[]{:S(2)}, u32[]{:S(2)}) collective-permute-start(bf16[24,768]{1,0:T(8,128)(2,1)S(1)} %collective-permute-done.15), channel_id=1, source_target_pairs={{0,4},{1,5},{2,6},{3,7},{4,0},{5,1},{6,2},{7,3},{8,12},{9,13},{10,... | collective-permute-start | bytes 110600 | tf_op jit(solution)/shard_map/ppermute | solution.py:136
  69.8 0.0 collective-permute-done.14
  69.9 3.2 %collective-permute-start.18 = (bf16[24,768]{1,0:T(8,128)(2,1)S(1)}, bf16[24,768]{1,0:T(8,128)(2,1)S(1)}, u32[]{:S(2)}, u32[]{:S(2)}) collective-permute-start(bf16[24,768]{1,0:T(8,128)(2,1)S(1)} %collective-permute-done.15), channel_id=1, source_target_pairs={{0,6},{1,7},{2,4},{3,5},{4,2},{5,3},{6,0},{7,1},{8,14},{9,15},{10,... | collective-permute-start | bytes 110600 | tf_op jit(solution)/shard_map/ppermute | solution.py:136
  73.0 0.1 pad_maximum_fusion
  73.1 0.1 constant_dynamic-slice_fusion.15
  73.2 0.1 pad_maximum_fusion.1
  73.3 0.1 slice_negate_fusion.1
  73.4 0.0 collective-permute-done.16
  73.4 0.2 collective-permute-start.9
  73.6 1.0 %collective-permute-done.17 = bf16[24,768]{1,0:T(8,128)(2,1)S(1)} collective-permute-done((bf16[24,768]{1,0:T(8,128)(2,1)S(1)}, bf16[24,768]{1,0:T(8,128)(2,1)S(1)}, u32[]{:S(2)}, u32[]{:S(2)}) %collective-permute-start.17) | collective-permute-done | bytes 36896 | tf_op jit(solution)/shard_map/ppermute | solution.py:136
  74.6 1.3 %collective-permute-done.18 = bf16[24,768]{1,0:T(8,128)(2,1)S(1)} collective-permute-done((bf16[24,768]{1,0:T(8,128)(2,1)S(1)}, bf16[24,768]{1,0:T(8,128)(2,1)S(1)}, u32[]{:S(2)}, u32[]{:S(2)}) %collective-permute-start.18) | collective-permute-done | bytes 36896 | tf_op jit(solution)/shard_map/ppermute | solution.py:136
  76.0 0.0 collective-permute-done.10
  76.0 0.0 collective-permute-done.11
  76.0 1.4 %collective-permute-done.9 = bf16[24,768]{1,0:T(8,128)(2,1)S(1)} collective-permute-done((bf16[24,768]{1,0:T(8,128)(2,1)S(1)}, bf16[24,768]{1,0:T(8,128)(2,1)S(1)}, u32[]{:S(2)}, u32[]{:S(2)}) %collective-permute-start.9) | collective-permute-done | bytes 36896 | tf_op jit(solution)/shard_map/ppermute | solution.py:136
  77.4 0.3 fusion.6
  77.9 0.2 collective-permute-start.21
  78.1 3.1 %collective-permute-start.20 = (bf16[120,768]{1,0:T(8,128)(2,1)S(1)}, bf16[120,768]{1,0:T(8,128)(2,1)S(1)}, u32[]{:S(2)}, u32[]{:S(2)}) collective-permute-start(bf16[120,768]{1,0:T(8,128)(2,1)S(1)} %get-tuple-element.50), channel_id=1, source_target_pairs={{0,8},{1,9},{2,10},{3,11},{4,12},{5,13},{6,14},{7,15},{8,0},{9,1},... | collective-permute-start | bytes 552968 | tf_op jit(solution)/shard_map/ppermute | solution.py:136
  81.2 1.7 %collective-permute-start.19 = (bf16[120,768]{1,0:T(8,128)(2,1)S(1)}, bf16[120,768]{1,0:T(8,128)(2,1)S(1)}, u32[]{:S(2)}, u32[]{:S(2)}) collective-permute-start(bf16[120,768]{1,0:T(8,128)(2,1)S(1)} %get-tuple-element.49), channel_id=1, source_target_pairs={{0,1},{1,0},{2,3},{3,2},{4,5},{5,4},{6,7},{7,6},{8,9},{9,8},{10,11... | collective-permute-start | bytes 552968 | tf_op jit(solution)/shard_map/ppermute | solution.py:136
  82.9 4.3 %collective-permute-done.21 = bf16[120,768]{1,0:T(8,128)(2,1)S(1)} collective-permute-done((bf16[120,768]{1,0:T(8,128)(2,1)S(1)}, bf16[120,768]{1,0:T(8,128)(2,1)S(1)}, u32[]{:S(2)}, u32[]{:S(2)}) %collective-permute-start.21) | collective-permute-done | bytes 184352 | tf_op jit(solution)/shard_map/ppermute | solution.py:136
  87.2 1.8 %collective-permute-done.20 = bf16[120,768]{1,0:T(8,128)(2,1)S(1)} collective-permute-done((bf16[120,768]{1,0:T(8,128)(2,1)S(1)}, bf16[120,768]{1,0:T(8,128)(2,1)S(1)}, u32[]{:S(2)}, u32[]{:S(2)}) %collective-permute-start.20) | collective-permute-done | bytes 184352 | tf_op jit(solution)/shard_map/ppermute | solution.py:136
  89.1 0.0 collective-permute-done.19
  89.2 0.1 pad_maximum_fusion.2
  89.3 0.1 constant_dynamic-slice_fusion.3
  89.3 0.1 pad_maximum_fusion.3
  89.5 0.1 slice_negate_fusion
  89.5 0.1 maximum_bitcast_fusion
  89.6 0.6 copy.19
  90.3 0.5 fusion.9
  90.8 0.8 copy.20
  (32 shorter events, 0.5 us)
Async XLA Ops:
  0.0 14.9 %copy-start.2 = (bf16[1,2,24,4,384]{4,3,2,1,0:T(4,128)(2,1)S(1)}, bf16[1,2,24,4,384]{4,3,2,1,0:T(4,128)(2,1)}, u32[]{:S(2)}) copy-start(bf16[1,2,24,4,384]{4,3,2,1,0:T(4,128)(2,1)} %param.5) | copy-start | bytes 442372
  9.8 21.8 %collective-permute-start.3 = (bf16[96,768]{1,0:T(8,128)(2,1)}, bf16[96,768]{1,0:T(8,128)(2,1)S(1)}, u32[]{:S(2)}, u32[]{:S(2)}) collective-permute-start(bf16[96,768]{1,0:T(8,128)(2,1)} %get-tuple-element.18), channel_id=1, source_target_pairs={{0,1},{1,0},{2,3},{3,2},{4,5},{5,4},{6,7},{7,6},{8,9},{9,8},{10,11... | collective-permute-start | bytes 442376 | tf_op jit(solution)/shard_map/ppermute | solution.py:136
  11.8 19.9 %collective-permute-start.4 = (bf16[96,768]{1,0:T(8,128)(2,1)}, bf16[96,768]{1,0:T(8,128)(2,1)S(1)}, u32[]{:S(2)}, u32[]{:S(2)}) collective-permute-start(bf16[96,768]{1,0:T(8,128)(2,1)} %get-tuple-element.19), channel_id=1, source_target_pairs={{0,8},{1,9},{2,10},{3,11},{4,12},{5,13},{6,14},{7,15},{8,0},{9,1},... | collective-permute-start | bytes 442376 | tf_op jit(solution)/shard_map/ppermute | solution.py:136
  14.9 16.9 %collective-permute-start.5 = (bf16[96,768]{1,0:T(8,128)(2,1)}, bf16[96,768]{1,0:T(8,128)(2,1)S(1)}, u32[]{:S(2)}, u32[]{:S(2)}) collective-permute-start(bf16[96,768]{1,0:T(8,128)(2,1)} %get-tuple-element.20), channel_id=1, source_target_pairs={{0,9},{1,8},{2,11},{3,10},{4,13},{5,12},{6,15},{7,14},{8,1},{9,0},... | collective-permute-start | bytes 442376 | tf_op jit(solution)/shard_map/ppermute | solution.py:136
  15.8 15.9 %copy-start = (f32[96,768]{1,0:T(8,128)S(1)}, f32[96,768]{1,0:T(8,128)}, u32[]{:S(2)}) copy-start(f32[96,768]{1,0:T(8,128)} %get-tuple-element.17) | copy-start | bytes 884740
  25.9 14.0 %copy-start.1 = (f32[96,768]{1,0:T(8,128)S(1)}, f32[96,768]{1,0:T(8,128)}, u32[]{:S(2)}) copy-start(f32[96,768]{1,0:T(8,128)} %get-tuple-element.13) | copy-start | bytes 884740
  25.9 6.2 %collective-permute-start = (bf16[120,768]{1,0:T(8,128)(2,1)}, bf16[120,768]{1,0:T(8,128)(2,1)S(1)}, u32[]{:S(2)}, u32[]{:S(2)}) collective-permute-start(bf16[120,768]{1,0:T(8,128)(2,1)} %get-tuple-element.14), channel_id=1, source_target_pairs={{0,1},{1,0},{2,3},{3,2},{4,5},{5,4},{6,7},{7,6},{8,9},{9,8},{10,11... | collective-permute-start | bytes 552968 | tf_op jit(solution)/shard_map/ppermute | solution.py:136
  27.9 10.1 %collective-permute-start.1 = (bf16[120,768]{1,0:T(8,128)(2,1)}, bf16[120,768]{1,0:T(8,128)(2,1)S(1)}, u32[]{:S(2)}, u32[]{:S(2)}) collective-permute-start(bf16[120,768]{1,0:T(8,128)(2,1)} %get-tuple-element.15), channel_id=1, source_target_pairs={{0,8},{1,9},{2,10},{3,11},{4,12},{5,13},{6,14},{7,15},{8,0},{9,1},... | collective-permute-start | bytes 552968 | tf_op jit(solution)/shard_map/ppermute | solution.py:136
  31.7 8.2 %collective-permute-start.2 = (bf16[120,768]{1,0:T(8,128)(2,1)}, bf16[120,768]{1,0:T(8,128)(2,1)S(1)}, u32[]{:S(2)}, u32[]{:S(2)}) collective-permute-start(bf16[120,768]{1,0:T(8,128)(2,1)} %get-tuple-element.16), channel_id=1, source_target_pairs={{0,9},{1,8},{2,11},{3,10},{4,13},{5,12},{6,15},{7,14},{8,1},{9,0},... | collective-permute-start | bytes 552968 | tf_op jit(solution)/shard_map/ppermute | solution.py:136
  40.0 14.6 %collective-permute-start.6 = (bf16[48,768]{1,0:T(8,128)(2,1)S(1)}, bf16[48,768]{1,0:T(8,128)(2,1)S(1)}, u32[]{:S(2)}, u32[]{:S(2)}) collective-permute-start(bf16[48,768]{1,0:T(8,128)(2,1)S(1)} %pad_maximum_fusion.12), channel_id=1, source_target_pairs={{0,2},{1,3},{2,0},{3,1},{4,6},{5,7},{6,4},{7,5},{8,10},{9,11},{10,... | collective-permute-start | bytes 221192 | tf_op jit(solution)/shard_map/ppermute | solution.py:136
  43.8 10.8 %collective-permute-start.7 = (bf16[48,768]{1,0:T(8,128)(2,1)S(1)}, bf16[48,768]{1,0:T(8,128)(2,1)S(1)}, u32[]{:S(2)}, u32[]{:S(2)}) collective-permute-start(bf16[48,768]{1,0:T(8,128)(2,1)S(1)} %pad_maximum_fusion.13), channel_id=1, source_target_pairs={{0,4},{1,5},{2,6},{3,7},{4,0},{5,1},{6,2},{7,3},{8,12},{9,13},{10,... | collective-permute-start | bytes 221192 | tf_op jit(solution)/shard_map/ppermute | solution.py:136
  47.8 8.0 %collective-permute-start.8 = (bf16[48,768]{1,0:T(8,128)(2,1)S(1)}, bf16[48,768]{1,0:T(8,128)(2,1)S(1)}, u32[]{:S(2)}, u32[]{:S(2)}) collective-permute-start(bf16[48,768]{1,0:T(8,128)(2,1)S(1)} %pad_maximum_fusion.14), channel_id=1, source_target_pairs={{0,6},{1,7},{2,4},{3,5},{4,2},{5,3},{6,0},{7,1},{8,14},{9,15},{10,... | collective-permute-start | bytes 221192 | tf_op jit(solution)/shard_map/ppermute | solution.py:136
  48.0 18.6 %collective-permute-start.12 = (bf16[96,768]{1,0:T(8,128)(2,1)S(1)}, bf16[96,768]{1,0:T(8,128)(2,1)S(1)}, u32[]{:S(2)}, u32[]{:S(2)}) collective-permute-start(bf16[96,768]{1,0:T(8,128)(2,1)S(1)} %bitcast.104), channel_id=1, source_target_pairs={{0,2},{1,3},{2,0},{3,1},{4,6},{5,7},{6,4},{7,5},{8,10},{9,11},{10,... | collective-permute-start | bytes 442376 | tf_op jit(solution)/shard_map/ppermute | solution.py:136
  50.5 16.1 %collective-permute-start.13 = (bf16[96,768]{1,0:T(8,128)(2,1)S(1)}, bf16[96,768]{1,0:T(8,128)(2,1)S(1)}, u32[]{:S(2)}, u32[]{:S(2)}) collective-permute-start(bf16[96,768]{1,0:T(8,128)(2,1)S(1)} %bitcast.105), channel_id=1, source_target_pairs={{0,4},{1,5},{2,6},{3,7},{4,0},{5,1},{6,2},{7,3},{8,12},{9,13},{10,... | collective-permute-start | bytes 442376 | tf_op jit(solution)/shard_map/ppermute | solution.py:136
  54.5 15.3 %collective-permute-start.14 = (bf16[96,768]{1,0:T(8,128)(2,1)S(1)}, bf16[96,768]{1,0:T(8,128)(2,1)S(1)}, u32[]{:S(2)}, u32[]{:S(2)}) collective-permute-start(bf16[96,768]{1,0:T(8,128)(2,1)S(1)} %bitcast.106), channel_id=1, source_target_pairs={{0,6},{1,7},{2,4},{3,5},{4,2},{5,3},{6,0},{7,1},{8,14},{9,15},{10,... | collective-permute-start | bytes 442376 | tf_op jit(solution)/shard_map/ppermute | solution.py:136
  55.9 4.5 %collective-permute-start.15 = (bf16[24,768]{1,0:T(8,128)(2,1)S(1)}, bf16[24,768]{1,0:T(8,128)(2,1)S(1)}, u32[]{:S(2)}, u32[]{:S(2)}) collective-permute-start(bf16[24,768]{1,0:T(8,128)(2,1)S(1)} %get-tuple-element.39), channel_id=1, source_target_pairs={{0,240},{16,224},{32,208},{48,192},{64,176},{80,160},{96,144},{112... | collective-permute-start | bytes 110600 | tf_op jit(solution)/shard_map/ppermute | solution.py:191
  56.0 20.0 %collective-permute-start.10 = (bf16[24,768]{1,0:T(8,128)(2,1)S(1)}, bf16[24,768]{1,0:T(8,128)(2,1)S(1)}, u32[]{:S(2)}, u32[]{:S(2)}) collective-permute-start(bf16[24,768]{1,0:T(8,128)(2,1)S(1)} %get-tuple-element.40), channel_id=1, source_target_pairs={{0,8},{1,9},{2,10},{3,11},{4,12},{5,13},{6,14},{7,15},{8,0},{9,1},... | collective-permute-start | bytes 110600 | tf_op jit(solution)/shard_map/ppermute | solution.py:136
  60.4 15.6 %collective-permute-start.11 = (bf16[24,768]{1,0:T(8,128)(2,1)S(1)}, bf16[24,768]{1,0:T(8,128)(2,1)S(1)}, u32[]{:S(2)}, u32[]{:S(2)}) collective-permute-start(bf16[24,768]{1,0:T(8,128)(2,1)S(1)} %get-tuple-element.40), channel_id=1, source_target_pairs={{0,9},{1,8},{2,11},{3,10},{4,13},{5,12},{6,15},{7,14},{8,1},{9,0},... | collective-permute-start | bytes 110600 | tf_op jit(solution)/shard_map/ppermute | solution.py:136
  66.5 6.8 %collective-permute-start.16 = (bf16[24,768]{1,0:T(8,128)(2,1)S(1)}, bf16[24,768]{1,0:T(8,128)(2,1)S(1)}, u32[]{:S(2)}, u32[]{:S(2)}) collective-permute-start(bf16[24,768]{1,0:T(8,128)(2,1)S(1)} %collective-permute-done.15), channel_id=1, source_target_pairs={{0,2},{1,3},{2,0},{3,1},{4,6},{5,7},{6,4},{7,5},{8,10},{9,11},{10,... | collective-permute-start | bytes 110600 | tf_op jit(solution)/shard_map/ppermute | solution.py:136
  66.5 8.1 %collective-permute-start.17 = (bf16[24,768]{1,0:T(8,128)(2,1)S(1)}, bf16[24,768]{1,0:T(8,128)(2,1)S(1)}, u32[]{:S(2)}, u32[]{:S(2)}) collective-permute-start(bf16[24,768]{1,0:T(8,128)(2,1)S(1)} %collective-permute-done.15), channel_id=1, source_target_pairs={{0,4},{1,5},{2,6},{3,7},{4,0},{5,1},{6,2},{7,3},{8,12},{9,13},{10,... | collective-permute-start | bytes 110600 | tf_op jit(solution)/shard_map/ppermute | solution.py:136
  69.9 6.1 %collective-permute-start.18 = (bf16[24,768]{1,0:T(8,128)(2,1)S(1)}, bf16[24,768]{1,0:T(8,128)(2,1)S(1)}, u32[]{:S(2)}, u32[]{:S(2)}) collective-permute-start(bf16[24,768]{1,0:T(8,128)(2,1)S(1)} %collective-permute-done.15), channel_id=1, source_target_pairs={{0,6},{1,7},{2,4},{3,5},{4,2},{5,3},{6,0},{7,1},{8,14},{9,15},{10,... | collective-permute-start | bytes 110600 | tf_op jit(solution)/shard_map/ppermute | solution.py:136
  73.4 4.0 %collective-permute-start.9 = (bf16[24,768]{1,0:T(8,128)(2,1)S(1)}, bf16[24,768]{1,0:T(8,128)(2,1)S(1)}, u32[]{:S(2)}, u32[]{:S(2)}) collective-permute-start(bf16[24,768]{1,0:T(8,128)(2,1)S(1)} %get-tuple-element.40), channel_id=1, source_target_pairs={{0,1},{1,0},{2,3},{3,2},{4,5},{5,4},{6,7},{7,6},{8,9},{9,8},{10,11... | collective-permute-start | bytes 110600 | tf_op jit(solution)/shard_map/ppermute | solution.py:136
  77.9 9.3 %collective-permute-start.21 = (bf16[120,768]{1,0:T(8,128)(2,1)S(1)}, bf16[120,768]{1,0:T(8,128)(2,1)S(1)}, u32[]{:S(2)}, u32[]{:S(2)}) collective-permute-start(bf16[120,768]{1,0:T(8,128)(2,1)S(1)} %get-tuple-element.51), channel_id=1, source_target_pairs={{0,9},{1,8},{2,11},{3,10},{4,13},{5,12},{6,15},{7,14},{8,1},{9,0},... | collective-permute-start | bytes 552968 | tf_op jit(solution)/shard_map/ppermute | solution.py:136
  78.1 11.0 %collective-permute-start.20 = (bf16[120,768]{1,0:T(8,128)(2,1)S(1)}, bf16[120,768]{1,0:T(8,128)(2,1)S(1)}, u32[]{:S(2)}, u32[]{:S(2)}) collective-permute-start(bf16[120,768]{1,0:T(8,128)(2,1)S(1)} %get-tuple-element.50), channel_id=1, source_target_pairs={{0,8},{1,9},{2,10},{3,11},{4,12},{5,13},{6,14},{7,15},{8,0},{9,1},... | collective-permute-start | bytes 552968 | tf_op jit(solution)/shard_map/ppermute | solution.py:136
  81.2 7.9 %collective-permute-start.19 = (bf16[120,768]{1,0:T(8,128)(2,1)S(1)}, bf16[120,768]{1,0:T(8,128)(2,1)S(1)}, u32[]{:S(2)}, u32[]{:S(2)}) collective-permute-start(bf16[120,768]{1,0:T(8,128)(2,1)S(1)} %get-tuple-element.49), channel_id=1, source_target_pairs={{0,1},{1,0},{2,3},{3,2},{4,5},{5,4},{6,7},{7,6},{8,9},{9,8},{10,11... | collective-permute-start | bytes 552968 | tf_op jit(solution)/shard_map/ppermute | solution.py:136

commit v5 on v4

--- a/solution.py
+++ b/solution.py
@@ -181,7 +181,8 @@
     spins = [lax.dynamic_index_in_dim(tau, member, keepdims=False)] + [part[4 * nrows :] for part in sink[1:]]
     spins = in_place(spins, member)
     source = around(source, MEMBER_BITS)
-    spins = around([spins.reshape(4 * nrows, 2 * nvec)] * 4, QUAD_BITS)
+    spins = spins.reshape(4 * nrows, 2 * nvec)
+    below, above = swap(spins, 2), swap(spins, 6)
     sink = spread(wide_sum([sink[0]] + [part[: 4 * nrows] for part in sink[1:]]), quad)
     source = wide_sum(source)
     source = spread(source, quad)
@@ -189,9 +190,11 @@
     source = wide_sum([source[0]] + [part[:nrows] for part in second[1:]]).astype(jnp.bfloat16)
     sink = wide_sum([sink[0]] + [part[nrows:] for part in second[1:]]).astype(jnp.bfloat16)
     source = lax.ppermute(source, "tm", [(t, 15 - t) for t in range(16)])
-    rows = jnp.concatenate(around([sink] * 4, MEMBER_BITS))
+    across = jnp.concatenate([swap(above[: 2 * nrows], 2), swap(below[2 * nrows :], 6)])
+    rows = jnp.concatenate([sink, swap(sink, 1)])
+    rows = jnp.concatenate([rows, swap(rows, 8)])
     source = in_place(around([source] * 4, QUAD_BITS), quad).reshape(4 * nrows, 2 * nvec)
-    spins = in_place(spins, quad).reshape(4, 4, nrows, 2 * nvec).transpose(1, 0, 2, 3)
+    spins = in_place([spins, below, across, above], quad).reshape(4, 4, nrows, 2 * nvec).transpose(1, 0, 2, 3)
     mixed = jnp.dot(rows, complex_right(by_owner(spins, nrows)), preferred_element_type=jnp.float32)
     mixed = mixed.astype(jnp.bfloat16).reshape(4, nrows, 2 * nvec)
     third = around([None] + [jnp.concatenate([source, mixed[m]]) for m in (1, 2, 3)], MEMBER_BITS)

time: 93.1 us -> 97 us (1.042); the launches traced: 91.6 us -> 96.6 us
  waiting for transfers between devices: 20.6 us -> 30.5 us
  starting transfers between devices: 45.6 us -> 40.7 us
    ppermute x21, waiting for transfers between devices: 19.2 us -> 30.5 us  [swap(): return lax.ppermute(value, 'space', [(i, i ^ bits) for i in range(16)])]
    ppermute x21, starting transfers between devices: 45.5 us -> 40.6 us  [swap(): return lax.ppermute(value, 'space', [(i, i ^ bits) for i in range(16)])]
    ppermute x1, waiting for transfers between devices: 1.41 us -> 0.01 us  [steps(): source = lax.ppermute(source, 'tm', [(t, 15 - t) for t in range(16)])]
  transfers between devices with their start and end apart: 22 -> 22, of which waited for: 10 -> 10; matrix products, arithmetic and copies ran while one was open for 2% -> 2% of each run, Pallas kernels for 11% -> 10%
where the time goes in v5:
time: 97 us; the launch traced here: 96.6 us
  starting transfers between devices  40.7 us (42%)
  waiting for transfers between devices  30.5 us (31%)
  Pallas kernels  19.9 us (21%)
  local copies, waits for them, and re-layouts  3.46 us (4%)
    ppermute x21, starting transfers between devices, swap(): return lax.ppermute(value, 'space', [(i, i ^ bits) for i in range(16)])  40.6 us
    ppermute x21, waiting for transfers between devices, swap(): return lax.ppermute(value, 'space', [(i, i ^ bits) for i in range(16)])  30.5 us
    pallas_call x2, Pallas kernels, gram(): pl.pallas_call(body, in_specs=[pl.BlockSpec(memory_space=pltpu.SMEM), pl....  19.9 us
  transfers between devices with their start and end apart: 22, of which 10 were waited for; matrix products, arithmetic and copies ran while one was open for 2% of the time, Pallas kernels for 10%

profile of v5, /device:TPU:8, one launch (start us, length us, event | category | flops | bytes accessed | tf_op | source)
XLA Modules:
  0.0 96.6 jit_solution(10965175665926635521)
XLA Ops:
  0.0 9.8 %shard_map.38 = (f32[96,768]{1,0:T(8,128)}, bf16[96,768]{1,0:T(8,128)(2,1)}, bf16[96,768]{1,0:T(8,128)(2,1)}, bf16[96,768]{1,0:T(8,128)(2,1)}) custom-call(s32[2,3]{1,0:T(2,128)} %m.1, bf16[1,2,3,1024,384]{4,3,2,1,0:T(8,128)(2,1)} %v.1), custom_call_target="tpu_custom_call" | custom-call | flops 3623878656 | bytes 4718592 | tf_op jit(solution)/shard_map/pallas_call | solution.py:118
  9.8 2.0 %collective-permute-start.3 = (bf16[96,768]{1,0:T(8,128)(2,1)}, bf16[96,768]{1,0:T(8,128)(2,1)S(1)}, u32[]{:S(2)}, u32[]{:S(2)}) collective-permute-start(bf16[96,768]{1,0:T(8,128)(2,1)} %get-tuple-element.18), channel_id=1, source_target_pairs={{0,1},{1,0},{2,3},{3,2},{4,5},{5,4},{6,7},{7,6},{8,9},{9,8},{10,11... | collective-permute-start | bytes 442376 | tf_op jit(solution)/shard_map/ppermute | solution.py:136
  11.8 3.0 %collective-permute-start.4 = (bf16[96,768]{1,0:T(8,128)(2,1)}, bf16[96,768]{1,0:T(8,128)(2,1)S(1)}, u32[]{:S(2)}, u32[]{:S(2)}) collective-permute-start(bf16[96,768]{1,0:T(8,128)(2,1)} %get-tuple-element.19), channel_id=1, source_target_pairs={{0,8},{1,9},{2,10},{3,11},{4,12},{5,13},{6,14},{7,15},{8,0},{9,1},... | collective-permute-start | bytes 442376 | tf_op jit(solution)/shard_map/ppermute | solution.py:136
  14.9 0.1 collective-permute-start.5
  14.9 0.1 copy.15
  15.0 0.8 reshape.51.spin_ref
  15.8 10.0 %shard_map.37 = (f32[96,768]{1,0:T(8,128)}, bf16[120,768]{1,0:T(8,128)(2,1)}, bf16[120,768]{1,0:T(8,128)(2,1)}, bf16[120,768]{1,0:T(8,128)(2,1)}) custom-call(s32[2,3]{1,0:T(2,128)} %m.1, bf16[1,2,3,1024,384]{4,3,2,1,0:T(8,128)(2,1)} %v.1, bf16[4,24,768]{2,1,0:T(8,128)(2,1)} %reshape.51.spin_ref), custom_call_target="tpu_custom_call" | custom-call | flops 3623878656 | bytes 4718592 | tf_op jit(solution)/shard_map/pallas_call | solution.py:118
  25.9 2.0 %collective-permute-start = (bf16[120,768]{1,0:T(8,128)(2,1)}, bf16[120,768]{1,0:T(8,128)(2,1)S(1)}, u32[]{:S(2)}, u32[]{:S(2)}) collective-permute-start(bf16[120,768]{1,0:T(8,128)(2,1)} %get-tuple-element.14), channel_id=1, source_target_pairs={{0,1},{1,0},{2,3},{3,2},{4,5},{5,4},{6,7},{7,6},{8,9},{9,8},{10,11... | collective-permute-start | bytes 552968 | tf_op jit(solution)/shard_map/ppermute | solution.py:136
  27.9 3.0 %collective-permute-start.1 = (bf16[120,768]{1,0:T(8,128)(2,1)}, bf16[120,768]{1,0:T(8,128)(2,1)S(1)}, u32[]{:S(2)}, u32[]{:S(2)}) collective-permute-start(bf16[120,768]{1,0:T(8,128)(2,1)} %get-tuple-element.15), channel_id=1, source_target_pairs={{0,8},{1,9},{2,10},{3,11},{4,12},{5,13},{6,14},{7,15},{8,0},{9,1},... | collective-permute-start | bytes 552968 | tf_op jit(solution)/shard_map/ppermute | solution.py:136
  30.9 0.8 constant_dynamic-slice_fusion.20
  31.7 0.0 collective-permute-done.3
  31.7 0.1 collective-permute-start.2
  31.7 0.0 collective-permute-done.4
  31.7 0.0 collective-permute-done.5
  31.7 0.1 convert_add_fusion
  31.8 0.2 collective-permute-done
  32.0 5.9 %collective-permute-done.1 = bf16[120,768]{1,0:T(8,128)(2,1)S(1)} collective-permute-done((bf16[120,768]{1,0:T(8,128)(2,1)}, bf16[120,768]{1,0:T(8,128)(2,1)S(1)}, u32[]{:S(2)}, u32[]{:S(2)}) %collective-permute-start.1) | collective-permute-done | bytes 184352 | tf_op jit(solution)/shard_map/ppermute | solution.py:136
  37.9 1.9 %collective-permute-done.2 = bf16[120,768]{1,0:T(8,128)(2,1)S(1)} collective-permute-done((bf16[120,768]{1,0:T(8,128)(2,1)}, bf16[120,768]{1,0:T(8,128)(2,1)S(1)}, u32[]{:S(2)}, u32[]{:S(2)}) %collective-permute-start.2) | collective-permute-done | bytes 184352 | tf_op jit(solution)/shard_map/ppermute | solution.py:136
  39.8 0.1 convert_add_fusion.1
  40.0 3.8 %collective-permute-start.6 = (bf16[48,768]{1,0:T(8,128)(2,1)S(1)}, bf16[48,768]{1,0:T(8,128)(2,1)S(1)}, u32[]{:S(2)}, u32[]{:S(2)}) collective-permute-start(bf16[48,768]{1,0:T(8,128)(2,1)S(1)} %pad_maximum_fusion.12), channel_id=1, source_target_pairs={{0,2},{1,3},{2,0},{3,1},{4,6},{5,7},{6,4},{7,5},{8,10},{9,11},{10,... | collective-permute-start | bytes 221192 | tf_op jit(solution)/shard_map/ppermute | solution.py:136
  43.8 4.1 %collective-permute-start.7 = (bf16[48,768]{1,0:T(8,128)(2,1)S(1)}, bf16[48,768]{1,0:T(8,128)(2,1)S(1)}, u32[]{:S(2)}, u32[]{:S(2)}) collective-permute-start(bf16[48,768]{1,0:T(8,128)(2,1)S(1)} %pad_maximum_fusion.13), channel_id=1, source_target_pairs={{0,4},{1,5},{2,6},{3,7},{4,0},{5,1},{6,2},{7,3},{8,12},{9,13},{10,... | collective-permute-start | bytes 221192 | tf_op jit(solution)/shard_map/ppermute | solution.py:136
  47.8 0.0 collective-permute-start.8
  47.9 0.0 collective-permute-done.6
  47.9 4.1 %collective-permute-done.7 = bf16[48,768]{1,0:T(8,128)(2,1)S(1)} collective-permute-done((bf16[48,768]{1,0:T(8,128)(2,1)S(1)}, bf16[48,768]{1,0:T(8,128)(2,1)S(1)}, u32[]{:S(2)}, u32[]{:S(2)}) %collective-permute-start.7) | collective-permute-done | bytes 73760 | tf_op jit(solution)/shard_map/ppermute | solution.py:136
  52.1 2.3 %collective-permute-done.8 = bf16[48,768]{1,0:T(8,128)(2,1)S(1)} collective-permute-done((bf16[48,768]{1,0:T(8,128)(2,1)S(1)}, bf16[48,768]{1,0:T(8,128)(2,1)S(1)}, u32[]{:S(2)}, u32[]{:S(2)}) %collective-permute-start.8) | collective-permute-done | bytes 73760 | tf_op jit(solution)/shard_map/ppermute | solution.py:136
  54.4 0.1 collective-permute-start.15
  54.5 1.8 %collective-permute-start.9 = (bf16[24,768]{1,0:T(8,128)(2,1)S(1)}, bf16[24,768]{1,0:T(8,128)(2,1)S(1)}, u32[]{:S(2)}, u32[]{:S(2)}) collective-permute-start(bf16[24,768]{1,0:T(8,128)(2,1)S(1)} %get-tuple-element.40), channel_id=1, source_target_pairs={{0,1},{1,0},{2,3},{3,2},{4,5},{5,4},{6,7},{7,6},{8,9},{9,8},{10,11... | collective-permute-start | bytes 110600 | tf_op jit(solution)/shard_map/ppermute | solution.py:136
  56.3 1.0 %collective-permute-start.12 = (bf16[96,768]{1,0:T(8,128)(2,1)S(1)}, bf16[96,768]{1,0:T(8,128)(2,1)S(1)}, u32[]{:S(2)}, u32[]{:S(2)}) collective-permute-start(bf16[96,768]{1,0:T(8,128)(2,1)S(1)} %bitcast.105), channel_id=1, source_target_pairs={{0,6},{1,7},{2,4},{3,5},{4,2},{5,3},{6,0},{7,1},{8,14},{9,15},{10,... | collective-permute-start | bytes 442376 | tf_op jit(solution)/shard_map/ppermute | solution.py:136
  57.3 2.2 %collective-permute-start.11 = (bf16[96,768]{1,0:T(8,128)(2,1)S(1)}, bf16[96,768]{1,0:T(8,128)(2,1)S(1)}, u32[]{:S(2)}, u32[]{:S(2)}) collective-permute-start(bf16[96,768]{1,0:T(8,128)(2,1)S(1)} %bitcast.106), channel_id=1, source_target_pairs={{0,2},{1,3},{2,0},{3,1},{4,6},{5,7},{6,4},{7,5},{8,10},{9,11},{10,... | collective-permute-start | bytes 442376 | tf_op jit(solution)/shard_map/ppermute | solution.py:136
  59.5 0.0 collective-permute-done.15
  59.5 1.5 %collective-permute-start.16 = (bf16[24,768]{1,0:T(8,128)(2,1)S(1)}, bf16[24,768]{1,0:T(8,128)(2,1)S(1)}, u32[]{:S(2)}, u32[]{:S(2)}) collective-permute-start(bf16[24,768]{1,0:T(8,128)(2,1)S(1)} %collective-permute-done.15), channel_id=1, source_target_pairs={{0,2},{1,3},{2,0},{3,1},{4,6},{5,7},{6,4},{7,5},{8,10},{9,11},{10,... | collective-permute-start | bytes 110600 | tf_op jit(solution)/shard_map/ppermute | solution.py:136
  60.9 2.7 %collective-permute-start.17 = (bf16[24,768]{1,0:T(8,128)(2,1)S(1)}, bf16[24,768]{1,0:T(8,128)(2,1)S(1)}, u32[]{:S(2)}, u32[]{:S(2)}) collective-permute-start(bf16[24,768]{1,0:T(8,128)(2,1)S(1)} %collective-permute-done.15), channel_id=1, source_target_pairs={{0,4},{1,5},{2,6},{3,7},{4,0},{5,1},{6,2},{7,3},{8,12},{9,13},{10,... | collective-permute-start | bytes 110600 | tf_op jit(solution)/shard_map/ppermute | solution.py:136
  63.7 0.0 collective-permute-done.9
  63.7 2.3 %collective-permute-start.18 = (bf16[24,768]{1,0:T(8,128)(2,1)S(1)}, bf16[24,768]{1,0:T(8,128)(2,1)S(1)}, u32[]{:S(2)}, u32[]{:S(2)}) collective-permute-start(bf16[24,768]{1,0:T(8,128)(2,1)S(1)} %collective-permute-done.15), channel_id=1, source_target_pairs={{0,6},{1,7},{2,4},{3,5},{4,2},{5,3},{6,0},{7,1},{8,14},{9,15},{10,... | collective-permute-start | bytes 110600 | tf_op jit(solution)/shard_map/ppermute | solution.py:136
  66.0 1.7 %collective-permute-done.12 = bf16[96,768]{1,0:T(8,128)(2,1)S(1)} collective-permute-done((bf16[96,768]{1,0:T(8,128)(2,1)S(1)}, bf16[96,768]{1,0:T(8,128)(2,1)S(1)}, u32[]{:S(2)}, u32[]{:S(2)}) %collective-permute-start.12) | collective-permute-done | bytes 147488 | tf_op jit(solution)/shard_map/ppermute | solution.py:136
  67.7 0.4 collective-permute-start.10
  68.1 0.0 collective-permute-done.16
  68.1 2.9 %collective-permute-start.13 = (bf16[48,768]{1,0:T(8,128)(2,1)S(1)}, bf16[48,768]{1,0:T(8,128)(2,1)S(1)}, u32[]{:S(2)}, u32[]{:S(2)}) collective-permute-start(bf16[48,768]{1,0:T(8,128)(2,1)S(1)} %slice.128), channel_id=1, source_target_pairs={{0,2},{1,3},{2,0},{3,1},{4,6},{5,7},{6,4},{7,5},{8,10},{9,11},{10,... | collective-permute-start | bytes 221192 | tf_op jit(solution)/shard_map/ppermute | solution.py:136
  71.0 1.4 %collective-permute-done.17 = bf16[24,768]{1,0:T(8,128)(2,1)S(1)} collective-permute-done((bf16[24,768]{1,0:T(8,128)(2,1)S(1)}, bf16[24,768]{1,0:T(8,128)(2,1)S(1)}, u32[]{:S(2)}, u32[]{:S(2)}) %collective-permute-start.17) | collective-permute-done | bytes 36896 | tf_op jit(solution)/shard_map/ppermute | solution.py:136
  72.3 0.0 collective-permute-done.18
  72.4 0.0 collective-permute-done.11
  72.4 2.9 %collective-permute-start.14 = (bf16[48,768]{1,0:T(8,128)(2,1)S(1)}, bf16[48,768]{1,0:T(8,128)(2,1)S(1)}, u32[]{:S(2)}, u32[]{:S(2)}) collective-permute-start(bf16[48,768]{1,0:T(8,128)(2,1)S(1)} %slice.129), channel_id=1, source_target_pairs={{0,6},{1,7},{2,4},{3,5},{4,2},{5,3},{6,0},{7,1},{8,14},{9,15},{10,... | collective-permute-start | bytes 221192 | tf_op jit(solution)/shard_map/ppermute | solution.py:136
  75.3 0.0 collective-permute-done.13
  75.3 5.1 %collective-permute-done.14 = bf16[48,768]{1,0:T(8,128)(2,1)S(1)} collective-permute-done((bf16[48,768]{1,0:T(8,128)(2,1)S(1)}, bf16[48,768]{1,0:T(8,128)(2,1)S(1)}, u32[]{:S(2)}, u32[]{:S(2)}) %collective-permute-start.14) | collective-permute-done | bytes 73760 | tf_op jit(solution)/shard_map/ppermute | solution.py:136
  80.4 0.1 pad_maximum_fusion
  80.5 0.1 constant_dynamic-slice_fusion.15
  80.6 0.1 pad_maximum_fusion.1
  80.7 0.1 slice_negate_fusion.1
  80.8 0.0 collective-permute-done.10
  80.8 0.3 fusion.6
  81.2 2.6 %collective-permute-start.21 = (bf16[120,768]{1,0:T(8,128)(2,1)S(1)}, bf16[120,768]{1,0:T(8,128)(2,1)S(1)}, u32[]{:S(2)}, u32[]{:S(2)}) collective-permute-start(bf16[120,768]{1,0:T(8,128)(2,1)S(1)} %get-tuple-element.51), channel_id=1, source_target_pairs={{0,9},{1,8},{2,11},{3,10},{4,13},{5,12},{6,15},{7,14},{8,1},{9,0},... | collective-permute-start | bytes 552968 | tf_op jit(solution)/shard_map/ppermute | solution.py:136
  83.7 0.5 collective-permute-start.20
  84.2 2.1 %collective-permute-start.19 = (bf16[120,768]{1,0:T(8,128)(2,1)S(1)}, bf16[120,768]{1,0:T(8,128)(2,1)S(1)}, u32[]{:S(2)}, u32[]{:S(2)}) collective-permute-start(bf16[120,768]{1,0:T(8,128)(2,1)S(1)} %get-tuple-element.49), channel_id=1, source_target_pairs={{0,1},{1,0},{2,3},{3,2},{4,5},{5,4},{6,7},{7,6},{8,9},{9,8},{10,11... | collective-permute-start | bytes 552968 | tf_op jit(solution)/shard_map/ppermute | solution.py:136
  86.3 5.0 %collective-permute-done.21 = bf16[120,768]{1,0:T(8,128)(2,1)S(1)} collective-permute-done((bf16[120,768]{1,0:T(8,128)(2,1)S(1)}, bf16[120,768]{1,0:T(8,128)(2,1)S(1)}, u32[]{:S(2)}, u32[]{:S(2)}) %collective-permute-start.21) | collective-permute-done | bytes 184352 | tf_op jit(solution)/shard_map/ppermute | solution.py:136
  91.2 2.9 %collective-permute-done.20 = bf16[120,768]{1,0:T(8,128)(2,1)S(1)} collective-permute-done((bf16[120,768]{1,0:T(8,128)(2,1)S(1)}, bf16[120,768]{1,0:T(8,128)(2,1)S(1)}, u32[]{:S(2)}, u32[]{:S(2)}) %collective-permute-start.20) | collective-permute-done | bytes 184352 | tf_op jit(solution)/shard_map/ppermute | solution.py:136
  94.1 0.0 collective-permute-done.19
  94.2 0.1 pad_maximum_fusion.2
  94.3 0.1 constant_dynamic-slice_fusion.3
  94.4 0.1 pad_maximum_fusion.3
  94.5 0.1 slice_negate_fusion
  94.6 0.1 maximum_bitcast_fusion
  94.7 0.6 copy.19
  95.3 0.5 fusion.9
  95.8 0.8 copy.20
  (36 shorter events, 0.5 us)
Async XLA Ops:
  0.0 14.9 %copy-start.2 = (bf16[1,2,24,4,384]{4,3,2,1,0:T(4,128)(2,1)S(1)}, bf16[1,2,24,4,384]{4,3,2,1,0:T(4,128)(2,1)}, u32[]{:S(2)}) copy-start(bf16[1,2,24,4,384]{4,3,2,1,0:T(4,128)(2,1)} %param.5) | copy-start | bytes 442372
  9.8 21.8 %collective-permute-start.3 = (bf16[96,768]{1,0:T(8,128)(2,1)}, bf16[96,768]{1,0:T(8,128)(2,1)S(1)}, u32[]{:S(2)}, u32[]{:S(2)}) collective-permute-start(bf16[96,768]{1,0:T(8,128)(2,1)} %get-tuple-element.18), channel_id=1, source_target_pairs={{0,1},{1,0},{2,3},{3,2},{4,5},{5,4},{6,7},{7,6},{8,9},{9,8},{10,11... | collective-permute-start | bytes 442376 | tf_op jit(solution)/shard_map/ppermute | solution.py:136
  11.8 19.9 %collective-permute-start.4 = (bf16[96,768]{1,0:T(8,128)(2,1)}, bf16[96,768]{1,0:T(8,128)(2,1)S(1)}, u32[]{:S(2)}, u32[]{:S(2)}) collective-permute-start(bf16[96,768]{1,0:T(8,128)(2,1)} %get-tuple-element.19), channel_id=1, source_target_pairs={{0,8},{1,9},{2,10},{3,11},{4,12},{5,13},{6,14},{7,15},{8,0},{9,1},... | collective-permute-start | bytes 442376 | tf_op jit(solution)/shard_map/ppermute | solution.py:136
  14.9 16.9 %collective-permute-start.5 = (bf16[96,768]{1,0:T(8,128)(2,1)}, bf16[96,768]{1,0:T(8,128)(2,1)S(1)}, u32[]{:S(2)}, u32[]{:S(2)}) collective-permute-start(bf16[96,768]{1,0:T(8,128)(2,1)} %get-tuple-element.20), channel_id=1, source_target_pairs={{0,9},{1,8},{2,11},{3,10},{4,13},{5,12},{6,15},{7,14},{8,1},{9,0},... | collective-permute-start | bytes 442376 | tf_op jit(solution)/shard_map/ppermute | solution.py:136
  15.8 15.9 %copy-start = (f32[96,768]{1,0:T(8,128)S(1)}, f32[96,768]{1,0:T(8,128)}, u32[]{:S(2)}) copy-start(f32[96,768]{1,0:T(8,128)} %get-tuple-element.17) | copy-start | bytes 884740
  25.9 14.0 %copy-start.1 = (f32[96,768]{1,0:T(8,128)S(1)}, f32[96,768]{1,0:T(8,128)}, u32[]{:S(2)}) copy-start(f32[96,768]{1,0:T(8,128)} %get-tuple-element.13) | copy-start | bytes 884740
  25.9 6.2 %collective-permute-start = (bf16[120,768]{1,0:T(8,128)(2,1)}, bf16[120,768]{1,0:T(8,128)(2,1)S(1)}, u32[]{:S(2)}, u32[]{:S(2)}) collective-permute-start(bf16[120,768]{1,0:T(8,128)(2,1)} %get-tuple-element.14), channel_id=1, source_target_pairs={{0,1},{1,0},{2,3},{3,2},{4,5},{5,4},{6,7},{7,6},{8,9},{9,8},{10,11... | collective-permute-start | bytes 552968 | tf_op jit(solution)/shard_map/ppermute | solution.py:136
  27.9 10.1 %collective-permute-start.1 = (bf16[120,768]{1,0:T(8,128)(2,1)}, bf16[120,768]{1,0:T(8,128)(2,1)S(1)}, u32[]{:S(2)}, u32[]{:S(2)}) collective-permute-start(bf16[120,768]{1,0:T(8,128)(2,1)} %get-tuple-element.15), channel_id=1, source_target_pairs={{0,8},{1,9},{2,10},{3,11},{4,12},{5,13},{6,14},{7,15},{8,0},{9,1},... | collective-permute-start | bytes 552968 | tf_op jit(solution)/shard_map/ppermute | solution.py:136
  31.7 8.2 %collective-permute-start.2 = (bf16[120,768]{1,0:T(8,128)(2,1)}, bf16[120,768]{1,0:T(8,128)(2,1)S(1)}, u32[]{:S(2)}, u32[]{:S(2)}) collective-permute-start(bf16[120,768]{1,0:T(8,128)(2,1)} %get-tuple-element.16), channel_id=1, source_target_pairs={{0,9},{1,8},{2,11},{3,10},{4,13},{5,12},{6,15},{7,14},{8,1},{9,0},... | collective-permute-start | bytes 552968 | tf_op jit(solution)/shard_map/ppermute | solution.py:136
  40.0 8.0 %collective-permute-start.6 = (bf16[48,768]{1,0:T(8,128)(2,1)S(1)}, bf16[48,768]{1,0:T(8,128)(2,1)S(1)}, u32[]{:S(2)}, u32[]{:S(2)}) collective-permute-start(bf16[48,768]{1,0:T(8,128)(2,1)S(1)} %pad_maximum_fusion.12), channel_id=1, source_target_pairs={{0,2},{1,3},{2,0},{3,1},{4,6},{5,7},{6,4},{7,5},{8,10},{9,11},{10,... | collective-permute-start | bytes 221192 | tf_op jit(solution)/shard_map/ppermute | solution.py:136
  43.8 8.3 %collective-permute-start.7 = (bf16[48,768]{1,0:T(8,128)(2,1)S(1)}, bf16[48,768]{1,0:T(8,128)(2,1)S(1)}, u32[]{:S(2)}, u32[]{:S(2)}) collective-permute-start(bf16[48,768]{1,0:T(8,128)(2,1)S(1)} %pad_maximum_fusion.13), channel_id=1, source_target_pairs={{0,4},{1,5},{2,6},{3,7},{4,0},{5,1},{6,2},{7,3},{8,12},{9,13},{10,... | collective-permute-start | bytes 221192 | tf_op jit(solution)/shard_map/ppermute | solution.py:136
  47.8 6.6 %collective-permute-start.8 = (bf16[48,768]{1,0:T(8,128)(2,1)S(1)}, bf16[48,768]{1,0:T(8,128)(2,1)S(1)}, u32[]{:S(2)}, u32[]{:S(2)}) collective-permute-start(bf16[48,768]{1,0:T(8,128)(2,1)S(1)} %pad_maximum_fusion.14), channel_id=1, source_target_pairs={{0,6},{1,7},{2,4},{3,5},{4,2},{5,3},{6,0},{7,1},{8,14},{9,15},{10,... | collective-permute-start | bytes 221192 | tf_op jit(solution)/shard_map/ppermute | solution.py:136
  54.4 5.0 %collective-permute-start.15 = (bf16[24,768]{1,0:T(8,128)(2,1)S(1)}, bf16[24,768]{1,0:T(8,128)(2,1)S(1)}, u32[]{:S(2)}, u32[]{:S(2)}) collective-permute-start(bf16[24,768]{1,0:T(8,128)(2,1)S(1)} %get-tuple-element.39), channel_id=1, source_target_pairs={{0,240},{16,224},{32,208},{48,192},{64,176},{80,160},{96,144},{112... | collective-permute-start | bytes 110600 | tf_op jit(solution)/shard_map/ppermute | solution.py:192
  54.5 9.2 %collective-permute-start.9 = (bf16[24,768]{1,0:T(8,128)(2,1)S(1)}, bf16[24,768]{1,0:T(8,128)(2,1)S(1)}, u32[]{:S(2)}, u32[]{:S(2)}) collective-permute-start(bf16[24,768]{1,0:T(8,128)(2,1)S(1)} %get-tuple-element.40), channel_id=1, source_target_pairs={{0,1},{1,0},{2,3},{3,2},{4,5},{5,4},{6,7},{7,6},{8,9},{9,8},{10,11... | collective-permute-start | bytes 110600 | tf_op jit(solution)/shard_map/ppermute | solution.py:136
  56.3 11.4 %collective-permute-start.12 = (bf16[96,768]{1,0:T(8,128)(2,1)S(1)}, bf16[96,768]{1,0:T(8,128)(2,1)S(1)}, u32[]{:S(2)}, u32[]{:S(2)}) collective-permute-start(bf16[96,768]{1,0:T(8,128)(2,1)S(1)} %bitcast.105), channel_id=1, source_target_pairs={{0,6},{1,7},{2,4},{3,5},{4,2},{5,3},{6,0},{7,1},{8,14},{9,15},{10,... | collective-permute-start | bytes 442376 | tf_op jit(solution)/shard_map/ppermute | solution.py:136
  57.3 15.1 %collective-permute-start.11 = (bf16[96,768]{1,0:T(8,128)(2,1)S(1)}, bf16[96,768]{1,0:T(8,128)(2,1)S(1)}, u32[]{:S(2)}, u32[]{:S(2)}) collective-permute-start(bf16[96,768]{1,0:T(8,128)(2,1)S(1)} %bitcast.106), channel_id=1, source_target_pairs={{0,2},{1,3},{2,0},{3,1},{4,6},{5,7},{6,4},{7,5},{8,10},{9,11},{10,... | collective-permute-start | bytes 442376 | tf_op jit(solution)/shard_map/ppermute | solution.py:136
  59.5 8.6 %collective-permute-start.16 = (bf16[24,768]{1,0:T(8,128)(2,1)S(1)}, bf16[24,768]{1,0:T(8,128)(2,1)S(1)}, u32[]{:S(2)}, u32[]{:S(2)}) collective-permute-start(bf16[24,768]{1,0:T(8,128)(2,1)S(1)} %collective-permute-done.15), channel_id=1, source_target_pairs={{0,2},{1,3},{2,0},{3,1},{4,6},{5,7},{6,4},{7,5},{8,10},{9,11},{10,... | collective-permute-start | bytes 110600 | tf_op jit(solution)/shard_map/ppermute | solution.py:136
  60.9 11.4 %collective-permute-start.17 = (bf16[24,768]{1,0:T(8,128)(2,1)S(1)}, bf16[24,768]{1,0:T(8,128)(2,1)S(1)}, u32[]{:S(2)}, u32[]{:S(2)}) collective-permute-start(bf16[24,768]{1,0:T(8,128)(2,1)S(1)} %collective-permute-done.15), channel_id=1, source_target_pairs={{0,4},{1,5},{2,6},{3,7},{4,0},{5,1},{6,2},{7,3},{8,12},{9,13},{10,... | collective-permute-start | bytes 110600 | tf_op jit(solution)/shard_map/ppermute | solution.py:136
  63.7 8.6 %collective-permute-start.18 = (bf16[24,768]{1,0:T(8,128)(2,1)S(1)}, bf16[24,768]{1,0:T(8,128)(2,1)S(1)}, u32[]{:S(2)}, u32[]{:S(2)}) collective-permute-start(bf16[24,768]{1,0:T(8,128)(2,1)S(1)} %collective-permute-done.15), channel_id=1, source_target_pairs={{0,6},{1,7},{2,4},{3,5},{4,2},{5,3},{6,0},{7,1},{8,14},{9,15},{10,... | collective-permute-start | bytes 110600 | tf_op jit(solution)/shard_map/ppermute | solution.py:136
  67.7 13.1 %collective-permute-start.10 = (bf16[48,768]{1,0:T(8,128)(2,1)S(1)}, bf16[48,768]{1,0:T(8,128)(2,1)S(1)}, u32[]{:S(2)}, u32[]{:S(2)}) collective-permute-start(bf16[48,768]{1,0:T(8,128)(2,1)S(1)} %pad_maximum_fusion.15), channel_id=1, source_target_pairs={{0,8},{1,9},{2,10},{3,11},{4,12},{5,13},{6,14},{7,15},{8,0},{9,1},... | collective-permute-start | bytes 221192 | tf_op jit(solution)/shard_map/ppermute | solution.py:136
  68.1 7.2 %collective-permute-start.13 = (bf16[48,768]{1,0:T(8,128)(2,1)S(1)}, bf16[48,768]{1,0:T(8,128)(2,1)S(1)}, u32[]{:S(2)}, u32[]{:S(2)}) collective-permute-start(bf16[48,768]{1,0:T(8,128)(2,1)S(1)} %slice.128), channel_id=1, source_target_pairs={{0,2},{1,3},{2,0},{3,1},{4,6},{5,7},{6,4},{7,5},{8,10},{9,11},{10,... | collective-permute-start | bytes 221192 | tf_op jit(solution)/shard_map/ppermute | solution.py:136
  72.4 8.0 %collective-permute-start.14 = (bf16[48,768]{1,0:T(8,128)(2,1)S(1)}, bf16[48,768]{1,0:T(8,128)(2,1)S(1)}, u32[]{:S(2)}, u32[]{:S(2)}) collective-permute-start(bf16[48,768]{1,0:T(8,128)(2,1)S(1)} %slice.129), channel_id=1, source_target_pairs={{0,6},{1,7},{2,4},{3,5},{4,2},{5,3},{6,0},{7,1},{8,14},{9,15},{10,... | collective-permute-start | bytes 221192 | tf_op jit(solution)/shard_map/ppermute | solution.py:136
  81.2 10.0 %collective-permute-start.21 = (bf16[120,768]{1,0:T(8,128)(2,1)S(1)}, bf16[120,768]{1,0:T(8,128)(2,1)S(1)}, u32[]{:S(2)}, u32[]{:S(2)}) collective-permute-start(bf16[120,768]{1,0:T(8,128)(2,1)S(1)} %get-tuple-element.51), channel_id=1, source_target_pairs={{0,9},{1,8},{2,11},{3,10},{4,13},{5,12},{6,15},{7,14},{8,1},{9,0},... | collective-permute-start | bytes 552968 | tf_op jit(solution)/shard_map/ppermute | solution.py:136
  83.7 10.4 %collective-permute-start.20 = (bf16[120,768]{1,0:T(8,128)(2,1)S(1)}, bf16[120,768]{1,0:T(8,128)(2,1)S(1)}, u32[]{:S(2)}, u32[]{:S(2)}) collective-permute-start(bf16[120,768]{1,0:T(8,128)(2,1)S(1)} %get-tuple-element.50), channel_id=1, source_target_pairs={{0,8},{1,9},{2,10},{3,11},{4,12},{5,13},{6,14},{7,15},{8,0},{9,1},... | collective-permute-start | bytes 552968 | tf_op jit(solution)/shard_map/ppermute | solution.py:136
  84.2 9.9 %collective-permute-start.19 = (bf16[120,768]{1,0:T(8,128)(2,1)S(1)}, bf16[120,768]{1,0:T(8,128)(2,1)S(1)}, u32[]{:S(2)}, u32[]{:S(2)}) collective-permute-start(bf16[120,768]{1,0:T(8,128)(2,1)S(1)} %get-tuple-element.49), channel_id=1, source_target_pairs={{0,1},{1,0},{2,3},{3,2},{4,5},{5,4},{6,7},{7,6},{8,9},{9,8},{10,11... | collective-permute-start | bytes 552968 | tf_op jit(solution)/shard_map/ppermute | solution.py:136

commit v6 on v5

--- a/solution.py
+++ b/solution.py
@@ -31,18 +31,17 @@
     return cos_out, sin_out
 
 
-def gram_kernel(which, chunks, momenta, vec_ref, spin_ref, keep_ref, *refs):
+def gram_kernel(which, sizes, momenta, vec_ref, spin_ref, keep_ref, *refs):
     send_refs = refs[:3]
-    vec_buf, y_ref, left0, left1, right0, right1, acc_ref, sems = refs[3:]
-    left = (left0, left1)
+    vec_buf, y_ref, right0, right1, acc_ref, sems = refs[3:]
     right = (right0, right1)
-    _, _, colors, sites, nvec = vec_ref.shape
-    depth = sites // chunks
-    rows_y = depth // LAT
+    _, parts, colors, _, nvec = vec_ref.shape
+    chunks = len(sizes)
+    starts = [sum(sizes[:i]) for i in range(chunks)]
 
     def fetch(step):
-        return pltpu.make_async_copy(
-            vec_ref.at[0, :, :, pl.ds(step * depth, depth), :], vec_buf.at[step], sems.at[step])
+        at = pl.ds(starts[step], sizes[step])
+        return pltpu.make_async_copy(vec_ref.at[0, :, :, at, :], vec_buf.at[:, :, at, :], sems.at[step])
 
     for step in range(chunks):
         fetch(step).start()
@@ -55,8 +54,11 @@
 
     def prepare(step):
         fetch(step).wait()
-        for y in range(rows_y):
-            at_y = step * rows_y + y
+        out = right[step % 2]
+        depth = sizes[step]
+        half = colors * depth
+        for y in range(depth // LAT):
+            at_y = starts[step] // LAT + y
             cos_row = jnp.broadcast_to(y_ref[0, at_y : at_y + 1], (LAT, LANES))
             sin_row = jnp.broadcast_to(y_ref[1, at_y : at_y + 1], (LAT, LANES))
             cosine = cos_x * cos_row - sin_x * sin_row
@@ -64,26 +66,35 @@
             cosine = jnp.concatenate([cosine] * (nvec // LANES), axis=1)
             sine = jnp.concatenate([sine] * (nvec // LANES), axis=1)
             for color in range(colors):
-                re = vec_buf[step, 0, color, y * LAT : (y + 1) * LAT]
-                im = vec_buf[step, 1, color, y * LAT : (y + 1) * LAT]
-                re32 = re.astype(jnp.float32)
-                im32 = im.astype(jnp.float32)
-                at = pl.ds(color * depth + y * LAT, LAT)
-                right[step % 2][at, :nvec] = (cosine * re32 + sine * im32).astype(jnp.bfloat16)
-                right[step % 2][at, nvec:] = (cosine * im32 - sine * re32).astype(jnp.bfloat16)
-                left[step % 2][at, :nvec] = re
-                left[step % 2][at, nvec:] = im
+                re32 = vec_buf[0, color, at_y * LAT : (at_y + 1) * LAT].astype(jnp.float32)
+                im32 = vec_buf[1, color, at_y * LAT : (at_y + 1) * LAT].astype(jnp.float32)
+                at = color * depth + y * LAT
+                real = (cosine * re32 + sine * im32).astype(jnp.bfloat16)
+                imag = (cosine * im32 - sine * re32).astype(jnp.bfloat16)
+                out[at : at + LAT, :nvec] = real
+                out[at : at + LAT, nvec:] = imag
+                out[half + at : half + at + LAT, :nvec] = imag
+                out[half + at : half + at + LAT, nvec:] = -real
+
+    def multiply(step):
+        depth = sizes[step]
+        half = colors * depth
+        for p in range(parts):
+            left = vec_buf[p, :, starts[step] : starts[step] + depth, :].reshape(half, nvec)
+            term = lax.dot_general(
+                left,
+                right[step % 2][p * half : (p + 1) * half, :],
+                (((0,), (0,)), ((), ())),
+                preferred_element_type=jnp.float32,
+            )
+            at = pl.ds(p * nvec, nvec)
+            acc_ref[at, :] = term if step == 0 else acc_ref[at, :] + term
 
     prepare(0)
     for step in range(chunks):
         if step + 1 < chunks:
             prepare(step + 1)
-        part = lax.dot_general(left[step % 2][...], right[step % 2][...], (((0,), (0,)), ((), ())),
-                               preferred_element_type=jnp.float32)
-        if step == 0:
-            acc_ref[...] = part
-        else:
-            acc_ref[...] += part
+        multiply(step)
     rows = nvec // 16
     here = space // 8 * 2 + space % 2
     for member, out_ref in enumerate((keep_ref, *send_refs)):
@@ -91,43 +102,41 @@
         for quad in range(4):
             owner = (target & 9) | (2 * quad)
             start = pl.multiple_of(owner * rows, 8)
-            real = pl.ds(start, rows)
-            imag = pl.ds(pl.multiple_of(start + nvec, 8), rows)
-            at = pl.ds(quad * rows, rows)
-            out_ref[at, :nvec] = (acc_ref[real, :nvec] + acc_ref[imag, nvec:]).astype(out_ref.dtype)
-            out_ref[at, nvec:] = (acc_ref[real, nvec:] - acc_ref[imag, :nvec]).astype(out_ref.dtype)
+            value = acc_ref[pl.ds(start, rows), :] + acc_ref[pl.ds(pl.multiple_of(start + nvec, 8), rows), :]
+            out_ref[pl.ds(quad * rows, rows), :] = value.astype(out_ref.dtype)
         if spin_ref is not None and member:
             out_ref[pl.ds(4 * rows, rows), :] = spin_ref[here ^ member]
 
 
-def gram(eigvec, momenta, which, spins=None, chunks=4):
+def gram(eigvec, momenta, which, spins=None, sizes=(128, 256, 256, 256, 128)):
     _, _, colors, sites, nvec = eigvec.shape
-    depth = sites // chunks
+    depth = max(sizes)
+    chunks = len(sizes)
     rows = nvec // 4
     extra = 0 if spins is None else spins.shape[1]
     outs = [((rows, 2 * nvec), jnp.float32)] + [((rows + extra, 2 * nvec), jnp.bfloat16)] * 3
     vmem = pl.BlockSpec(memory_space=pltpu.VMEM)
-    kern = functools.partial(gram_kernel, which, chunks)
+    kern = functools.partial(gram_kernel, which, sizes)
     if spins is None:
         body = lambda m, v, *r: kern(m, v, None, *r)
         ins = ()
     else:
         body = kern
         ins = (spins,)
-    operand = pltpu.VMEM((colors * depth, 2 * nvec), jnp.bfloat16)
+    operand = pltpu.VMEM((2 * colors * depth, 2 * nvec), jnp.bfloat16)
     return pl.pallas_call(
         body,
-        in_specs=[pl.BlockSpec(memory_space=pltpu.SMEM), pl.BlockSpec(memory_space=pl.ANY)] + [vmem] * len(ins),
+        in_specs=[pl.BlockSpec(memory_space=pltpu.SMEM), pl.BlockSpec(memory_space=pltpu.HBM)] + [vmem] * len(ins),
         out_specs=[vmem] * 4,
         scratch_shapes=[
-            pltpu.VMEM((chunks, 2, colors, depth, nvec), jnp.bfloat16),
+            pltpu.VMEM((2, colors, sites, nvec), jnp.bfloat16),
             pltpu.VMEM((2, LAT, LANES), jnp.float32),
-            operand, operand, operand, operand,
+            operand, operand,
             pltpu.VMEM((2 * nvec, 2 * nvec), jnp.float32),
             pltpu.SemaphoreType.DMA((chunks,)),
         ],
         out_shape=[jax.ShapeDtypeStruct(shape, kind) for shape, kind in outs],
-        compiler_params=pltpu.CompilerParams(vmem_limit_bytes=62 << 20),
+        compiler_params=pltpu.CompilerParams(vmem_limit_bytes=51 << 20),
         cost_estimate=pl.CostEstimate(flops=8 * nvec * nvec * colors * sites, bytes_accessed=eigvec.size * 2, transcendentals=0),
     )(momenta, eigvec, *ins)
 
@@ -202,7 +211,8 @@
     mixed = mixed.transpose(1, 0, 2).reshape(nrows * SPIN, 2 * nvec)
     source = in_place([source] + [part[: 4 * nrows] for part in third[1:]], member)
     dressed = jnp.dot(mixed, complex_right(by_owner(source, nrows)), preferred_element_type=jnp.float32)
-    return dressed.reshape(1, nrows, SPIN, 2, nvec).astype(jnp.bfloat16)
+    dressed = lax.optimization_barrier(dressed.astype(jnp.bfloat16))
+    return dressed.reshape(1, nrows, SPIN, 2, nvec)
 
 
 def solution(mesh):

time: 97 us -> 89.2 us (0.920)
  Pallas kernels: 19.9 us -> 14.3 us
  waiting for transfers between devices: 30.5 us -> 27.4 us
  starting transfers between devices: 40.7 us -> 42.7 us
  local copies, waits for them, and re-layouts: 3.46 us -> 2.09 us
    pallas_call x2, Pallas kernels: 19.9 us -> 14.3 us  [gram(): pl.pallas_call(body, in_specs=[pl.BlockSpec(memory_space=pltpu.SMEM), pl....]
    ppermute x21, waiting for transfers between devices: 30.5 us -> 27.4 us  [swap(): return lax.ppermute(value, 'space', [(i, i ^ bits) for i in range(16)])]
    ppermute x21, starting transfers between devices: 40.6 us -> 42.6 us  [swap(): return lax.ppermute(value, 'space', [(i, i ^ bits) for i in range(16)])]
  transfers between devices with their start and end apart: 22 -> 22, of which waited for: 10 -> 9; matrix products, arithmetic and copies ran while one was open for 2% -> 1% of each run, Pallas kernels for 10% -> 8%
where the time goes in v6:
time: 89.2 us; the launch traced here: 88.4 us
  starting transfers between devices  42.7 us (48%)
  waiting for transfers between devices  27.4 us (31%)
  Pallas kernels  14.3 us (16%)
  local copies, waits for them, and re-layouts  2.09 us (2%)
    ppermute x21, starting transfers between devices, swap(): return lax.ppermute(value, 'space', [(i, i ^ bits) for i in range(16)])  42.6 us
    ppermute x21, waiting for transfers between devices, swap(): return lax.ppermute(value, 'space', [(i, i ^ bits) for i in range(16)])  27.4 us
    pallas_call x2, Pallas kernels, gram(): pl.pallas_call(body, in_specs=[pl.BlockSpec(memory_space=pltpu.SMEM), pl....  14.3 us
  transfers between devices with their start and end apart: 22, of which 9 were waited for; matrix products, arithmetic and copies ran while one was open for 1% of the time, Pallas kernels for 8%

profile of v6, /device:TPU:8, one launch (start us, length us, event | category | flops | bytes accessed | tf_op | source)
XLA Modules:
  0.0 88.4 jit_solution(8910307786313423216)
XLA Ops:
  0.0 0.7 copy-done
  0.7 7.2 %shard_map.38 = (f32[96,768]{1,0:T(8,128)S(1)}, bf16[96,768]{1,0:T(8,128)(2,1)S(1)}, bf16[96,768]{1,0:T(8,128)(2,1)S(1)}, bf16[96,768]{1,0:T(8,128)(2,1)S(1)}) custom-call(s32[2,3]{1,0:T(2,128)S(1)} %copy-done, bf16[1,2,3,1024,384]{4,3,2,1,0:T(8,128)(2,1)} %v.1), custom_call_target="tpu_custom_call" | custom-call | flops 3623878656 | bytes 4718592 | tf_op jit(solution)/shard_map/pallas_call | solution.py:127
  7.8 2.0 %collective-permute-start.3 = (bf16[96,768]{1,0:T(8,128)(2,1)S(1)}, bf16[96,768]{1,0:T(8,128)(2,1)S(1)}, u32[]{:S(2)}, u32[]{:S(2)}) collective-permute-start(bf16[96,768]{1,0:T(8,128)(2,1)S(1)} %get-tuple-element.18), channel_id=1, source_target_pairs={{0,1},{1,0},{2,3},{3,2},{4,5},{5,4},{6,7},{7,6},{8,9},{9,8},{10,11... | collective-permute-start | bytes 442376 | tf_op jit(solution)/shard_map/ppermute | solution.py:145
  9.8 3.0 %collective-permute-start.4 = (bf16[96,768]{1,0:T(8,128)(2,1)S(1)}, bf16[96,768]{1,0:T(8,128)(2,1)S(1)}, u32[]{:S(2)}, u32[]{:S(2)}) collective-permute-start(bf16[96,768]{1,0:T(8,128)(2,1)S(1)} %get-tuple-element.19), channel_id=1, source_target_pairs={{0,8},{1,9},{2,10},{3,11},{4,12},{5,13},{6,14},{7,15},{8,0},{9,1},... | collective-permute-start | bytes 442376 | tf_op jit(solution)/shard_map/ppermute | solution.py:145
  12.9 0.1 collective-permute-start.5
  12.9 0.0 copy-done.2
  12.9 0.1 copy.12
  13.0 0.1 reshape.50.spin_ref
  13.2 7.2 %shard_map.37 = (f32[96,768]{1,0:T(8,128)S(1)}, bf16[120,768]{1,0:T(8,128)(2,1)S(1)}, bf16[120,768]{1,0:T(8,128)(2,1)S(1)}, bf16[120,768]{1,0:T(8,128)(2,1)S(1)}) custom-call(s32[2,3]{1,0:T(2,128)S(1)} %copy-done.1, bf16[1,2,3,1024,384]{4,3,2,1,0:T(8,128)(2,1)} %v.1, bf16[4,24,768]{2,1,0:T(8,128)(2,1)S(1)} %reshape.50.spin_ref), custom_call_target="tpu_custom_call" | custom-call | flops 3623878656 | bytes 4718592 | tf_op jit(solution)/shard_map/pallas_call | solution.py:127
  20.3 2.0 %collective-permute-start = (bf16[120,768]{1,0:T(8,128)(2,1)S(1)}, bf16[120,768]{1,0:T(8,128)(2,1)S(1)}, u32[]{:S(2)}, u32[]{:S(2)}) collective-permute-start(bf16[120,768]{1,0:T(8,128)(2,1)S(1)} %get-tuple-element.14), channel_id=1, source_target_pairs={{0,1},{1,0},{2,3},{3,2},{4,5},{5,4},{6,7},{7,6},{8,9},{9,8},{10,11... | collective-permute-start | bytes 552968 | tf_op jit(solution)/shard_map/ppermute | solution.py:145
  22.3 3.0 %collective-permute-start.1 = (bf16[120,768]{1,0:T(8,128)(2,1)S(1)}, bf16[120,768]{1,0:T(8,128)(2,1)S(1)}, u32[]{:S(2)}, u32[]{:S(2)}) collective-permute-start(bf16[120,768]{1,0:T(8,128)(2,1)S(1)} %get-tuple-element.15), channel_id=1, source_target_pairs={{0,8},{1,9},{2,10},{3,11},{4,12},{5,13},{6,14},{7,15},{8,0},{9,1},... | collective-permute-start | bytes 552968 | tf_op jit(solution)/shard_map/ppermute | solution.py:145
  25.4 0.0 collective-permute-done.3
  25.4 0.2 collective-permute-start.2
  25.6 0.0 collective-permute-done.4
  25.6 0.0 collective-permute-done.5
  25.6 0.1 convert_add_fusion
  25.7 0.7 collective-permute-done
  26.3 5.8 %collective-permute-done.1 = bf16[120,768]{1,0:T(8,128)(2,1)S(1)} collective-permute-done((bf16[120,768]{1,0:T(8,128)(2,1)S(1)}, bf16[120,768]{1,0:T(8,128)(2,1)S(1)}, u32[]{:S(2)}, u32[]{:S(2)}) %collective-permute-start.1) | collective-permute-done | bytes 184352 | tf_op jit(solution)/shard_map/ppermute | solution.py:145
  32.1 1.3 %collective-permute-done.2 = bf16[120,768]{1,0:T(8,128)(2,1)S(1)} collective-permute-done((bf16[120,768]{1,0:T(8,128)(2,1)S(1)}, bf16[120,768]{1,0:T(8,128)(2,1)S(1)}, u32[]{:S(2)}, u32[]{:S(2)}) %collective-permute-start.2) | collective-permute-done | bytes 184352 | tf_op jit(solution)/shard_map/ppermute | solution.py:145
  33.3 0.1 convert_add_fusion.1
  33.5 3.4 %collective-permute-start.6 = (bf16[48,768]{1,0:T(8,128)(2,1)S(1)}, bf16[48,768]{1,0:T(8,128)(2,1)S(1)}, u32[]{:S(2)}, u32[]{:S(2)}) collective-permute-start(bf16[48,768]{1,0:T(8,128)(2,1)S(1)} %pad_maximum_fusion.12), channel_id=1, source_target_pairs={{0,2},{1,3},{2,0},{3,1},{4,6},{5,7},{6,4},{7,5},{8,10},{9,11},{10,... | collective-permute-start | bytes 221192 | tf_op jit(solution)/shard_map/ppermute | solution.py:145
  36.8 4.5 %collective-permute-start.7 = (bf16[48,768]{1,0:T(8,128)(2,1)S(1)}, bf16[48,768]{1,0:T(8,128)(2,1)S(1)}, u32[]{:S(2)}, u32[]{:S(2)}) collective-permute-start(bf16[48,768]{1,0:T(8,128)(2,1)S(1)} %pad_maximum_fusion.13), channel_id=1, source_target_pairs={{0,4},{1,5},{2,6},{3,7},{4,0},{5,1},{6,2},{7,3},{8,12},{9,13},{10,... | collective-permute-start | bytes 221192 | tf_op jit(solution)/shard_map/ppermute | solution.py:145
  41.4 0.0 collective-permute-start.8
  41.5 0.0 collective-permute-done.6
  41.5 4.1 %collective-permute-done.7 = bf16[48,768]{1,0:T(8,128)(2,1)S(1)} collective-permute-done((bf16[48,768]{1,0:T(8,128)(2,1)S(1)}, bf16[48,768]{1,0:T(8,128)(2,1)S(1)}, u32[]{:S(2)}, u32[]{:S(2)}) %collective-permute-start.7) | collective-permute-done | bytes 73760 | tf_op jit(solution)/shard_map/ppermute | solution.py:145
  45.6 2.4 %collective-permute-done.8 = bf16[48,768]{1,0:T(8,128)(2,1)S(1)} collective-permute-done((bf16[48,768]{1,0:T(8,128)(2,1)S(1)}, bf16[48,768]{1,0:T(8,128)(2,1)S(1)}, u32[]{:S(2)}, u32[]{:S(2)}) %collective-permute-start.8) | collective-permute-done | bytes 73760 | tf_op jit(solution)/shard_map/ppermute | solution.py:145
  48.0 0.1 collective-permute-start.15
  48.1 1.8 %collective-permute-start.9 = (bf16[24,768]{1,0:T(8,128)(2,1)S(1)}, bf16[24,768]{1,0:T(8,128)(2,1)S(1)}, u32[]{:S(2)}, u32[]{:S(2)}) collective-permute-start(bf16[24,768]{1,0:T(8,128)(2,1)S(1)} %get-tuple-element.40), channel_id=1, source_target_pairs={{0,1},{1,0},{2,3},{3,2},{4,5},{5,4},{6,7},{7,6},{8,9},{9,8},{10,11... | collective-permute-start | bytes 110600 | tf_op jit(solution)/shard_map/ppermute | solution.py:145
  49.9 1.1 %collective-permute-start.12 = (bf16[96,768]{1,0:T(8,128)(2,1)S(1)}, bf16[96,768]{1,0:T(8,128)(2,1)S(1)}, u32[]{:S(2)}, u32[]{:S(2)}) collective-permute-start(bf16[96,768]{1,0:T(8,128)(2,1)S(1)} %bitcast.92), channel_id=1, source_target_pairs={{0,6},{1,7},{2,4},{3,5},{4,2},{5,3},{6,0},{7,1},{8,14},{9,15},{10,... | collective-permute-start | bytes 442376 | tf_op jit(solution)/shard_map/ppermute | solution.py:145
  51.0 2.5 %collective-permute-start.11 = (bf16[96,768]{1,0:T(8,128)(2,1)S(1)}, bf16[96,768]{1,0:T(8,128)(2,1)S(1)}, u32[]{:S(2)}, u32[]{:S(2)}) collective-permute-start(bf16[96,768]{1,0:T(8,128)(2,1)S(1)} %bitcast.93), channel_id=1, source_target_pairs={{0,2},{1,3},{2,0},{3,1},{4,6},{5,7},{6,4},{7,5},{8,10},{9,11},{10,... | collective-permute-start | bytes 442376 | tf_op jit(solution)/shard_map/ppermute | solution.py:145
  53.4 0.0 collective-permute-done.15
  53.5 1.3 %collective-permute-start.16 = (bf16[24,768]{1,0:T(8,128)(2,1)S(1)}, bf16[24,768]{1,0:T(8,128)(2,1)S(1)}, u32[]{:S(2)}, u32[]{:S(2)}) collective-permute-start(bf16[24,768]{1,0:T(8,128)(2,1)S(1)} %collective-permute-done.15), channel_id=1, source_target_pairs={{0,2},{1,3},{2,0},{3,1},{4,6},{5,7},{6,4},{7,5},{8,10},{9,11},{10,... | collective-permute-start | bytes 110600 | tf_op jit(solution)/shard_map/ppermute | solution.py:145
  54.8 2.5 %collective-permute-start.17 = (bf16[24,768]{1,0:T(8,128)(2,1)S(1)}, bf16[24,768]{1,0:T(8,128)(2,1)S(1)}, u32[]{:S(2)}, u32[]{:S(2)}) collective-permute-start(bf16[24,768]{1,0:T(8,128)(2,1)S(1)} %collective-permute-done.15), channel_id=1, source_target_pairs={{0,4},{1,5},{2,6},{3,7},{4,0},{5,1},{6,2},{7,3},{8,12},{9,13},{10,... | collective-permute-start | bytes 110600 | tf_op jit(solution)/shard_map/ppermute | solution.py:145
  57.3 0.0 collective-permute-done.9
  57.3 2.7 %collective-permute-start.18 = (bf16[24,768]{1,0:T(8,128)(2,1)S(1)}, bf16[24,768]{1,0:T(8,128)(2,1)S(1)}, u32[]{:S(2)}, u32[]{:S(2)}) collective-permute-start(bf16[24,768]{1,0:T(8,128)(2,1)S(1)} %collective-permute-done.15), channel_id=1, source_target_pairs={{0,6},{1,7},{2,4},{3,5},{4,2},{5,3},{6,0},{7,1},{8,14},{9,15},{10,... | collective-permute-start | bytes 110600 | tf_op jit(solution)/shard_map/ppermute | solution.py:145
  60.0 0.0 collective-permute-done.12
  60.0 2.6 %collective-permute-start.10 = (bf16[48,768]{1,0:T(8,128)(2,1)S(1)}, bf16[48,768]{1,0:T(8,128)(2,1)S(1)}, u32[]{:S(2)}, u32[]{:S(2)}) collective-permute-start(bf16[48,768]{1,0:T(8,128)(2,1)S(1)} %pad_maximum_fusion.15), channel_id=1, source_target_pairs={{0,8},{1,9},{2,10},{3,11},{4,12},{5,13},{6,14},{7,15},{8,0},{9,1},... | collective-permute-start | bytes 221192 | tf_op jit(solution)/shard_map/ppermute | solution.py:145
  62.5 0.0 collective-permute-done.16
  62.6 1.6 %collective-permute-start.13 = (bf16[48,768]{1,0:T(8,128)(2,1)S(1)}, bf16[48,768]{1,0:T(8,128)(2,1)S(1)}, u32[]{:S(2)}, u32[]{:S(2)}) collective-permute-start(bf16[48,768]{1,0:T(8,128)(2,1)S(1)} %slice.128), channel_id=1, source_target_pairs={{0,2},{1,3},{2,0},{3,1},{4,6},{5,7},{6,4},{7,5},{8,10},{9,11},{10,... | collective-permute-start | bytes 221192 | tf_op jit(solution)/shard_map/ppermute | solution.py:145
  64.2 0.0 collective-permute-done.17
  64.2 0.0 collective-permute-done.18
  64.3 0.0 collective-permute-done.11
  64.3 3.3 %collective-permute-start.14 = (bf16[48,768]{1,0:T(8,128)(2,1)S(1)}, bf16[48,768]{1,0:T(8,128)(2,1)S(1)}, u32[]{:S(2)}, u32[]{:S(2)}) collective-permute-start(bf16[48,768]{1,0:T(8,128)(2,1)S(1)} %slice.129), channel_id=1, source_target_pairs={{0,6},{1,7},{2,4},{3,5},{4,2},{5,3},{6,0},{7,1},{8,14},{9,15},{10,... | collective-permute-start | bytes 221192 | tf_op jit(solution)/shard_map/ppermute | solution.py:145
  67.6 2.0 %collective-permute-done.13 = bf16[48,768]{1,0:T(8,128)(2,1)S(1)} collective-permute-done((bf16[48,768]{1,0:T(8,128)(2,1)S(1)}, bf16[48,768]{1,0:T(8,128)(2,1)S(1)}, u32[]{:S(2)}, u32[]{:S(2)}) %collective-permute-start.13) | collective-permute-done | bytes 73760 | tf_op jit(solution)/shard_map/ppermute | solution.py:145
  69.6 3.5 %collective-permute-done.14 = bf16[48,768]{1,0:T(8,128)(2,1)S(1)} collective-permute-done((bf16[48,768]{1,0:T(8,128)(2,1)S(1)}, bf16[48,768]{1,0:T(8,128)(2,1)S(1)}, u32[]{:S(2)}, u32[]{:S(2)}) %collective-permute-start.14) | collective-permute-done | bytes 73760 | tf_op jit(solution)/shard_map/ppermute | solution.py:145
  73.1 0.1 pad_maximum_fusion
  73.2 0.1 constant_dynamic-slice_fusion.15
  73.3 0.1 pad_maximum_fusion.1
  73.4 0.1 slice_negate_fusion.1
  73.5 0.0 collective-permute-done.10
  73.5 0.3 fusion.15
  73.9 3.5 %collective-permute-start.21 = (bf16[120,768]{1,0:T(8,128)(2,1)S(1)}, bf16[120,768]{1,0:T(8,128)(2,1)S(1)}, u32[]{:S(2)}, u32[]{:S(2)}) collective-permute-start(bf16[120,768]{1,0:T(8,128)(2,1)S(1)} %get-tuple-element.51), channel_id=1, source_target_pairs={{0,9},{1,8},{2,11},{3,10},{4,13},{5,12},{6,15},{7,14},{8,1},{9,0},... | collective-permute-start | bytes 552968 | tf_op jit(solution)/shard_map/ppermute | solution.py:145
  77.4 1.5 %collective-permute-start.20 = (bf16[120,768]{1,0:T(8,128)(2,1)S(1)}, bf16[120,768]{1,0:T(8,128)(2,1)S(1)}, u32[]{:S(2)}, u32[]{:S(2)}) collective-permute-start(bf16[120,768]{1,0:T(8,128)(2,1)S(1)} %get-tuple-element.50), channel_id=1, source_target_pairs={{0,8},{1,9},{2,10},{3,11},{4,12},{5,13},{6,14},{7,15},{8,0},{9,1},... | collective-permute-start | bytes 552968 | tf_op jit(solution)/shard_map/ppermute | solution.py:145
  78.8 0.1 collective-permute-start.19
  79.0 5.0 %collective-permute-done.21 = bf16[120,768]{1,0:T(8,128)(2,1)S(1)} collective-permute-done((bf16[120,768]{1,0:T(8,128)(2,1)S(1)}, bf16[120,768]{1,0:T(8,128)(2,1)S(1)}, u32[]{:S(2)}, u32[]{:S(2)}) %collective-permute-start.21) | collective-permute-done | bytes 184352 | tf_op jit(solution)/shard_map/ppermute | solution.py:145
  83.9 2.8 %collective-permute-done.20 = bf16[120,768]{1,0:T(8,128)(2,1)S(1)} collective-permute-done((bf16[120,768]{1,0:T(8,128)(2,1)S(1)}, bf16[120,768]{1,0:T(8,128)(2,1)S(1)}, u32[]{:S(2)}, u32[]{:S(2)}) %collective-permute-start.20) | collective-permute-done | bytes 184352 | tf_op jit(solution)/shard_map/ppermute | solution.py:145
  86.8 0.0 collective-permute-done.19
  86.8 0.1 pad_maximum_fusion.2
  86.9 0.1 constant_dynamic-slice_fusion.3
  86.9 0.1 pad_maximum_fusion.3
  87.1 0.1 slice_negate_fusion
  87.3 0.1 copy.15
  87.4 0.3 fusion.12
  87.7 0.7 reshape.61
  (37 shorter events, 0.6 us)
Async XLA Ops:
  0.0 0.7 copy-start
  0.7 12.3 %copy-start.2 = (bf16[1,2,24,4,384]{4,3,2,1,0:T(4,128)(2,1)S(1)}, bf16[1,2,24,4,384]{4,3,2,1,0:T(4,128)(2,1)}, u32[]{:S(2)}) copy-start(bf16[1,2,24,4,384]{4,3,2,1,0:T(4,128)(2,1)} %param.5) | copy-start | bytes 442372
  0.7 12.5 %copy-start.1 = (s32[2,3]{1,0:T(2,128)S(1)}, s32[2,3]{1,0:T(2,128)}, u32[]{:S(2)}) copy-start(s32[2,3]{1,0:T(2,128)} %m.1) | copy-start | bytes 76
  7.8 17.5 %collective-permute-start.3 = (bf16[96,768]{1,0:T(8,128)(2,1)S(1)}, bf16[96,768]{1,0:T(8,128)(2,1)S(1)}, u32[]{:S(2)}, u32[]{:S(2)}) collective-permute-start(bf16[96,768]{1,0:T(8,128)(2,1)S(1)} %get-tuple-element.18), channel_id=1, source_target_pairs={{0,1},{1,0},{2,3},{3,2},{4,5},{5,4},{6,7},{7,6},{8,9},{9,8},{10,11... | collective-permute-start | bytes 442376 | tf_op jit(solution)/shard_map/ppermute | solution.py:145
  9.8 15.7 %collective-permute-start.4 = (bf16[96,768]{1,0:T(8,128)(2,1)S(1)}, bf16[96,768]{1,0:T(8,128)(2,1)S(1)}, u32[]{:S(2)}, u32[]{:S(2)}) collective-permute-start(bf16[96,768]{1,0:T(8,128)(2,1)S(1)} %get-tuple-element.19), channel_id=1, source_target_pairs={{0,8},{1,9},{2,10},{3,11},{4,12},{5,13},{6,14},{7,15},{8,0},{9,1},... | collective-permute-start | bytes 442376 | tf_op jit(solution)/shard_map/ppermute | solution.py:145
  12.9 12.7 %collective-permute-start.5 = (bf16[96,768]{1,0:T(8,128)(2,1)S(1)}, bf16[96,768]{1,0:T(8,128)(2,1)S(1)}, u32[]{:S(2)}, u32[]{:S(2)}) collective-permute-start(bf16[96,768]{1,0:T(8,128)(2,1)S(1)} %get-tuple-element.20), channel_id=1, source_target_pairs={{0,9},{1,8},{2,11},{3,10},{4,13},{5,12},{6,15},{7,14},{8,1},{9,0},... | collective-permute-start | bytes 442376 | tf_op jit(solution)/shard_map/ppermute | solution.py:145
  20.3 6.0 %collective-permute-start = (bf16[120,768]{1,0:T(8,128)(2,1)S(1)}, bf16[120,768]{1,0:T(8,128)(2,1)S(1)}, u32[]{:S(2)}, u32[]{:S(2)}) collective-permute-start(bf16[120,768]{1,0:T(8,128)(2,1)S(1)} %get-tuple-element.14), channel_id=1, source_target_pairs={{0,1},{1,0},{2,3},{3,2},{4,5},{5,4},{6,7},{7,6},{8,9},{9,8},{10,11... | collective-permute-start | bytes 552968 | tf_op jit(solution)/shard_map/ppermute | solution.py:145
  22.3 9.7 %collective-permute-start.1 = (bf16[120,768]{1,0:T(8,128)(2,1)S(1)}, bf16[120,768]{1,0:T(8,128)(2,1)S(1)}, u32[]{:S(2)}, u32[]{:S(2)}) collective-permute-start(bf16[120,768]{1,0:T(8,128)(2,1)S(1)} %get-tuple-element.15), channel_id=1, source_target_pairs={{0,8},{1,9},{2,10},{3,11},{4,12},{5,13},{6,14},{7,15},{8,0},{9,1},... | collective-permute-start | bytes 552968 | tf_op jit(solution)/shard_map/ppermute | solution.py:145
  25.4 8.0 %collective-permute-start.2 = (bf16[120,768]{1,0:T(8,128)(2,1)S(1)}, bf16[120,768]{1,0:T(8,128)(2,1)S(1)}, u32[]{:S(2)}, u32[]{:S(2)}) collective-permute-start(bf16[120,768]{1,0:T(8,128)(2,1)S(1)} %get-tuple-element.16), channel_id=1, source_target_pairs={{0,9},{1,8},{2,11},{3,10},{4,13},{5,12},{6,15},{7,14},{8,1},{9,0},... | collective-permute-start | bytes 552968 | tf_op jit(solution)/shard_map/ppermute | solution.py:145
  33.5 8.0 %collective-permute-start.6 = (bf16[48,768]{1,0:T(8,128)(2,1)S(1)}, bf16[48,768]{1,0:T(8,128)(2,1)S(1)}, u32[]{:S(2)}, u32[]{:S(2)}) collective-permute-start(bf16[48,768]{1,0:T(8,128)(2,1)S(1)} %pad_maximum_fusion.12), channel_id=1, source_target_pairs={{0,2},{1,3},{2,0},{3,1},{4,6},{5,7},{6,4},{7,5},{8,10},{9,11},{10,... | collective-permute-start | bytes 221192 | tf_op jit(solution)/shard_map/ppermute | solution.py:145
  36.8 8.7 %collective-permute-start.7 = (bf16[48,768]{1,0:T(8,128)(2,1)S(1)}, bf16[48,768]{1,0:T(8,128)(2,1)S(1)}, u32[]{:S(2)}, u32[]{:S(2)}) collective-permute-start(bf16[48,768]{1,0:T(8,128)(2,1)S(1)} %pad_maximum_fusion.13), channel_id=1, source_target_pairs={{0,4},{1,5},{2,6},{3,7},{4,0},{5,1},{6,2},{7,3},{8,12},{9,13},{10,... | collective-permute-start | bytes 221192 | tf_op jit(solution)/shard_map/ppermute | solution.py:145
  41.4 6.6 %collective-permute-start.8 = (bf16[48,768]{1,0:T(8,128)(2,1)S(1)}, bf16[48,768]{1,0:T(8,128)(2,1)S(1)}, u32[]{:S(2)}, u32[]{:S(2)}) collective-permute-start(bf16[48,768]{1,0:T(8,128)(2,1)S(1)} %pad_maximum_fusion.14), channel_id=1, source_target_pairs={{0,6},{1,7},{2,4},{3,5},{4,2},{5,3},{6,0},{7,1},{8,14},{9,15},{10,... | collective-permute-start | bytes 221192 | tf_op jit(solution)/shard_map/ppermute | solution.py:145
  48.0 5.5 %collective-permute-start.15 = (bf16[24,768]{1,0:T(8,128)(2,1)S(1)}, bf16[24,768]{1,0:T(8,128)(2,1)S(1)}, u32[]{:S(2)}, u32[]{:S(2)}) collective-permute-start(bf16[24,768]{1,0:T(8,128)(2,1)S(1)} %get-tuple-element.39), channel_id=1, source_target_pairs={{0,240},{16,224},{32,208},{48,192},{64,176},{80,160},{96,144},{112... | collective-permute-start | bytes 110600 | tf_op jit(solution)/shard_map/ppermute | solution.py:201
  48.1 9.2 %collective-permute-start.9 = (bf16[24,768]{1,0:T(8,128)(2,1)S(1)}, bf16[24,768]{1,0:T(8,128)(2,1)S(1)}, u32[]{:S(2)}, u32[]{:S(2)}) collective-permute-start(bf16[24,768]{1,0:T(8,128)(2,1)S(1)} %get-tuple-element.40), channel_id=1, source_target_pairs={{0,1},{1,0},{2,3},{3,2},{4,5},{5,4},{6,7},{7,6},{8,9},{9,8},{10,11... | collective-permute-start | bytes 110600 | tf_op jit(solution)/shard_map/ppermute | solution.py:145
  49.9 10.1 %collective-permute-start.12 = (bf16[96,768]{1,0:T(8,128)(2,1)S(1)}, bf16[96,768]{1,0:T(8,128)(2,1)S(1)}, u32[]{:S(2)}, u32[]{:S(2)}) collective-permute-start(bf16[96,768]{1,0:T(8,128)(2,1)S(1)} %bitcast.92), channel_id=1, source_target_pairs={{0,6},{1,7},{2,4},{3,5},{4,2},{5,3},{6,0},{7,1},{8,14},{9,15},{10,... | collective-permute-start | bytes 442376 | tf_op jit(solution)/shard_map/ppermute | solution.py:145
  51.0 13.3 %collective-permute-start.11 = (bf16[96,768]{1,0:T(8,128)(2,1)S(1)}, bf16[96,768]{1,0:T(8,128)(2,1)S(1)}, u32[]{:S(2)}, u32[]{:S(2)}) collective-permute-start(bf16[96,768]{1,0:T(8,128)(2,1)S(1)} %bitcast.93), channel_id=1, source_target_pairs={{0,2},{1,3},{2,0},{3,1},{4,6},{5,7},{6,4},{7,5},{8,10},{9,11},{10,... | collective-permute-start | bytes 442376 | tf_op jit(solution)/shard_map/ppermute | solution.py:145
  53.5 9.1 %collective-permute-start.16 = (bf16[24,768]{1,0:T(8,128)(2,1)S(1)}, bf16[24,768]{1,0:T(8,128)(2,1)S(1)}, u32[]{:S(2)}, u32[]{:S(2)}) collective-permute-start(bf16[24,768]{1,0:T(8,128)(2,1)S(1)} %collective-permute-done.15), channel_id=1, source_target_pairs={{0,2},{1,3},{2,0},{3,1},{4,6},{5,7},{6,4},{7,5},{8,10},{9,11},{10,... | collective-permute-start | bytes 110600 | tf_op jit(solution)/shard_map/ppermute | solution.py:145
  54.8 9.4 %collective-permute-start.17 = (bf16[24,768]{1,0:T(8,128)(2,1)S(1)}, bf16[24,768]{1,0:T(8,128)(2,1)S(1)}, u32[]{:S(2)}, u32[]{:S(2)}) collective-permute-start(bf16[24,768]{1,0:T(8,128)(2,1)S(1)} %collective-permute-done.15), channel_id=1, source_target_pairs={{0,4},{1,5},{2,6},{3,7},{4,0},{5,1},{6,2},{7,3},{8,12},{9,13},{10,... | collective-permute-start | bytes 110600 | tf_op jit(solution)/shard_map/ppermute | solution.py:145
  57.3 6.9 %collective-permute-start.18 = (bf16[24,768]{1,0:T(8,128)(2,1)S(1)}, bf16[24,768]{1,0:T(8,128)(2,1)S(1)}, u32[]{:S(2)}, u32[]{:S(2)}) collective-permute-start(bf16[24,768]{1,0:T(8,128)(2,1)S(1)} %collective-permute-done.15), channel_id=1, source_target_pairs={{0,6},{1,7},{2,4},{3,5},{4,2},{5,3},{6,0},{7,1},{8,14},{9,15},{10,... | collective-permute-start | bytes 110600 | tf_op jit(solution)/shard_map/ppermute | solution.py:145
  60.0 13.5 %collective-permute-start.10 = (bf16[48,768]{1,0:T(8,128)(2,1)S(1)}, bf16[48,768]{1,0:T(8,128)(2,1)S(1)}, u32[]{:S(2)}, u32[]{:S(2)}) collective-permute-start(bf16[48,768]{1,0:T(8,128)(2,1)S(1)} %pad_maximum_fusion.15), channel_id=1, source_target_pairs={{0,8},{1,9},{2,10},{3,11},{4,12},{5,13},{6,14},{7,15},{8,0},{9,1},... | collective-permute-start | bytes 221192 | tf_op jit(solution)/shard_map/ppermute | solution.py:145
  62.6 7.1 %collective-permute-start.13 = (bf16[48,768]{1,0:T(8,128)(2,1)S(1)}, bf16[48,768]{1,0:T(8,128)(2,1)S(1)}, u32[]{:S(2)}, u32[]{:S(2)}) collective-permute-start(bf16[48,768]{1,0:T(8,128)(2,1)S(1)} %slice.128), channel_id=1, source_target_pairs={{0,2},{1,3},{2,0},{3,1},{4,6},{5,7},{6,4},{7,5},{8,10},{9,11},{10,... | collective-permute-start | bytes 221192 | tf_op jit(solution)/shard_map/ppermute | solution.py:145
  64.3 8.8 %collective-permute-start.14 = (bf16[48,768]{1,0:T(8,128)(2,1)S(1)}, bf16[48,768]{1,0:T(8,128)(2,1)S(1)}, u32[]{:S(2)}, u32[]{:S(2)}) collective-permute-start(bf16[48,768]{1,0:T(8,128)(2,1)S(1)} %slice.129), channel_id=1, source_target_pairs={{0,6},{1,7},{2,4},{3,5},{4,2},{5,3},{6,0},{7,1},{8,14},{9,15},{10,... | collective-permute-start | bytes 221192 | tf_op jit(solution)/shard_map/ppermute | solution.py:145
  73.9 10.0 %collective-permute-start.21 = (bf16[120,768]{1,0:T(8,128)(2,1)S(1)}, bf16[120,768]{1,0:T(8,128)(2,1)S(1)}, u32[]{:S(2)}, u32[]{:S(2)}) collective-permute-start(bf16[120,768]{1,0:T(8,128)(2,1)S(1)} %get-tuple-element.51), channel_id=1, source_target_pairs={{0,9},{1,8},{2,11},{3,10},{4,13},{5,12},{6,15},{7,14},{8,1},{9,0},... | collective-permute-start | bytes 552968 | tf_op jit(solution)/shard_map/ppermute | solution.py:145
  77.4 9.4 %collective-permute-start.20 = (bf16[120,768]{1,0:T(8,128)(2,1)S(1)}, bf16[120,768]{1,0:T(8,128)(2,1)S(1)}, u32[]{:S(2)}, u32[]{:S(2)}) collective-permute-start(bf16[120,768]{1,0:T(8,128)(2,1)S(1)} %get-tuple-element.50), channel_id=1, source_target_pairs={{0,8},{1,9},{2,10},{3,11},{4,12},{5,13},{6,14},{7,15},{8,0},{9,1},... | collective-permute-start | bytes 552968 | tf_op jit(solution)/shard_map/ppermute | solution.py:145
  78.8 7.9 %collective-permute-start.19 = (bf16[120,768]{1,0:T(8,128)(2,1)S(1)}, bf16[120,768]{1,0:T(8,128)(2,1)S(1)}, u32[]{:S(2)}, u32[]{:S(2)}) collective-permute-start(bf16[120,768]{1,0:T(8,128)(2,1)S(1)} %get-tuple-element.49), channel_id=1, source_target_pairs={{0,1},{1,0},{2,3},{3,2},{4,5},{5,4},{6,7},{7,6},{8,9},{9,8},{10,11... | collective-permute-start | bytes 552968 | tf_op jit(solution)/shard_map/ppermute | solution.py:145

commit v7 on v6

--- a/solution.py
+++ b/solution.py
@@ -13,7 +13,6 @@
 LANES = 128
 SPIN = 4
 MEMBER_BITS = (0, 1, 8, 9)
-QUAD_BITS = (0, 2, 4, 6)
 
 
 def phase_of(winding):
@@ -79,17 +78,26 @@
     def multiply(step):
         depth = sizes[step]
         half = colors * depth
-        for p in range(parts):
-            left = vec_buf[p, :, starts[step] : starts[step] + depth, :].reshape(half, nvec)
+        if half % 256:
+            left = vec_buf[:, :, starts[step] : starts[step] + depth, :].reshape(parts * half, nvec)
+            spans = [(left, 0, parts * half, step % parts)]
+        else:
+            spans = [
+                (vec_buf[p, :, starts[step] : starts[step] + depth, :].reshape(half, nvec), p * half, half, p)
+                for p in range(parts)
+            ]
+        for left, start, length, slot in spans:
             term = lax.dot_general(
                 left,
-                right[step % 2][p * half : (p + 1) * half, :],
+                right[step % 2][start : start + length, :],
                 (((0,), (0,)), ((), ())),
                 preferred_element_type=jnp.float32,
             )
-            at = pl.ds(p * nvec, nvec)
-            acc_ref[at, :] = term if step == 0 else acc_ref[at, :] + term
-
+            at = pl.ds(slot * nvec, nvec)
+            acc_ref[at, :] = acc_ref[at, :] + term if slot in filled else term
+            filled.add(slot)
+
+    filled = set()
     prepare(0)
     for step in range(chunks):
         if step + 1 < chunks:
@@ -108,7 +116,7 @@
             out_ref[pl.ds(4 * rows, rows), :] = spin_ref[here ^ member]
 
 
-def gram(eigvec, momenta, which, spins=None, sizes=(128, 256, 256, 256, 128)):
+def gram(eigvec, momenta, which, spins=None, sizes=(128, 128, 256, 256, 256)):
     _, _, colors, sites, nvec = eigvec.shape
     depth = max(sizes)
     chunks = len(sizes)
@@ -138,7 +146,7 @@
         out_shape=[jax.ShapeDtypeStruct(shape, kind) for shape, kind in outs],
         compiler_params=pltpu.CompilerParams(vmem_limit_bytes=51 << 20),
         cost_estimate=pl.CostEstimate(flops=8 * nvec * nvec * colors * sites, bytes_accessed=eigvec.size * 2, transcendentals=0),
-    )(momenta, eigvec, *ins)
+    )(pltpu.with_memory_space_constraint(momenta, pltpu.HBM), eigvec, *ins)
 
 
 def swap(value, bits):
@@ -164,8 +172,7 @@
 def spread(total, here):
     rows = total.shape[0] // 4
     total = total.reshape(4, rows, total.shape[1])
-    parts = [lax.dynamic_index_in_dim(total, here ^ m, keepdims=False) for m in range(4)]
-    return parts[:1] + [part.astype(jnp.bfloat16) for part in parts[1:]]
+    return [lax.dynamic_index_in_dim(total, here ^ m, keepdims=False) for m in range(4)]
 
 
 def complex_right(value):
@@ -195,14 +202,22 @@
     sink = spread(wide_sum([sink[0]] + [part[: 4 * nrows] for part in sink[1:]]), quad)
     source = wide_sum(source)
     source = spread(source, quad)
-    second = around([None] + [jnp.concatenate([source[m], sink[m]]) for m in (1, 2, 3)], QUAD_BITS)
-    source = wide_sum([source[0]] + [part[:nrows] for part in second[1:]]).astype(jnp.bfloat16)
-    sink = wide_sum([sink[0]] + [part[nrows:] for part in second[1:]]).astype(jnp.bfloat16)
+    left = swap(source[2].astype(jnp.bfloat16), 2)
+    right = swap(sink[2].astype(jnp.bfloat16), 6)
+    left = wide_sum([source[3], left])
+    right = wide_sum([sink[1], right])
+    to_left = jnp.concatenate([source[1], right]).astype(jnp.bfloat16)
+    to_right = jnp.concatenate([left, sink[3]]).astype(jnp.bfloat16)
+    second = [swap(to_left, 2), swap(to_right, 6)]
+    source = wide_sum([source[0]] + [part[:nrows] for part in second]).astype(jnp.bfloat16)
+    sink = wide_sum([sink[0]] + [part[nrows:] for part in second]).astype(jnp.bfloat16)
     source = lax.ppermute(source, "tm", [(t, 15 - t) for t in range(16)])
     across = jnp.concatenate([swap(above[: 2 * nrows], 2), swap(below[2 * nrows :], 6)])
     rows = jnp.concatenate([sink, swap(sink, 1)])
     rows = jnp.concatenate([rows, swap(rows, 8)])
-    source = in_place(around([source] * 4, QUAD_BITS), quad).reshape(4 * nrows, 2 * nvec)
+    left, right = swap(source, 2), swap(source, 6)
+    opposite = jnp.concatenate([swap(right[:16], 2), swap(left[16:], 6)])
+    source = in_place([source, left, opposite, right], quad).reshape(4 * nrows, 2 * nvec)
     spins = in_place([spins, below, across, above], quad).reshape(4, 4, nrows, 2 * nvec).transpose(1, 0, 2, 3)
     mixed = jnp.dot(rows, complex_right(by_owner(spins, nrows)), preferred_element_type=jnp.float32)
     mixed = mixed.astype(jnp.bfloat16).reshape(4, nrows, 2 * nvec)

time: 89.2 us -> 90 us (level)
  starting transfers between devices: 42.7 us -> 47.9 us
  waiting for transfers between devices: 27.4 us -> 23.5 us
    ppermute x21 -> x23, waiting for transfers between devices: 27.4 us -> 22.2 us  [swap(): return lax.ppermute(value, 'space', [(i, i ^ bits) for i in range(16)])]
    ppermute x21 -> x23, starting transfers between devices: 42.6 us -> 47.8 us  [swap(): return lax.ppermute(value, 'space', [(i, i ^ bits) for i in range(16)])]
    ppermute x1, waiting for transfers between devices: 0.01 us -> 1.34 us  [steps(): source = lax.ppermute(source, 'tm', [(t, 15 - t) for t in range(16)])]
  transfers between devices with their start and end apart: 22 -> 24, of which waited for: 9 -> 10; matrix products, arithmetic and copies ran while one was open for 1% -> 1% of each run, Pallas kernels for 8% -> 8%
where the time goes in v7:
time: 90 us; the launch traced here: 88.8 us
  starting transfers between devices  47.9 us (53%)
  waiting for transfers between devices  23.5 us (26%)
  Pallas kernels  14.1 us (16%)
  local copies, waits for them, and re-layouts  1.41 us (2%)
    ppermute x23, starting transfers between devices, swap(): return lax.ppermute(value, 'space', [(i, i ^ bits) for i in range(16)])  47.8 us
    ppermute x23, waiting for transfers between devices, swap(): return lax.ppermute(value, 'space', [(i, i ^ bits) for i in range(16)])  22.2 us
    pallas_call x2, Pallas kernels, gram(): pl.pallas_call(body, in_specs=[pl.BlockSpec(memory_space=pltpu.SMEM), pl....  14.1 us
  transfers between devices with their start and end apart: 24, of which 10 were waited for; matrix products, arithmetic and copies ran while one was open for 1% of the time, Pallas kernels for 8%

profile of v7, /device:TPU:8, one launch (start us, length us, event | category | flops | bytes accessed | tf_op | source)
XLA Modules:
  0.0 88.8 jit_solution(17828288731647012739)
XLA Ops:
  0.0 7.1 %shard_map.38 = (f32[96,768]{1,0:T(8,128)S(1)}, bf16[96,768]{1,0:T(8,128)(2,1)S(1)}, bf16[96,768]{1,0:T(8,128)(2,1)S(1)}, bf16[96,768]{1,0:T(8,128)(2,1)S(1)}) custom-call(s32[2,3]{1,0:T(2,128)} %m.1, bf16[1,2,3,1024,384]{4,3,2,1,0:T(8,128)(2,1)} %v.1), custom_call_target="tpu_custom_call" | custom-call | flops 3623878656 | bytes 4718592 | tf_op jit(solution)/shard_map/pallas_call | solution.py:135
  7.1 2.0 %collective-permute-start.3 = (bf16[96,768]{1,0:T(8,128)(2,1)S(1)}, bf16[96,768]{1,0:T(8,128)(2,1)S(1)}, u32[]{:S(2)}, u32[]{:S(2)}) collective-permute-start(bf16[96,768]{1,0:T(8,128)(2,1)S(1)} %get-tuple-element.18), channel_id=1, source_target_pairs={{0,1},{1,0},{2,3},{3,2},{4,5},{5,4},{6,7},{7,6},{8,9},{9,8},{10,11... | collective-permute-start | bytes 442376 | tf_op jit(solution)/shard_map/ppermute | solution.py:153
  9.1 3.0 %collective-permute-start.4 = (bf16[96,768]{1,0:T(8,128)(2,1)S(1)}, bf16[96,768]{1,0:T(8,128)(2,1)S(1)}, u32[]{:S(2)}, u32[]{:S(2)}) collective-permute-start(bf16[96,768]{1,0:T(8,128)(2,1)S(1)} %get-tuple-element.19), channel_id=1, source_target_pairs={{0,8},{1,9},{2,10},{3,11},{4,12},{5,13},{6,14},{7,15},{8,0},{9,1},... | collective-permute-start | bytes 442376 | tf_op jit(solution)/shard_map/ppermute | solution.py:153
  12.2 0.1 collective-permute-start.5
  12.2 0.1 copy.12
  12.3 0.1 reshape.46.spin_ref
  12.4 7.0 %shard_map.37 = (f32[96,768]{1,0:T(8,128)S(1)}, bf16[120,768]{1,0:T(8,128)(2,1)S(1)}, bf16[120,768]{1,0:T(8,128)(2,1)S(1)}, bf16[120,768]{1,0:T(8,128)(2,1)S(1)}) custom-call(s32[2,3]{1,0:T(2,128)} %m.1, bf16[1,2,3,1024,384]{4,3,2,1,0:T(8,128)(2,1)} %v.1, bf16[4,24,768]{2,1,0:T(8,128)(2,1)S(1)} %reshape.46.spin_ref), custom_call_target="tpu_custom_call" | custom-call | flops 3623878656 | bytes 4718592 | tf_op jit(solution)/shard_map/pallas_call | solution.py:135
  19.5 2.0 %collective-permute-start = (bf16[120,768]{1,0:T(8,128)(2,1)S(1)}, bf16[120,768]{1,0:T(8,128)(2,1)S(1)}, u32[]{:S(2)}, u32[]{:S(2)}) collective-permute-start(bf16[120,768]{1,0:T(8,128)(2,1)S(1)} %get-tuple-element.14), channel_id=1, source_target_pairs={{0,1},{1,0},{2,3},{3,2},{4,5},{5,4},{6,7},{7,6},{8,9},{9,8},{10,11... | collective-permute-start | bytes 552968 | tf_op jit(solution)/shard_map/ppermute | solution.py:153
  21.5 3.0 %collective-permute-start.1 = (bf16[120,768]{1,0:T(8,128)(2,1)S(1)}, bf16[120,768]{1,0:T(8,128)(2,1)S(1)}, u32[]{:S(2)}, u32[]{:S(2)}) collective-permute-start(bf16[120,768]{1,0:T(8,128)(2,1)S(1)} %get-tuple-element.15), channel_id=1, source_target_pairs={{0,8},{1,9},{2,10},{3,11},{4,12},{5,13},{6,14},{7,15},{8,0},{9,1},... | collective-permute-start | bytes 552968 | tf_op jit(solution)/shard_map/ppermute | solution.py:153
  24.5 0.0 collective-permute-done.3
  24.5 0.2 collective-permute-start.2
  24.7 0.0 collective-permute-done.4
  24.7 0.0 collective-permute-done.5
  24.7 0.1 convert_add_fusion
  24.8 3.4 %collective-permute-start.8 = (bf16[24,768]{1,0:T(8,128)(2,1)S(1)}, bf16[24,768]{1,0:T(8,128)(2,1)S(1)}, u32[]{:S(2)}, u32[]{:S(2)}) collective-permute-start(bf16[24,768]{1,0:T(8,128)(2,1)S(1)} %get-tuple-element.34), channel_id=1, source_target_pairs={{0,2},{1,3},{2,0},{3,1},{4,6},{5,7},{6,4},{7,5},{8,10},{9,11},{10,... | collective-permute-start | bytes 110600 | tf_op jit(solution)/shard_map/ppermute | solution.py:153
  28.2 0.0 collective-permute-done
  28.2 3.9 %collective-permute-done.1 = bf16[120,768]{1,0:T(8,128)(2,1)S(1)} collective-permute-done((bf16[120,768]{1,0:T(8,128)(2,1)S(1)}, bf16[120,768]{1,0:T(8,128)(2,1)S(1)}, u32[]{:S(2)}, u32[]{:S(2)}) %collective-permute-start.1) | collective-permute-done | bytes 184352 | tf_op jit(solution)/shard_map/ppermute | solution.py:153
  32.0 0.8 collective-permute-done.2
  32.8 0.1 convert_add_fusion.1
  32.9 5.5 %collective-permute-start.6 = (bf16[24,768]{1,0:T(8,128)(2,1)S(1)}, bf16[24,768]{1,0:T(8,128)(2,1)S(1)}, u32[]{:S(2)}, u32[]{:S(2)}) collective-permute-start(bf16[24,768]{1,0:T(8,128)(2,1)S(1)} %get-tuple-element.35), channel_id=1, source_target_pairs={{0,6},{1,7},{2,4},{3,5},{4,2},{5,3},{6,0},{7,1},{8,14},{9,15},{10,... | collective-permute-start | bytes 110600 | tf_op jit(solution)/shard_map/ppermute | solution.py:153
  38.4 0.0 collective-permute-done.8
  38.4 0.1 collective-permute-start.9
  38.6 1.9 %collective-permute-done.6 = bf16[24,768]{1,0:T(8,128)(2,1)S(1)} collective-permute-done((bf16[24,768]{1,0:T(8,128)(2,1)S(1)}, bf16[24,768]{1,0:T(8,128)(2,1)S(1)}, u32[]{:S(2)}, u32[]{:S(2)}) %collective-permute-start.6) | collective-permute-done | bytes 36896 | tf_op jit(solution)/shard_map/ppermute | solution.py:153
  40.5 1.8 %collective-permute-start.7 = (bf16[48,768]{1,0:T(8,128)(2,1)S(1)}, bf16[48,768]{1,0:T(8,128)(2,1)S(1)}, u32[]{:S(2)}, u32[]{:S(2)}) collective-permute-start(bf16[48,768]{1,0:T(8,128)(2,1)S(1)} %pad_maximum_fusion.12), channel_id=1, source_target_pairs={{0,2},{1,3},{2,0},{3,1},{4,6},{5,7},{6,4},{7,5},{8,10},{9,11},{10,... | collective-permute-start | bytes 221192 | tf_op jit(solution)/shard_map/ppermute | solution.py:153
  42.3 2.8 %collective-permute-done.9 = bf16[48,768]{1,0:T(8,128)(2,1)S(1)} collective-permute-done((bf16[48,768]{1,0:T(8,128)(2,1)S(1)}, bf16[48,768]{1,0:T(8,128)(2,1)S(1)}, u32[]{:S(2)}, u32[]{:S(2)}) %collective-permute-start.9) | collective-permute-done | bytes 73760 | tf_op jit(solution)/shard_map/ppermute | solution.py:153
  45.1 0.7 collective-permute-done.7
  45.8 0.1 collective-permute-start.16
  46.0 2.9 %collective-permute-start.10 = (bf16[24,768]{1,0:T(8,128)(2,1)S(1)}, bf16[24,768]{1,0:T(8,128)(2,1)S(1)}, u32[]{:S(2)}, u32[]{:S(2)}) collective-permute-start(bf16[24,768]{1,0:T(8,128)(2,1)S(1)} %get-tuple-element.53), channel_id=1, source_target_pairs={{0,1},{1,0},{2,3},{3,2},{4,5},{5,4},{6,7},{7,6},{8,9},{9,8},{10,11... | collective-permute-start | bytes 110600 | tf_op jit(solution)/shard_map/ppermute | solution.py:153
  48.9 1.3 %collective-permute-done.16 = bf16[24,768]{1,0:T(8,128)(2,1)S(1)} collective-permute-done((bf16[24,768]{1,0:T(8,128)(2,1)S(1)}, bf16[24,768]{1,0:T(8,128)(2,1)S(1)}, u32[]{:S(2)}, u32[]{:S(2)}) %collective-permute-start.16) | collective-permute-done | bytes 36896 | tf_op jit(solution)/shard_map/ppermute | solution.py:214
  50.2 4.4 %collective-permute-start.18 = (bf16[24,768]{1,0:T(8,128)(2,1)S(1)}, bf16[24,768]{1,0:T(8,128)(2,1)S(1)}, u32[]{:S(2)}, u32[]{:S(2)}) collective-permute-start(bf16[24,768]{1,0:T(8,128)(2,1)S(1)} %collective-permute-done.16), channel_id=1, source_target_pairs={{0,6},{1,7},{2,4},{3,5},{4,2},{5,3},{6,0},{7,1},{8,14},{9,15},{10,... | collective-permute-start | bytes 110600 | tf_op jit(solution)/shard_map/ppermute | solution.py:153
  54.6 2.2 %collective-permute-start.17 = (bf16[24,768]{1,0:T(8,128)(2,1)S(1)}, bf16[24,768]{1,0:T(8,128)(2,1)S(1)}, u32[]{:S(2)}, u32[]{:S(2)}) collective-permute-start(bf16[24,768]{1,0:T(8,128)(2,1)S(1)} %collective-permute-done.16), channel_id=1, source_target_pairs={{0,2},{1,3},{2,0},{3,1},{4,6},{5,7},{6,4},{7,5},{8,10},{9,11},{10,... | collective-permute-start | bytes 110600 | tf_op jit(solution)/shard_map/ppermute | solution.py:153
  56.9 0.1 collective-permute-start.13
  57.0 0.8 collective-permute-start.12
  57.8 0.0 collective-permute-done.18
  57.8 2.2 %collective-permute-start.19 = (bf16[16,768]{1,0:T(8,128)(2,1)S(1)}, bf16[16,768]{1,0:T(8,128)(2,1)S(1)}, u32[]{:S(2)}, u32[]{:S(2)}) collective-permute-start(bf16[16,768]{1,0:T(8,128)(2,1)S(1)} %slice.134), channel_id=1, source_target_pairs={{0,2},{1,3},{2,0},{3,1},{4,6},{5,7},{6,4},{7,5},{8,10},{9,11},{10,... | collective-permute-start | bytes 73736 | tf_op jit(solution)/shard_map/ppermute | solution.py:153
  60.0 0.0 collective-permute-done.17
  60.0 4.0 %collective-permute-start.20 = (bf16[8,768]{1,0:T(8,128)(2,1)S(1)}, bf16[8,768]{1,0:T(8,128)(2,1)S(1)}, u32[]{:S(2)}, u32[]{:S(2)}) collective-permute-start(bf16[8,768]{1,0:T(8,128)(2,1)S(1)} %slice.135), channel_id=1, source_target_pairs={{0,6},{1,7},{2,4},{3,5},{4,2},{5,3},{6,0},{7,1},{8,14},{9,15},{10,... | collective-permute-start | bytes 36872 | tf_op jit(solution)/shard_map/ppermute | solution.py:153
  64.1 2.5 %collective-permute-start.11 = (bf16[48,768]{1,0:T(8,128)(2,1)S(1)}, bf16[48,768]{1,0:T(8,128)(2,1)S(1)}, u32[]{:S(2)}, u32[]{:S(2)}) collective-permute-start(bf16[48,768]{1,0:T(8,128)(2,1)S(1)} %pad_maximum_fusion.14), channel_id=1, source_target_pairs={{0,8},{1,9},{2,10},{3,11},{4,12},{5,13},{6,14},{7,15},{8,0},{9,1},... | collective-permute-start | bytes 221192 | tf_op jit(solution)/shard_map/ppermute | solution.py:153
  66.6 1.8 %collective-permute-start.14 = (bf16[48,768]{1,0:T(8,128)(2,1)S(1)}, bf16[48,768]{1,0:T(8,128)(2,1)S(1)}, u32[]{:S(2)}, u32[]{:S(2)}) collective-permute-start(bf16[48,768]{1,0:T(8,128)(2,1)S(1)} %slice.127), channel_id=1, source_target_pairs={{0,2},{1,3},{2,0},{3,1},{4,6},{5,7},{6,4},{7,5},{8,10},{9,11},{10,... | collective-permute-start | bytes 221192 | tf_op jit(solution)/shard_map/ppermute | solution.py:153
  68.5 0.0 collective-permute-done.12
  68.5 0.6 collective-permute-start.15
  69.1 0.0 collective-permute-done.20
  69.1 0.0 collective-permute-done.19
  69.2 2.8 %collective-permute-done.14 = bf16[48,768]{1,0:T(8,128)(2,1)S(1)} collective-permute-done((bf16[48,768]{1,0:T(8,128)(2,1)S(1)}, bf16[48,768]{1,0:T(8,128)(2,1)S(1)}, u32[]{:S(2)}, u32[]{:S(2)}) %collective-permute-start.14) | collective-permute-done | bytes 73760 | tf_op jit(solution)/shard_map/ppermute | solution.py:153
  72.0 3.1 %collective-permute-done.15 = bf16[48,768]{1,0:T(8,128)(2,1)S(1)} collective-permute-done((bf16[48,768]{1,0:T(8,128)(2,1)S(1)}, bf16[48,768]{1,0:T(8,128)(2,1)S(1)}, u32[]{:S(2)}, u32[]{:S(2)}) %collective-permute-start.15) | collective-permute-done | bytes 73760 | tf_op jit(solution)/shard_map/ppermute | solution.py:153
  75.1 0.1 pad_maximum_fusion
  75.2 0.1 constant_dynamic-slice_fusion.15
  75.3 0.1 pad_maximum_fusion.1
  75.4 0.1 slice_negate_fusion.1
  75.5 0.0 collective-permute-done.11
  75.5 0.3 fusion.15
  75.9 4.3 %collective-permute-start.23 = (bf16[120,768]{1,0:T(8,128)(2,1)S(1)}, bf16[120,768]{1,0:T(8,128)(2,1)S(1)}, u32[]{:S(2)}, u32[]{:S(2)}) collective-permute-start(bf16[120,768]{1,0:T(8,128)(2,1)S(1)} %get-tuple-element.47), channel_id=1, source_target_pairs={{0,9},{1,8},{2,11},{3,10},{4,13},{5,12},{6,15},{7,14},{8,1},{9,0},... | collective-permute-start | bytes 552968 | tf_op jit(solution)/shard_map/ppermute | solution.py:153
  80.1 0.0 collective-permute-start.22
  80.1 0.8 collective-permute-start.21
  81.0 3.7 %collective-permute-done.23 = bf16[120,768]{1,0:T(8,128)(2,1)S(1)} collective-permute-done((bf16[120,768]{1,0:T(8,128)(2,1)S(1)}, bf16[120,768]{1,0:T(8,128)(2,1)S(1)}, u32[]{:S(2)}, u32[]{:S(2)}) %collective-permute-start.23) | collective-permute-done | bytes 184352 | tf_op jit(solution)/shard_map/ppermute | solution.py:153
  84.6 2.5 %collective-permute-done.22 = bf16[120,768]{1,0:T(8,128)(2,1)S(1)} collective-permute-done((bf16[120,768]{1,0:T(8,128)(2,1)S(1)}, bf16[120,768]{1,0:T(8,128)(2,1)S(1)}, u32[]{:S(2)}, u32[]{:S(2)}) %collective-permute-start.22) | collective-permute-done | bytes 184352 | tf_op jit(solution)/shard_map/ppermute | solution.py:153
  87.2 0.0 collective-permute-done.21
  87.2 0.1 pad_maximum_fusion.2
  87.3 0.1 constant_dynamic-slice_fusion.3
  87.4 0.1 pad_maximum_fusion.3
  87.5 0.1 slice_negate_fusion
  87.7 0.1 copy.15
  87.8 0.3 fusion.12
  88.1 0.7 reshape.57
  (42 shorter events, 0.6 us)
Async XLA Ops:
  0.0 12.2 %copy-start = (bf16[1,2,24,4,384]{4,3,2,1,0:T(4,128)(2,1)S(1)}, bf16[1,2,24,4,384]{4,3,2,1,0:T(4,128)(2,1)}, u32[]{:S(2)}) copy-start(bf16[1,2,24,4,384]{4,3,2,1,0:T(4,128)(2,1)} %param.5) | copy-start | bytes 442372
  7.1 17.4 %collective-permute-start.3 = (bf16[96,768]{1,0:T(8,128)(2,1)S(1)}, bf16[96,768]{1,0:T(8,128)(2,1)S(1)}, u32[]{:S(2)}, u32[]{:S(2)}) collective-permute-start(bf16[96,768]{1,0:T(8,128)(2,1)S(1)} %get-tuple-element.18), channel_id=1, source_target_pairs={{0,1},{1,0},{2,3},{3,2},{4,5},{5,4},{6,7},{7,6},{8,9},{9,8},{10,11... | collective-permute-start | bytes 442376 | tf_op jit(solution)/shard_map/ppermute | solution.py:153
  9.1 15.6 %collective-permute-start.4 = (bf16[96,768]{1,0:T(8,128)(2,1)S(1)}, bf16[96,768]{1,0:T(8,128)(2,1)S(1)}, u32[]{:S(2)}, u32[]{:S(2)}) collective-permute-start(bf16[96,768]{1,0:T(8,128)(2,1)S(1)} %get-tuple-element.19), channel_id=1, source_target_pairs={{0,8},{1,9},{2,10},{3,11},{4,12},{5,13},{6,14},{7,15},{8,0},{9,1},... | collective-permute-start | bytes 442376 | tf_op jit(solution)/shard_map/ppermute | solution.py:153
  12.2 12.5 %collective-permute-start.5 = (bf16[96,768]{1,0:T(8,128)(2,1)S(1)}, bf16[96,768]{1,0:T(8,128)(2,1)S(1)}, u32[]{:S(2)}, u32[]{:S(2)}) collective-permute-start(bf16[96,768]{1,0:T(8,128)(2,1)S(1)} %get-tuple-element.20), channel_id=1, source_target_pairs={{0,9},{1,8},{2,11},{3,10},{4,13},{5,12},{6,15},{7,14},{8,1},{9,0},... | collective-permute-start | bytes 442376 | tf_op jit(solution)/shard_map/ppermute | solution.py:153
  19.5 8.7 %collective-permute-start = (bf16[120,768]{1,0:T(8,128)(2,1)S(1)}, bf16[120,768]{1,0:T(8,128)(2,1)S(1)}, u32[]{:S(2)}, u32[]{:S(2)}) collective-permute-start(bf16[120,768]{1,0:T(8,128)(2,1)S(1)} %get-tuple-element.14), channel_id=1, source_target_pairs={{0,1},{1,0},{2,3},{3,2},{4,5},{5,4},{6,7},{7,6},{8,9},{9,8},{10,11... | collective-permute-start | bytes 552968 | tf_op jit(solution)/shard_map/ppermute | solution.py:153
  21.5 10.6 %collective-permute-start.1 = (bf16[120,768]{1,0:T(8,128)(2,1)S(1)}, bf16[120,768]{1,0:T(8,128)(2,1)S(1)}, u32[]{:S(2)}, u32[]{:S(2)}) collective-permute-start(bf16[120,768]{1,0:T(8,128)(2,1)S(1)} %get-tuple-element.15), channel_id=1, source_target_pairs={{0,8},{1,9},{2,10},{3,11},{4,12},{5,13},{6,14},{7,15},{8,0},{9,1},... | collective-permute-start | bytes 552968 | tf_op jit(solution)/shard_map/ppermute | solution.py:153
  24.5 8.3 %collective-permute-start.2 = (bf16[120,768]{1,0:T(8,128)(2,1)S(1)}, bf16[120,768]{1,0:T(8,128)(2,1)S(1)}, u32[]{:S(2)}, u32[]{:S(2)}) collective-permute-start(bf16[120,768]{1,0:T(8,128)(2,1)S(1)} %get-tuple-element.16), channel_id=1, source_target_pairs={{0,9},{1,8},{2,11},{3,10},{4,13},{5,12},{6,15},{7,14},{8,1},{9,0},... | collective-permute-start | bytes 552968 | tf_op jit(solution)/shard_map/ppermute | solution.py:153
  24.8 13.6 %collective-permute-start.8 = (bf16[24,768]{1,0:T(8,128)(2,1)S(1)}, bf16[24,768]{1,0:T(8,128)(2,1)S(1)}, u32[]{:S(2)}, u32[]{:S(2)}) collective-permute-start(bf16[24,768]{1,0:T(8,128)(2,1)S(1)} %get-tuple-element.34), channel_id=1, source_target_pairs={{0,2},{1,3},{2,0},{3,1},{4,6},{5,7},{6,4},{7,5},{8,10},{9,11},{10,... | collective-permute-start | bytes 110600 | tf_op jit(solution)/shard_map/ppermute | solution.py:153
  32.9 7.5 %collective-permute-start.6 = (bf16[24,768]{1,0:T(8,128)(2,1)S(1)}, bf16[24,768]{1,0:T(8,128)(2,1)S(1)}, u32[]{:S(2)}, u32[]{:S(2)}) collective-permute-start(bf16[24,768]{1,0:T(8,128)(2,1)S(1)} %get-tuple-element.35), channel_id=1, source_target_pairs={{0,6},{1,7},{2,4},{3,5},{4,2},{5,3},{6,0},{7,1},{8,14},{9,15},{10,... | collective-permute-start | bytes 110600 | tf_op jit(solution)/shard_map/ppermute | solution.py:153
  38.4 6.7 %collective-permute-start.9 = (bf16[48,768]{1,0:T(8,128)(2,1)S(1)}, bf16[48,768]{1,0:T(8,128)(2,1)S(1)}, u32[]{:S(2)}, u32[]{:S(2)}) collective-permute-start(bf16[48,768]{1,0:T(8,128)(2,1)S(1)} %pad_maximum_fusion.13), channel_id=1, source_target_pairs={{0,6},{1,7},{2,4},{3,5},{4,2},{5,3},{6,0},{7,1},{8,14},{9,15},{10,... | collective-permute-start | bytes 221192 | tf_op jit(solution)/shard_map/ppermute | solution.py:153
  40.5 5.3 %collective-permute-start.7 = (bf16[48,768]{1,0:T(8,128)(2,1)S(1)}, bf16[48,768]{1,0:T(8,128)(2,1)S(1)}, u32[]{:S(2)}, u32[]{:S(2)}) collective-permute-start(bf16[48,768]{1,0:T(8,128)(2,1)S(1)} %pad_maximum_fusion.12), channel_id=1, source_target_pairs={{0,2},{1,3},{2,0},{3,1},{4,6},{5,7},{6,4},{7,5},{8,10},{9,11},{10,... | collective-permute-start | bytes 221192 | tf_op jit(solution)/shard_map/ppermute | solution.py:153
  45.8 4.4 %collective-permute-start.16 = (bf16[24,768]{1,0:T(8,128)(2,1)S(1)}, bf16[24,768]{1,0:T(8,128)(2,1)S(1)}, u32[]{:S(2)}, u32[]{:S(2)}) collective-permute-start(bf16[24,768]{1,0:T(8,128)(2,1)S(1)} %get-tuple-element.52), channel_id=1, source_target_pairs={{0,240},{16,224},{32,208},{48,192},{64,176},{80,160},{96,144},{112... | collective-permute-start | bytes 110600 | tf_op jit(solution)/shard_map/ppermute | solution.py:214
  46.0 18.1 %collective-permute-start.10 = (bf16[24,768]{1,0:T(8,128)(2,1)S(1)}, bf16[24,768]{1,0:T(8,128)(2,1)S(1)}, u32[]{:S(2)}, u32[]{:S(2)}) collective-permute-start(bf16[24,768]{1,0:T(8,128)(2,1)S(1)} %get-tuple-element.53), channel_id=1, source_target_pairs={{0,1},{1,0},{2,3},{3,2},{4,5},{5,4},{6,7},{7,6},{8,9},{9,8},{10,11... | collective-permute-start | bytes 110600 | tf_op jit(solution)/shard_map/ppermute | solution.py:153
  50.2 7.6 %collective-permute-start.18 = (bf16[24,768]{1,0:T(8,128)(2,1)S(1)}, bf16[24,768]{1,0:T(8,128)(2,1)S(1)}, u32[]{:S(2)}, u32[]{:S(2)}) collective-permute-start(bf16[24,768]{1,0:T(8,128)(2,1)S(1)} %collective-permute-done.16), channel_id=1, source_target_pairs={{0,6},{1,7},{2,4},{3,5},{4,2},{5,3},{6,0},{7,1},{8,14},{9,15},{10,... | collective-permute-start | bytes 110600 | tf_op jit(solution)/shard_map/ppermute | solution.py:153
  54.6 5.4 %collective-permute-start.17 = (bf16[24,768]{1,0:T(8,128)(2,1)S(1)}, bf16[24,768]{1,0:T(8,128)(2,1)S(1)}, u32[]{:S(2)}, u32[]{:S(2)}) collective-permute-start(bf16[24,768]{1,0:T(8,128)(2,1)S(1)} %collective-permute-done.16), channel_id=1, source_target_pairs={{0,2},{1,3},{2,0},{3,1},{4,6},{5,7},{6,4},{7,5},{8,10},{9,11},{10,... | collective-permute-start | bytes 110600 | tf_op jit(solution)/shard_map/ppermute | solution.py:153
  56.9 9.7 %collective-permute-start.13 = (bf16[96,768]{1,0:T(8,128)(2,1)S(1)}, bf16[96,768]{1,0:T(8,128)(2,1)S(1)}, u32[]{:S(2)}, u32[]{:S(2)}) collective-permute-start(bf16[96,768]{1,0:T(8,128)(2,1)S(1)} %bitcast.95), channel_id=1, source_target_pairs={{0,6},{1,7},{2,4},{3,5},{4,2},{5,3},{6,0},{7,1},{8,14},{9,15},{10,... | collective-permute-start | bytes 442376 | tf_op jit(solution)/shard_map/ppermute | solution.py:153
  57.0 11.5 %collective-permute-start.12 = (bf16[96,768]{1,0:T(8,128)(2,1)S(1)}, bf16[96,768]{1,0:T(8,128)(2,1)S(1)}, u32[]{:S(2)}, u32[]{:S(2)}) collective-permute-start(bf16[96,768]{1,0:T(8,128)(2,1)S(1)} %bitcast.96), channel_id=1, source_target_pairs={{0,2},{1,3},{2,0},{3,1},{4,6},{5,7},{6,4},{7,5},{8,10},{9,11},{10,... | collective-permute-start | bytes 442376 | tf_op jit(solution)/shard_map/ppermute | solution.py:153
  57.8 11.3 %collective-permute-start.19 = (bf16[16,768]{1,0:T(8,128)(2,1)S(1)}, bf16[16,768]{1,0:T(8,128)(2,1)S(1)}, u32[]{:S(2)}, u32[]{:S(2)}) collective-permute-start(bf16[16,768]{1,0:T(8,128)(2,1)S(1)} %slice.134), channel_id=1, source_target_pairs={{0,2},{1,3},{2,0},{3,1},{4,6},{5,7},{6,4},{7,5},{8,10},{9,11},{10,... | collective-permute-start | bytes 73736 | tf_op jit(solution)/shard_map/ppermute | solution.py:153
  60.0 9.0 %collective-permute-start.20 = (bf16[8,768]{1,0:T(8,128)(2,1)S(1)}, bf16[8,768]{1,0:T(8,128)(2,1)S(1)}, u32[]{:S(2)}, u32[]{:S(2)}) collective-permute-start(bf16[8,768]{1,0:T(8,128)(2,1)S(1)} %slice.135), channel_id=1, source_target_pairs={{0,6},{1,7},{2,4},{3,5},{4,2},{5,3},{6,0},{7,1},{8,14},{9,15},{10,... | collective-permute-start | bytes 36872 | tf_op jit(solution)/shard_map/ppermute | solution.py:153
  64.1 11.4 %collective-permute-start.11 = (bf16[48,768]{1,0:T(8,128)(2,1)S(1)}, bf16[48,768]{1,0:T(8,128)(2,1)S(1)}, u32[]{:S(2)}, u32[]{:S(2)}) collective-permute-start(bf16[48,768]{1,0:T(8,128)(2,1)S(1)} %pad_maximum_fusion.14), channel_id=1, source_target_pairs={{0,8},{1,9},{2,10},{3,11},{4,12},{5,13},{6,14},{7,15},{8,0},{9,1},... | collective-permute-start | bytes 221192 | tf_op jit(solution)/shard_map/ppermute | solution.py:153
  66.6 5.3 %collective-permute-start.14 = (bf16[48,768]{1,0:T(8,128)(2,1)S(1)}, bf16[48,768]{1,0:T(8,128)(2,1)S(1)}, u32[]{:S(2)}, u32[]{:S(2)}) collective-permute-start(bf16[48,768]{1,0:T(8,128)(2,1)S(1)} %slice.127), channel_id=1, source_target_pairs={{0,2},{1,3},{2,0},{3,1},{4,6},{5,7},{6,4},{7,5},{8,10},{9,11},{10,... | collective-permute-start | bytes 221192 | tf_op jit(solution)/shard_map/ppermute | solution.py:153
  68.5 6.6 %collective-permute-start.15 = (bf16[48,768]{1,0:T(8,128)(2,1)S(1)}, bf16[48,768]{1,0:T(8,128)(2,1)S(1)}, u32[]{:S(2)}, u32[]{:S(2)}) collective-permute-start(bf16[48,768]{1,0:T(8,128)(2,1)S(1)} %slice.128), channel_id=1, source_target_pairs={{0,6},{1,7},{2,4},{3,5},{4,2},{5,3},{6,0},{7,1},{8,14},{9,15},{10,... | collective-permute-start | bytes 221192 | tf_op jit(solution)/shard_map/ppermute | solution.py:153
  75.9 8.7 %collective-permute-start.23 = (bf16[120,768]{1,0:T(8,128)(2,1)S(1)}, bf16[120,768]{1,0:T(8,128)(2,1)S(1)}, u32[]{:S(2)}, u32[]{:S(2)}) collective-permute-start(bf16[120,768]{1,0:T(8,128)(2,1)S(1)} %get-tuple-element.47), channel_id=1, source_target_pairs={{0,9},{1,8},{2,11},{3,10},{4,13},{5,12},{6,15},{7,14},{8,1},{9,0},... | collective-permute-start | bytes 552968 | tf_op jit(solution)/shard_map/ppermute | solution.py:153
  80.1 7.0 %collective-permute-start.22 = (bf16[120,768]{1,0:T(8,128)(2,1)S(1)}, bf16[120,768]{1,0:T(8,128)(2,1)S(1)}, u32[]{:S(2)}, u32[]{:S(2)}) collective-permute-start(bf16[120,768]{1,0:T(8,128)(2,1)S(1)} %get-tuple-element.46), channel_id=1, source_target_pairs={{0,8},{1,9},{2,10},{3,11},{4,12},{5,13},{6,14},{7,15},{8,0},{9,1},... | collective-permute-start | bytes 552968 | tf_op jit(solution)/shard_map/ppermute | solution.py:153
  80.1 7.1 %collective-permute-start.21 = (bf16[120,768]{1,0:T(8,128)(2,1)S(1)}, bf16[120,768]{1,0:T(8,128)(2,1)S(1)}, u32[]{:S(2)}, u32[]{:S(2)}) collective-permute-start(bf16[120,768]{1,0:T(8,128)(2,1)S(1)} %get-tuple-element.45), channel_id=1, source_target_pairs={{0,1},{1,0},{2,3},{3,2},{4,5},{5,4},{6,7},{7,6},{8,9},{9,8},{10,11... | collective-permute-start | bytes 552968 | tf_op jit(solution)/shard_map/ppermute | solution.py:153
